TPU v7x, 128 devices: a whole 4x4x4 slice. The times are simulated.
128 devices in a mesh: row: 8 (over x, core), col: 16 (over y, z).
Axes of the slice: x: 4, y: 4, z: 4, core: 2. Of those that a mesh axis runs over, the one named last changes fastest.
Arguments:
- displacement: float32 [3, 64, 128, 8, 384], P(None, 'row', 'col'), may hold values from -6 to 6
- flux: float32 [16384, 384], P(('row', 'col')), may hold values from -6 to 6
- stiffness: float32 [64, 128, 8], P('row', 'col'), may hold values from 0.3 to 3
- mixing: float32 [3, 3], replicated, may hold values from -3.5 to 3.5
- single_layer: bfloat16 [16384, 16384], P('row', 'col'), may hold values from -0.09375 to 0.09375
- double_layer: bfloat16 [16384, 16384], P('row', 'col'), may hold values from -0.09375 to 0.09375
- near_blocks: bfloat16 [64, 16, 128, 128], P('row', 'col'), may hold values from -1 to 1
- near_rows: int32 [64, 16], P('row', 'col'), may hold values from 0 to 15
- near_cols: int32 [64, 16], P('row', 'col'), may hold values from 0 to 7
- near_counts: int32 [8, 16], P('row', 'col'), may hold values from 1 to 8, as said below
- routes: int32 [16384], P(('row', 'col')), may hold values from 0 to 127, as said below
Outputs:
- new_displacement: float32 [3, 64, 128, 8, 384], P(None, 'row', 'col')
- new_flux: float32 [16384, 384], P(('row', 'col'))
Inputs may be any that keep to these rules, and one draw needn't show every extreme that they name: `routes`: each device's 128 values are a permutation of 0 to 127; value q sends the panel to tile column q // 8. `near_counts`: some tile has all 8 places live.
All inputs are finite; a program needn't handle non-finite values.
Results may differ from a plain program's by a relative error of at most 0.004.
Values may be sent and summed in bfloat16 or wider, within the bound.
No kernel may reach another device: no remote copies, remote signals or barrier semaphores. Data moves between devices by JAX's collectives and lax.ppermute only.
A program may use at most 128 MiB of HBM per device.

v0:
```python
import jax
import jax.numpy as jnp
from jax import lax
from jax.sharding import PartitionSpec as P


def with_halo(cells, sides, width):
    for axis, dim in sides:
        count = lax.axis_size(axis)
        ends = count - 1
        head = lax.slice_in_dim(cells, 0, width, axis=dim)
        tail = lax.slice_in_dim(cells, cells.shape[dim] - width, cells.shape[dim], axis=dim)
        cells = jnp.concatenate(
            [
                lax.ppermute(tail, axis, [(i, (i + 1) % count) for i in range(ends)]),
                cells,
                lax.ppermute(head, axis, [((i + 1) % count, i) for i in range(ends)]),
            ],
            axis=dim,
        )
    return cells


def apply_stiffness(field, stiffness, mixing):
    padded = with_halo(field, (("row", 1), ("col", 2)), 1)
    padded = jnp.pad(padded, ((0, 0), (0, 0), (0, 0), (1, 1), (0, 0)))
    beside = padded[:, 2:, 1:-1, 1:-1] + padded[:, :-2, 1:-1, 1:-1]
    beside = beside + padded[:, 1:-1, 2:, 1:-1] + padded[:, 1:-1, :-2, 1:-1]
    beside = beside + padded[:, 1:-1, 1:-1, 2:] + padded[:, 1:-1, 1:-1, :-2]
    mixed = jnp.einsum("ij,jxyzq->ixyzq", mixing, field, precision=lax.Precision.HIGHEST)
    return stiffness[None, :, :, :, None] * (field - beside / 6.0) + mixed


def route_panels(packed_phi, packed_trace):
    swapped = (
        lax.all_to_all(packed_phi, "col", split_axis=0, concat_axis=0, tiled=True),
        lax.all_to_all(packed_trace, "col", split_axis=0, concat_axis=0, tiled=True),
    )
    routed = (
        lax.all_gather(swapped[0], "row", axis=0, tiled=True),
        lax.all_gather(swapped[1], "row", axis=0, tiled=True),
    )
    return (routed[0], routed[1])


def apply_once(
    field,
    flux,
    stiffness,
    mixing,
    single_layer,
    double_layer,
    near_blocks,
    near_rows,
    near_cols,
    near_counts,
    routes,
):
    cells_x = field.shape[1]
    cells_y = field.shape[2]
    depth = field.shape[3]
    waves = field.shape[4]
    owned = flux.shape[0]
    tile_rows = single_layer.shape[0]
    block = near_blocks.shape[2]
    places = near_blocks.shape[0]
    faces = jnp.stack([field[2, :, :, 0], field[2, :, :, depth - 1]], 0)
    trace = faces.reshape(owned, waves)
    selector = (routes[None, :] == jnp.arange(owned, dtype=jnp.int32)[:, None]).astype(jnp.bfloat16)
    packed_phi = jnp.dot(
        selector, flux.astype(jnp.bfloat16), preferred_element_type=jnp.float32
    ).astype(jnp.bfloat16)
    packed_trace = jnp.dot(
        selector, trace.astype(jnp.bfloat16), preferred_element_type=jnp.float32
    ).astype(jnp.bfloat16)
    routed_phi, routed_trace = route_panels(packed_phi, packed_trace)
    blocks = near_blocks.reshape(places, block, block)
    columns = routed_phi.reshape(routed_phi.shape[0] // block, block, waves)
    picked = columns[near_cols.reshape(places)]
    products = jnp.einsum("kab,kbq->kaq", blocks, picked, preferred_element_type=jnp.float32)
    live = (jnp.arange(places) < near_counts.reshape(())).astype(jnp.float32)
    onehot = (near_rows.reshape(places)[:, None] == jnp.arange(tile_rows // block)[None, :]).astype(
        jnp.float32
    ) * live[:, None]
    near = jnp.einsum("ki,kaq->iaq", onehot, products, precision=lax.Precision.HIGHEST).reshape(
        tile_rows, waves
    )
    total = jnp.dot(single_layer, routed_phi, preferred_element_type=jnp.float32)
    total = total + jnp.dot(double_layer, routed_trace, preferred_element_type=jnp.float32)
    summed = lax.psum_scatter(total + near, "col", scatter_dimension=0, tiled=True)
    new_flux = summed - 0.5 * trace
    spread = flux.reshape(2, cells_x, cells_y, waves)
    new_field = apply_stiffness(field, stiffness, mixing)
    new_field = new_field.at[2, :, :, 0].add(-spread[0])
    new_field = new_field.at[2, :, :, depth - 1].add(-spread[1])
    return (new_field, new_flux)


def local(
    displacement,
    flux,
    stiffness,
    mixing,
    single_layer,
    double_layer,
    near_blocks,
    near_rows,
    near_cols,
    near_counts,
    routes,
):
    field, values = (displacement, flux)
    for step in range(2):
        field, values = apply_once(
            field,
            values,
            stiffness,
            mixing,
            single_layer,
            double_layer,
            near_blocks,
            near_rows,
            near_cols,
            near_counts,
            routes,
        )
    return (field, values)


def solution(mesh):
    return jax.shard_map(
        local,
        mesh=mesh,
        in_specs=(
            P(None, "row", "col", None, None),
            P(("row", "col"), None),
            P("row", "col", None),
            P(),
            P("row", "col"),
            P("row", "col"),
            P("row", "col", None, None),
            P("row", "col"),
            P("row", "col"),
            P("row", "col"),
            P(("row", "col")),
        ),
        out_specs=(P(None, "row", "col", None, None), P(("row", "col"), None)),
        check_vma=False,
    )
```

profile of v0, /device:TPU:2, one launch (start us, length us, event | category | flops | bytes accessed | tf_op | source)
XLA Modules:
  0.0 303.5 jit_solution(11258190049650687744)
XLA Ops:
  7.2 3.3 %copy.78 = f32[3,8,8,8,384]{4,0,3,2,1:T(4,128)S(1)} copy(f32[3,8,8,8,384]{4,3,2,1,0:T(8,128)} %param.19) | data formatting | bytes 4718592 | tf_op args[0]
  10.6 1.7 copy-done.7
  13.4 0.8 fusion.18
  14.2 8.0 %all-to-all-start.1 = ((bf16[16,8,384]{2,1,0:T(8,128)(2,1)}), bf16[16,8,384]{2,1,0:T(8,128)(2,1)S(1)}, u32[]{:S(2)}, u32[]{:S(2)}) async-start(bf16[16,8,384]{2,1,0:T(8,128)(2,1)} %fusion.18), calls=%async_computation.1 | async-start | bytes 196608 | tf_op jit(solution)/shard_map/all_to_all | solution.py:37
  22.3 0.8 fusion.17
  23.8 6.2 %all-to-all-done.1 = bf16[16,8,384]{2,1,0:T(8,128)(2,1)S(1)} async-done(((bf16[16,8,384]{2,1,0:T(8,128)(2,1)}), bf16[16,8,384]{2,1,0:T(8,128)(2,1)S(1)}, u32[]{:S(2)}, u32[]{:S(2)}) %all-to-all-start.1) | async-done | bytes 98336 | tf_op jit(solution)/shard_map/all_to_all | solution.py:37
  30.0 3.5 %all-to-all-start = ((bf16[16,8,384]{2,1,0:T(8,128)(2,1)}), bf16[16,8,384]{2,1,0:T(8,128)(2,1)S(1)}, u32[]{:S(2)}, u32[]{:S(2)}) async-start(bf16[16,8,384]{2,1,0:T(8,128)(2,1)} %fusion.17), calls=%async_computation | async-start | bytes 196608 | tf_op jit(solution)/shard_map/all_to_all | solution.py:36
  33.6 14.5 %all_gather.13 = bf16[1024,384]{1,0:T(8,128)(2,1)} all-gather(bf16[128,384]{1,0:T(8,128)(2,1)S(1)} %bitcast.90), channel_id=1, replica_groups=mesh['row'=8,'col'=16] {'row'}, dimensions={0}, use_global_device_ids=true | all-gather | bytes 884736 | tf_op jit(solution)/shard_map/all_gather | solution.py:41
  48.1 13.6 %all_gather.12 = bf16[1024,384]{1,0:T(8,128)(2,1)S(1)} all-gather(bf16[128,384]{1,0:T(8,128)(2,1)S(1)} %bitcast.91), channel_id=1, replica_groups=mesh['row'=8,'col'=16] {'row'}, dimensions={0}, use_global_device_ids=true | all-gather | bytes 884736 | tf_op jit(solution)/shard_map/all_gather | solution.py:40
  63.7 2.8 fusion.34
  66.5 1.0 copy.87
  67.6 1.3 copy-done.37
  68.9 2.3 fusion.53
  71.3 4.2 %bitcast_add_fusion.1 = f32[2048,384]{1,0:T(8,128)} fusion(f32[16,128,384]{2,1,0:T(8,128)S(1)} %copy.87, f32[384,2048]{0,1:T(8,128)S(1)} %fusion.53, bf16[2048,1024]{1,0:T(8,128)(2,1)S(1)} %copy-done.3, bf16[1024,384]{1,0:T(8,128)(2,1)S(1)} %copy-done.10), kind=kOutput, calls=%fused_computation.42 | convolution fusion | flops 1612185600 | bytes 14417920 | tf_op jit(solution)/shard_map/dot_general | solution.py:89
  75.6 1.4 fusion.51
  77.0 2.3 collective-permute-start.1
  79.3 3.6 %collective-permute-start = (f32[3,1,8,8,384]{4,0,3,2,1:T(4,128)S(1)}, f32[3,1,8,8,384]{4,0,3,2,1:T(4,128)S(1)}, u32[]{:S(2)}, u32[]{:S(2)}) collective-permute-start(f32[3,1,8,8,384]{4,0,3,2,1:T(4,128)S(1)} %get-tuple-element.66), channel_id=1, source_target_pairs={{16,0},{32,16},{48,32},{64,48},{80,64},{96,80},{112,96},{17,1},{33... | collective-permute-start | bytes 884744 | tf_op jit(solution)/shard_map/ppermute | solution.py:17
  82.9 3.2 %collective-permute-done.1 = f32[3,1,8,8,384]{4,0,3,2,1:T(4,128)S(1)} collective-permute-done((f32[3,1,8,8,384]{4,0,3,2,1:T(4,128)S(1)}, f32[3,1,8,8,384]{4,0,3,2,1:T(4,128)S(1)}, u32[]{:S(2)}, u32[]{:S(2)}) %collective-permute-start.1) | collective-permute-done | bytes 294944 | tf_op jit(solution)/shard_map/ppermute | solution.py:15
  86.1 0.7 copy-done.30
  86.9 1.9 copy_dynamic-update-slice_fusion
  88.9 0.8 copy-done.32
  89.8 1.9 copy-done.5
  91.8 1.3 collective-permute-start.2
  93.1 4.6 %collective-permute-start.3 = (f32[3,10,1,8,384]{4,0,3,2,1:T(4,128)S(1)}, f32[3,10,1,8,384]{4,0,3,2,1:T(4,128)S(1)}, u32[]{:S(2)}, u32[]{:S(2)}) collective-permute-start(f32[3,10,1,8,384]{4,0,3,2,1:T(4,128)S(1)} %get-tuple-element.60), channel_id=1, source_target_pairs={{0,1},{1,2},{2,3},{3,4},{4,5},{5,6},{6,7},{7,8},{8,9},{9,10},{10,1... | collective-permute-start | bytes 1105928 | tf_op jit(solution)/shard_map/ppermute | solution.py:15
  97.8 0.7 neg.45
  100.1 11.4 %collective-permute-done.2 = f32[3,10,1,8,384]{4,0,3,2,1:T(4,128)S(1)} collective-permute-done((f32[3,10,1,8,384]{4,0,3,2,1:T(4,128)S(1)}, f32[3,10,1,8,384]{4,0,3,2,1:T(4,128)S(1)}, u32[]{:S(2)}, u32[]{:S(2)}) %collective-permute-start.2) | collective-permute-done | bytes 368672 | tf_op jit(solution)/shard_map/ppermute | solution.py:17
  112.3 0.8 copy-done.29
  113.1 3.5 %select_maximum_fusion.4 = f32[3,10,10,10,384]{4,0,3,2,1:T(4,128)S(1)} fusion(f32[3,10,1,8,384]{4,0,3,2,1:T(4,128)S(1)} %collective-permute-done.2, f32[3,10,8,8,384]{4,0,3,2,1:T(4,128)} %copy-done.5, f32[3,10,1,8,384]{4,0,3,2,1:T(4,128)S(1)} %collective-permute-done.3), kind=kLoop, calls=%fused_computation.8 | loop fusion | flops 9216000 | bytes 8294400 | tf_op jit(solution)/shard_map/concatenate | solution.py:13
  116.7 12.0 %fusion.11 = f32[3,8,8,8,384]{4,0,3,2,1:T(4,128)S(1)} fusion(f32[3,8,8,8,384]{4,0,3,2,1:T(4,128)S(1)} %copy-done.8, f32[3,10,10,10,384]{4,0,3,2,1:T(4,128)S(1)} %select_maximum_fusion.4, f32[3,10,8,8,384]{4,0,3,2,1:T(4,128)S(1)} %copy-done.6, f32[3,10,1,8,384]{4,0,3,2,1:T(4,128)} %copy-done.29, f32[3,10,1,8,384]{4,0,3,2,1:T(4,128)} %copy-done.28, ...), kind=kOutput, calls=%fused_computation.33 | convolution fusion | flops 28901376 | bytes 20432896 | tf_op jit(solution)/shard_map/ij,jxyzq->ixyzq/dot_general | solution.py:30
  128.8 2.4 scatter-add.14
  131.2 1.0 slice_add_fusion.6
  132.3 2.4 scatter-add.15
  135.7 0.8 fusion.20
  136.5 9.5 %all-to-all-start.3 = ((bf16[16,8,384]{2,1,0:T(8,128)(2,1)}), bf16[16,8,384]{2,1,0:T(8,128)(2,1)}, u32[]{:S(2)}, u32[]{:S(2)}) async-start(bf16[16,8,384]{2,1,0:T(8,128)(2,1)} %fusion.20), calls=%async_computation.4 | async-start | bytes 196608 | tf_op jit(solution)/shard_map/all_to_all | solution.py:37
  146.0 11.2 %reduce-scatter.3.cloned.1.call-done = f32[128,384]{1,0:T(8,128)} async-done(((f32[2048,384]{1,0:T(8,128)}), f32[128,384]{1,0:T(8,128)}) %reduce-scatter.3.cloned.1.call-update) | async-done | bytes 196624 | tf_op jit(solution)/shard_map/reduce_scatter | solution.py:90
  157.2 1.0 bitcast_subtract_fusion
  158.9 0.8 fusion.19
  159.8 5.0 %all-to-all-start.2 = ((bf16[16,8,384]{2,1,0:T(8,128)(2,1)}), bf16[16,8,384]{2,1,0:T(8,128)(2,1)}, u32[]{:S(2)}, u32[]{:S(2)}) async-start(bf16[16,8,384]{2,1,0:T(8,128)(2,1)} %fusion.19), calls=%async_computation.3 | async-start | bytes 196608 | tf_op jit(solution)/shard_map/all_to_all | solution.py:36
  164.8 14.7 %all_gather.15 = bf16[1024,384]{1,0:T(8,128)(2,1)} all-gather(bf16[128,384]{1,0:T(8,128)(2,1)} %bitcast.29), channel_id=1, replica_groups=mesh['row'=8,'col'=16] {'row'}, dimensions={0}, use_global_device_ids=true | all-gather | bytes 884736 | tf_op jit(solution)/shard_map/all_gather | solution.py:41
  179.5 14.1 %all_gather.14 = bf16[1024,384]{1,0:T(8,128)(2,1)S(1)} all-gather(bf16[128,384]{1,0:T(8,128)(2,1)} %bitcast.24), channel_id=1, replica_groups=mesh['row'=8,'col'=16] {'row'}, dimensions={0}, use_global_device_ids=true | all-gather | bytes 884736 | tf_op jit(solution)/shard_map/all_gather | solution.py:40
  193.6 5.9 %fusion.52 = f32[384,2048]{1,0:T(8,128)} fusion(bf16[1024,384]{1,0:T(8,128)(2,1)S(1)} %all_gather.14, bf16[2048,1024]{1,0:T(8,128)(2,1)} %param.23), kind=kOutput, calls=%fused_computation.113 | convolution fusion | flops 1610612736 | bytes 8126464 | tf_op jit(solution)/shard_map/dot_general | solution.py:88
  199.5 2.7 gather_fusion.1
  202.2 1.7 convolution_bitcast_fusion
  203.9 3.4 %fusion.15 = f32[16,128,384]{1,0,2:T(8,128)S(1)} fusion(f32[8,128,384]{1,2,0:T(8,128)S(1)} %convolution_bitcast_fusion, f32[8]{0:T(128)S(1)} %compare_convert_fusion, s32[8]{0:T(128)S(1)} %bitcast.95), kind=kOutput, calls=%fused_computation.43 | convolution fusion | flops 75497728 | bytes 4718656 | tf_op jit(solution)/shard_map/ki,kaq->iaq/dot_general | solution.py:85
  207.3 6.2 %bitcast_add_fusion = f32[2048,384]{0,1:T(8,128)} fusion(f32[48,8,16,128]{3,2,1,0:T(8,128)S(1)} %bitcast.84, f32[384,2048]{1,0:T(8,128)} %fusion.52, bf16[1024,384]{1,0:T(8,128)(2,1)S(1)} %copy-done.24, bf16[2048,1024]{1,0:T(8,128)(2,1)S(1)} %copy-done.4), kind=kOutput, calls=%fused_computation.11 | convolution fusion | flops 1612185600 | bytes 14417920 | tf_op jit(solution)/shard_map/dot_general | solution.py:89
  213.7 2.7 collective-permute-start.4
  216.4 1.9 collective-permute-start.5
  218.3 3.3 %collective-permute-done.4 = f32[3,1,8,8,384]{4,0,3,2,1:T(4,128)S(1)} collective-permute-done((f32[3,1,8,8,384]{4,0,3,2,1:T(4,128)S(1)}, f32[3,1,8,8,384]{4,0,3,2,1:T(4,128)S(1)}, u32[]{:S(2)}, u32[]{:S(2)}) %collective-permute-start.4) | collective-permute-done | bytes 294944 | tf_op jit(solution)/shard_map/ppermute | solution.py:17
  221.7 3.8 %collective-permute-done.5 = f32[3,1,8,8,384]{4,0,3,2,1:T(4,128)S(1)} collective-permute-done((f32[3,1,8,8,384]{4,0,3,2,1:T(4,128)S(1)}, f32[3,1,8,8,384]{4,0,3,2,1:T(4,128)S(1)}, u32[]{:S(2)}, u32[]{:S(2)}) %collective-permute-start.5) | collective-permute-done | bytes 294944 | tf_op jit(solution)/shard_map/ppermute | solution.py:15
  225.5 1.2 pad_maximum_fusion.12
  226.7 1.3 collective-permute-start.6
  228.0 5.5 %collective-permute-start.7 = (f32[3,10,1,8,384]{4,0,3,2,1:T(4,128)}, f32[3,10,1,8,384]{4,0,3,2,1:T(4,128)}, u32[]{:S(2)}, u32[]{:S(2)}) collective-permute-start(f32[3,10,1,8,384]{4,0,3,2,1:T(4,128)} %get-tuple-element.58), channel_id=1, source_target_pairs={{0,1},{1,2},{2,3},{3,4},{4,5},{5,6},{6,7},{7,8},{8,9},{9,10},{10,1... | collective-permute-start | bytes 1105928 | tf_op jit(solution)/shard_map/ppermute | solution.py:15
  233.8 0.8 copy.96
  234.6 11.0 %collective-permute-done.6 = f32[3,10,1,8,384]{4,0,3,2,1:T(4,128)} collective-permute-done((f32[3,10,1,8,384]{4,0,3,2,1:T(4,128)}, f32[3,10,1,8,384]{4,0,3,2,1:T(4,128)}, u32[]{:S(2)}, u32[]{:S(2)}) %collective-permute-start.6) | collective-permute-done | bytes 368672 | tf_op jit(solution)/shard_map/ppermute | solution.py:17
  246.3 5.5 %select_maximum_fusion = f32[3,10,10,10,384]{4,0,3,2,1:T(4,128)S(1)} fusion(f32[3,10,1,8,384]{4,0,3,2,1:T(4,128)} %collective-permute-done.6, f32[3,10,1,8,384]{4,0,3,2,1:T(4,128)} %collective-permute-done.7, f32[3,1,8,8,384]{4,0,3,2,1:T(4,128)} %copy-done.16, f32[3,8,8,8,384]{4,0,3,2,1:T(4,128)S(1)} %scatter-add.15, f32[3,1,8,8,384]{4,0,3,2,1:T(4,128)} %copy-done.18), kind=kLoop, calls=%fused_computation.4 | loop fusion | flops 13824000 | bytes 8294400 | tf_op jit(solution)/shard_map/concatenate | solution.py:13
  251.9 10.5 %fusion.4 = f32[3,8,8,8,384]{4,0,3,2,1:T(4,128)S(1)} fusion(f32[3,8,8,8,384]{4,0,3,2,1:T(4,128)S(1)} %scatter-add.15, f32[3,10,10,10,384]{4,0,3,2,1:T(4,128)S(1)} %select_maximum_fusion, f32[3,10,1,8,384]{4,0,3,2,1:T(4,128)} %collective-permute-done.7, f32[3,1,8,8,384]{4,0,3,2,1:T(4,128)S(1)} %copy-done.17, f32[3,1,8,8,384]{4,0,3,2,1:T(4,128)S(1)} %copy-done.19, ...), kind=kOutput, calls=%fused_computation.16 | convolution fusion | flops 31260672 | bytes 16500736 | tf_op jit(solution)/shard_map/ij,jxyzq->ixyzq/dot_general | solution.py:30
  262.5 1.7 copy-done.9
  264.3 3.2 %scatter-add.16 = f32[3,8,8,8,384]{4,0,3,2,1:T(4,128)} dynamic-update-slice(f32[3,8,8,8,384]{4,0,3,2,1:T(4,128)} %copy-done.9, f32[1,8,8,1,384]{4,0,3,2,1:T(1,128)S(1)} %slice_add_fusion.5, s32[]{:T(128)} %constant.115.clone.1, s32[]{:T(128)} %constant.116.clone.1, s32[]{:T(128)} %constant.116.clone.1, s32[]{:T(128)} %constant.116.clone.1, s32[]{:T(128)} %constant.116.clone.1) | dynamic-update-slice | bytes 196612 | tf_op jit(solution)/shard_map/scatter-add | solution.py:94
  267.6 1.2 slice_add_fusion.4
  268.7 3.2 %scatter-add.19 = f32[3,8,8,8,384]{4,0,3,2,1:T(4,128)} dynamic-update-slice(f32[3,8,8,8,384]{4,0,3,2,1:T(4,128)} %scatter-add.16, f32[1,8,8,1,384]{4,0,3,2,1:T(1,128)S(1)} %slice_add_fusion.4, s32[]{:T(128)} %constant.115.clone.1, s32[]{:T(128)} %constant.116.clone.1, s32[]{:T(128)} %constant.116.clone.1, s32[]{:T(128)} %constant.117.clone.1, s32[]{:T(128)} %constant.116.clone.1) | dynamic-update-slice | bytes 196612 | tf_op jit(solution)/shard_map/scatter-add | solution.py:95
  272.0 3.6 %copy.97 = f32[3,8,8,8,384]{4,3,2,1,0:T(8,128)} copy(f32[3,8,8,8,384]{4,0,3,2,1:T(4,128)} %scatter-add.19) | data formatting | bytes 4718592
  275.6 19.2 %reduce-scatter.5.cloned.1.call-done = f32[128,384]{0,1:T(8,128)} async-done(((f32[2048,384]{0,1:T(8,128)}), f32[128,384]{0,1:T(8,128)}) %reduce-scatter.5.cloned.1.call-update) | async-done | bytes 196624 | tf_op jit(solution)/shard_map/reduce_scatter | solution.py:90
  294.8 0.9 sub.15
  295.7 0.8 copy.98
  (112 shorter events, 9.1 us)
Async XLA Ops:
  7.2 55.4 %copy-start = (bf16[8,1,128,128]{3,2,1,0:T(8,128)(2,1)S(1)}, bf16[8,1,128,128]{3,2,1,0:T(8,128)(2,1)}, u32[]{:S(2)}) copy-start(bf16[8,1,128,128]{3,2,1,0:T(8,128)(2,1)} %param.25) | copy-start | bytes 786436
  7.2 6.2 %copy-start.35 = (s32[128]{0:T(128)S(1)}, s32[128]{0:T(128)}, u32[]{:S(2)}) copy-start(s32[128]{0:T(128)} %param.29) | copy-start | bytes 1540
  7.2 15.1 %copy-start.25 = (f32[128,384]{1,0:T(8,128)S(1)}, f32[128,384]{1,0:T(8,128)}, u32[]{:S(2)}) copy-start(f32[128,384]{1,0:T(8,128)} %param.20) | copy-start | bytes 589828
  7.2 15.9 %copy-start.41 = (s32[8,1]{0,1:T(1,128)S(1)}, s32[8,1]{0,1:T(1,128)}, u32[]{:S(2)}) copy-start(s32[8,1]{0,1:T(1,128)} %param.27) | copy-start | bytes 100
  10.6 1.8 copy-start.7
  12.5 0.6 copy-start.22
  14.2 15.8 %all-to-all-start.1 = ((bf16[16,8,384]{2,1,0:T(8,128)(2,1)}), bf16[16,8,384]{2,1,0:T(8,128)(2,1)S(1)}, u32[]{:S(2)}, u32[]{:S(2)}) async-start(bf16[16,8,384]{2,1,0:T(8,128)(2,1)} %fusion.18), calls=%async_computation.1 | async-start | bytes 196608 | tf_op jit(solution)/shard_map/all_to_all | solution.py:37
  30.0 18.1 %all-to-all-start = ((bf16[16,8,384]{2,1,0:T(8,128)(2,1)}), bf16[16,8,384]{2,1,0:T(8,128)(2,1)S(1)}, u32[]{:S(2)}, u32[]{:S(2)}) async-start(bf16[16,8,384]{2,1,0:T(8,128)(2,1)} %fusion.17), calls=%async_computation | async-start | bytes 196608 | tf_op jit(solution)/shard_map/all_to_all | solution.py:36
  33.5 123.7 %reduce-scatter.3.cloned.1.call-start = ((), (), s32[]{:S(2)}) async-start(), calls=%async_computation.6 | async-start | bytes 3342336 | tf_op jit(solution)/shard_map/reduce_scatter | solution.py:90
  61.7 0.9 copy-start.11
  62.6 1.0 copy-start.36
  66.5 1.1 copy-start.12
  66.5 2.4 copy-start.37
  68.9 2.4 copy-start.3
  68.9 2.4 copy-start.10
  75.6 11.3 %copy-start.2 = (f32[3,8,8,8,384]{4,3,2,1,0:T(8,128)S(1)}, f32[3,8,8,8,384]{4,3,2,1,0:T(8,128)}, u32[]{:S(2)}) copy-start(f32[3,8,8,8,384]{4,3,2,1,0:T(8,128)} %param.19) | copy-start | bytes 7077892
  77.0 9.1 %collective-permute-start.1 = (f32[3,1,8,8,384]{4,0,3,2,1:T(4,128)S(1)}, f32[3,1,8,8,384]{4,0,3,2,1:T(4,128)S(1)}, u32[]{:S(2)}, u32[]{:S(2)}) collective-permute-start(f32[3,1,8,8,384]{4,0,3,2,1:T(4,128)S(1)} %get-tuple-element.67), channel_id=1, source_target_pairs={{0,16},{16,32},{32,48},{48,64},{64,80},{80,96},{96,112},{1,17},{17... | collective-permute-start | bytes 884744 | tf_op jit(solution)/shard_map/ppermute | solution.py:15
  79.3 9.6 %collective-permute-start = (f32[3,1,8,8,384]{4,0,3,2,1:T(4,128)S(1)}, f32[3,1,8,8,384]{4,0,3,2,1:T(4,128)S(1)}, u32[]{:S(2)}, u32[]{:S(2)}) collective-permute-start(f32[3,1,8,8,384]{4,0,3,2,1:T(4,128)S(1)} %get-tuple-element.66), channel_id=1, source_target_pairs={{16,0},{32,16},{48,32},{64,48},{80,64},{96,80},{112,96},{17,1},{33... | collective-permute-start | bytes 884744 | tf_op jit(solution)/shard_map/ppermute | solution.py:17
  86.1 0.7 copy-start.30
  86.9 10.8 %copy-start.26 = (f32[128,384]{1,0:T(8,128)S(1)}, f32[128,384]{1,0:T(8,128)}, u32[]{:S(2)}) copy-start(f32[128,384]{1,0:T(8,128)} %param.20) | copy-start | bytes 589828
  88.9 10.3 %copy-start.23 = (f32[1,8,8,384]{3,0,2,1:T(1,128)S(1)}, f32[1,8,8,384]{3,0,2,1:T(1,128)}, u32[]{:S(2)}) copy-start(f32[1,8,8,384]{3,0,2,1:T(1,128)} %copy-done.22) | copy-start | bytes 294916
  88.9 0.8 copy-start.32
  89.8 1.9 copy-start.5
  91.8 19.7 %collective-permute-start.2 = (f32[3,10,1,8,384]{4,0,3,2,1:T(4,128)S(1)}, f32[3,10,1,8,384]{4,0,3,2,1:T(4,128)S(1)}, u32[]{:S(2)}, u32[]{:S(2)}) collective-permute-start(f32[3,10,1,8,384]{4,0,3,2,1:T(4,128)S(1)} %get-tuple-element.61), channel_id=1, source_target_pairs={{1,0},{2,1},{3,2},{4,3},{5,4},{6,5},{7,6},{8,7},{9,8},{10,9},{11,1... | collective-permute-start | bytes 1105928 | tf_op jit(solution)/shard_map/ppermute | solution.py:17
  93.1 19.0 %collective-permute-start.3 = (f32[3,10,1,8,384]{4,0,3,2,1:T(4,128)S(1)}, f32[3,10,1,8,384]{4,0,3,2,1:T(4,128)S(1)}, u32[]{:S(2)}, u32[]{:S(2)}) collective-permute-start(f32[3,10,1,8,384]{4,0,3,2,1:T(4,128)S(1)} %get-tuple-element.60), channel_id=1, source_target_pairs={{0,1},{1,2},{2,3},{3,4},{4,5},{5,6},{6,7},{7,8},{8,9},{9,10},{10,1... | collective-permute-start | bytes 1105928 | tf_op jit(solution)/shard_map/ppermute | solution.py:15
  100.1 16.5 %copy-start.6 = (f32[3,10,8,8,384]{4,0,3,2,1:T(4,128)S(1)}, f32[3,10,8,8,384]{4,0,3,2,1:T(4,128)}, u32[]{:S(2)}) copy-start(f32[3,10,8,8,384]{4,0,3,2,1:T(4,128)} %copy-done.5) | copy-start | bytes 8847364
  100.1 16.5 %copy-start.8 = (f32[3,8,8,8,384]{4,0,3,2,1:T(4,128)S(1)}, f32[3,8,8,8,384]{4,0,3,2,1:T(4,128)}, u32[]{:S(2)}) copy-start(f32[3,8,8,8,384]{4,0,3,2,1:T(4,128)} %copy-done.7) | copy-start | bytes 7077892
  100.1 16.5 %copy-start.31 = (f32[3,1,8,8,384]{4,0,3,2,1:T(4,128)S(1)}, f32[3,1,8,8,384]{4,0,3,2,1:T(4,128)}, u32[]{:S(2)}) copy-start(f32[3,1,8,8,384]{4,0,3,2,1:T(4,128)} %copy-done.30) | copy-start | bytes 884740
  100.1 16.5 %copy-start.33 = (f32[3,1,8,8,384]{4,0,3,2,1:T(4,128)S(1)}, f32[3,1,8,8,384]{4,0,3,2,1:T(4,128)}, u32[]{:S(2)}) copy-start(f32[3,1,8,8,384]{4,0,3,2,1:T(4,128)} %copy-done.32) | copy-start | bytes 884740
  100.1 16.5 %copy-start.38 = (f32[8,8,8]{2,1,0:T(8,128)S(1)}, f32[8,8,8]{2,1,0:T(8,128)}, u32[]{:S(2)}) copy-start(f32[8,8,8]{2,1,0:T(8,128)} %param.21) | copy-start | bytes 6148
  100.1 16.5 %copy-start.39 = (f32[3,3]{1,0:T(4,128)S(1)}, f32[3,3]{1,0:T(4,128)}, u32[]{:S(2)}) copy-start(f32[3,3]{1,0:T(4,128)} %param.22) | copy-start | bytes 112
  111.5 0.8 copy-start.28
  112.3 0.8 copy-start.29
  116.7 12.0 %copy-start.34 = (f32[1,8,8,1,384]{4,0,3,2,1:T(1,128)S(1)}, f32[1,8,8,1,384]{4,0,3,2,1:T(1,128)}, u32[]{:S(2)}) copy-start(f32[1,8,8,1,384]{4,0,3,2,1:T(1,128)} %neg.45) | copy-start | bytes 294916
  134.8 0.6 copy-start.20
  136.5 23.3 %all-to-all-start.3 = ((bf16[16,8,384]{2,1,0:T(8,128)(2,1)}), bf16[16,8,384]{2,1,0:T(8,128)(2,1)}, u32[]{:S(2)}, u32[]{:S(2)}) async-start(bf16[16,8,384]{2,1,0:T(8,128)(2,1)} %fusion.20), calls=%async_computation.4 | async-start | bytes 196608 | tf_op jit(solution)/shard_map/all_to_all | solution.py:37
  158.3 0.7 copy-start.14
  159.8 19.7 %all-to-all-start.2 = ((bf16[16,8,384]{2,1,0:T(8,128)(2,1)}), bf16[16,8,384]{2,1,0:T(8,128)(2,1)}, u32[]{:S(2)}, u32[]{:S(2)}) async-start(bf16[16,8,384]{2,1,0:T(8,128)(2,1)} %fusion.19), calls=%async_computation.3 | async-start | bytes 196608 | tf_op jit(solution)/shard_map/all_to_all | solution.py:36
  164.7 130.0 %reduce-scatter.5.cloned.1.call-start = ((), (), s32[]{:S(2)}) async-start(), calls=%async_computation.7 | async-start | bytes 3342336 | tf_op jit(solution)/shard_map/reduce_scatter | solution.py:90
  193.6 5.9 %copy-start.13 = (bf16[1024,384]{1,0:T(8,128)(2,1)}, bf16[1024,384]{1,0:T(8,128)(2,1)S(1)}, u32[]{:S(2)}) copy-start(bf16[1024,384]{1,0:T(8,128)(2,1)S(1)} %all_gather.14) | copy-start | bytes 2359300
  202.2 5.1 %copy-start.4 = (bf16[2048,1024]{1,0:T(8,128)(2,1)S(1)}, bf16[2048,1024]{1,0:T(8,128)(2,1)}, u32[]{:S(2)}) copy-start(bf16[2048,1024]{1,0:T(8,128)(2,1)} %param.24) | copy-start | bytes 12582916
  202.2 5.1 %copy-start.24 = (bf16[1024,384]{1,0:T(8,128)(2,1)S(1)}, bf16[1024,384]{1,0:T(8,128)(2,1)}, u32[]{:S(2)}) copy-start(bf16[1024,384]{1,0:T(8,128)(2,1)} %all_gather.15) | copy-start | bytes 2359300
  213.5 20.0 %copy-start.21 = (f32[1,8,8,384]{3,0,2,1:T(1,128)S(1)}, f32[1,8,8,384]{3,0,2,1:T(1,128)}, u32[]{:S(2)}) copy-start(f32[1,8,8,384]{3,0,2,1:T(1,128)} %copy-done.20) | copy-start | bytes 294916
  213.7 8.0 %collective-permute-start.4 = (f32[3,1,8,8,384]{4,0,3,2,1:T(4,128)S(1)}, f32[3,1,8,8,384]{4,0,3,2,1:T(4,128)S(1)}, u32[]{:S(2)}, u32[]{:S(2)}) collective-permute-start(f32[3,1,8,8,384]{4,0,3,2,1:T(4,128)S(1)} %get-tuple-element.65), channel_id=1, source_target_pairs={{16,0},{32,16},{48,32},{64,48},{80,64},{96,80},{112,96},{17,1},{33... | collective-permute-start | bytes 884744 | tf_op jit(solution)/shard_map/ppermute | solution.py:17
  216.4 9.1 %collective-permute-start.5 = (f32[3,1,8,8,384]{4,0,3,2,1:T(4,128)S(1)}, f32[3,1,8,8,384]{4,0,3,2,1:T(4,128)S(1)}, u32[]{:S(2)}, u32[]{:S(2)}) collective-permute-start(f32[3,1,8,8,384]{4,0,3,2,1:T(4,128)S(1)} %get-tuple-element.64), channel_id=1, source_target_pairs={{0,16},{16,32},{32,48},{48,64},{64,80},{80,96},{96,112},{1,17},{17... | collective-permute-start | bytes 884744 | tf_op jit(solution)/shard_map/ppermute | solution.py:15
  221.7 3.8 %copy-start.16 = (f32[3,1,8,8,384]{4,0,3,2,1:T(4,128)}, f32[3,1,8,8,384]{4,0,3,2,1:T(4,128)S(1)}, u32[]{:S(2)}) copy-start(f32[3,1,8,8,384]{4,0,3,2,1:T(4,128)S(1)} %collective-permute-done.4) | copy-start | bytes 884740
  225.5 1.2 copy-start.18
  226.7 18.9 %collective-permute-start.6 = (f32[3,10,1,8,384]{4,0,3,2,1:T(4,128)}, f32[3,10,1,8,384]{4,0,3,2,1:T(4,128)}, u32[]{:S(2)}, u32[]{:S(2)}) collective-permute-start(f32[3,10,1,8,384]{4,0,3,2,1:T(4,128)} %get-tuple-element.59), channel_id=1, source_target_pairs={{1,0},{2,1},{3,2},{4,3},{5,4},{6,5},{7,6},{8,7},{9,8},{10,9},{11,1... | collective-permute-start | bytes 1105928 | tf_op jit(solution)/shard_map/ppermute | solution.py:17
  228.0 18.3 %collective-permute-start.7 = (f32[3,10,1,8,384]{4,0,3,2,1:T(4,128)}, f32[3,10,1,8,384]{4,0,3,2,1:T(4,128)}, u32[]{:S(2)}, u32[]{:S(2)}) collective-permute-start(f32[3,10,1,8,384]{4,0,3,2,1:T(4,128)} %get-tuple-element.58), channel_id=1, source_target_pairs={{0,1},{1,2},{2,3},{3,4},{4,5},{5,6},{6,7},{7,8},{8,9},{9,10},{10,1... | collective-permute-start | bytes 1105928 | tf_op jit(solution)/shard_map/ppermute | solution.py:15
  234.6 17.3 %copy-start.17 = (f32[3,1,8,8,384]{4,0,3,2,1:T(4,128)S(1)}, f32[3,1,8,8,384]{4,0,3,2,1:T(4,128)}, u32[]{:S(2)}) copy-start(f32[3,1,8,8,384]{4,0,3,2,1:T(4,128)} %copy-done.16) | copy-start | bytes 884740
  234.6 17.3 %copy-start.19 = (f32[3,1,8,8,384]{4,0,3,2,1:T(4,128)S(1)}, f32[3,1,8,8,384]{4,0,3,2,1:T(4,128)}, u32[]{:S(2)}) copy-start(f32[3,1,8,8,384]{4,0,3,2,1:T(4,128)} %copy-done.18) | copy-start | bytes 884740
  234.6 17.3 %copy-start.40 = (f32[3,3]{1,0:T(4,128)S(1)}, f32[3,3]{1,0:T(4,128)}, u32[]{:S(2)}) copy-start(f32[3,3]{1,0:T(4,128)} %param.22) | copy-start | bytes 112
  251.9 10.6 %copy-start.15 = (f32[128,384]{1,0:T(8,128)S(1)}, f32[128,384]{1,0:T(8,128)}, u32[]{:S(2)}) copy-start(f32[128,384]{1,0:T(8,128)} %copy-done.14) | copy-start | bytes 589828
  262.5 1.7 copy-start.9
  264.3 30.4 %copy-start.27 = (f32[128,384]{0,1:T(8,128)S(1)}, f32[128,384]{0,1:T(8,128)}, u32[]{:S(2)}) copy-start(f32[128,384]{0,1:T(8,128)} %copy.96) | copy-start | bytes 589828
  268.7 27.8 %copy-start.1 = (bf16[8,1,128,128]{3,2,1,0:T(8,128)(2,1)S(1)}, bf16[8,1,128,128]{3,2,1,0:T(8,128)(2,1)}, u32[]{:S(2)}) copy-start(bf16[8,1,128,128]{3,2,1,0:T(8,128)(2,1)} %param.25) | copy-start | bytes 786436
Sparse Core Ops, SparseCore 0:
  75.7 81.4 reduce-scatter.2
  213.6 81.0 reduce-scatter.4
where the time goes:
time: 308 us; the launch traced here: 304 us
  waiting for transfers between devices  70.8 us (23%)
  blocking collectives  57 us (19%)
  matrix products  52.8 us (17%)
  starting transfers between devices  49.3 us (16%)
  local copies, waits for them, and re-layouts  42.5 us (14%)
  other arithmetic  15.6 us (5%)
  between operations  15.6 us (5%)
    reduce_scatter x2, waiting for transfers between devices, apply_once(): lax.psum_scatter(total + near, 'col', scatter_dimension=0, tiled=True)  30.4 us
    all_gather x2, blocking collectives, route_panels(): lax.all_gather(swapped[1], 'row', axis=0, tiled=True)  29.2 us
    all_gather x2, blocking collectives, route_panels(): lax.all_gather(swapped[0], 'row', axis=0, tiled=True)  27.8 us
    ppermute x4, waiting for transfers between devices, with_halo(): lax.ppermute(head, axis, [((i + 1) % count, i) for i in range(ends)])  25.8 us
    dot_general x2, matrix products, apply_stiffness(): jnp.einsum('ij,jxyzq->ixyzq', mixing, field, precision=lax.Precision.HIGH...  22.5 us
    unnamed x89, local copies, waits for them, and re-layouts  21.1 us
    all_to_all x2, starting transfers between devices, route_panels(): lax.all_to_all(packed_trace, 'col', split_axis=0, concat_axis=0, tiled=True)  17.5 us
    ppermute x4, starting transfers between devices, with_halo(): lax.ppermute(tail, axis, [(i, (i + 1) % count) for i in range(ends)])  14.3 us
  transfers between devices with their start and end apart: 14, of which 10 were waited for; matrix products, arithmetic and copies ran while one was open for 20% of the time, Pallas kernels for 0%

commit v1 on v0

v1 whole, which is shorter than its diff:
```python
import jax
import jax.numpy as jnp
from jax import lax
from jax.experimental import pallas as pl
from jax.experimental.pallas import tpu as pltpu
from jax.sharding import PartitionSpec as P

BF = jnp.bfloat16
F32 = jnp.float32
WAVES = 384
LANES = 128


def onehot(keys, count):
    rows = lax.broadcasted_iota(jnp.int32, (count, keys.shape[1]), 0)
    return (rows == keys).astype(F32).astype(BF)


def pack_kernel(flux_ref, comp_ref, route_ref, face_ref, out_ref):
    by_panel = onehot(route_ref[...], 128)
    by_cell = onehot(face_ref[...], 128)
    out_ref[:, 0:WAVES] = jnp.dot(by_panel, flux_ref[...].astype(BF), preferred_element_type=F32).astype(BF)
    cells = comp_ref[...].reshape(512, WAVES).astype(BF)
    out_ref[:, WAVES : 2 * WAVES] = jnp.dot(by_cell, cells, preferred_element_type=F32).astype(BF)
    out_ref[:, 2 * WAVES :] = jnp.broadcast_to(route_ref[...].astype(F32), (128, 128)).astype(BF)


def pack(flux, field, route_row, face_row):
    return pl.pallas_call(
        pack_kernel,
        grid=(1,),
        in_specs=[
            pl.BlockSpec((128, WAVES), lambda i: (0, 0)),
            pl.BlockSpec((None, 8, 8, 8, WAVES), lambda i: (2, 0, 0, 0, 0)),
            pl.BlockSpec((1, 128), lambda i: (0, 0)),
            pl.BlockSpec((1, 512), lambda i: (0, 0)),
        ],
        out_specs=pl.BlockSpec((128, 2 * WAVES + 128), lambda i: (0, 0)),
        out_shape=jax.ShapeDtypeStruct((128, 2 * WAVES + 128), BF),
        name="pack",
    )(flux, field, route_row, face_row)


def stencil_kernel(first, mix_ref, *refs):
    if first:
        u_ref, xl, xh, yl, yh, st_ref, flux_ref, route_ref, out_ref, w_ref, wp_ref, f0, f1, f2, f3 = refs
    else:
        u_ref, xl, xh, yl, yh, st_ref, out_ref = refs
    depth = lax.broadcasted_iota(jnp.int32, (8, LANES), 0)
    bottom = depth == 0
    top = depth == 7
    mix = [[mix_ref[i, j] for j in range(3)] for i in range(3)]

    def plane(x, below, above):
        for y in range(8):
            cell = [u_ref[c, x, y] for c in range(3)]
            stiff = jnp.broadcast_to(st_ref[x, y], (8, LANES))
            for c in range(3):
                u = cell[c]
                total = below(c, y) + above(c, y)
                total = total + (u_ref[c, x, y - 1] if y > 0 else yl[c, x].astype(F32))
                total = total + (u_ref[c, x, y + 1] if y < 7 else yh[c, x].astype(F32))
                total = total + jnp.where(bottom, 0.0, pltpu.roll(u, 1, 0))
                total = total + jnp.where(top, 0.0, pltpu.roll(u, 7, 0))
                mixed = mix[c][0] * cell[0] + mix[c][1] * cell[1] + mix[c][2] * cell[2]
                value = stiff * (u - total * (1.0 / 6.0)) + mixed
                if first and c == 2:
                    low = flux_ref[pl.ds(x * 8 + y, 1), :]
                    high = flux_ref[pl.ds(64 + x * 8 + y, 1), :]
                    value = value - jnp.where(bottom, low, jnp.where(top, high, 0.0))
                    w_ref[pl.ds(x * 8 + y, 1), :] = value[0:1]
                    w_ref[pl.ds(64 + x * 8 + y, 1), :] = value[7:8]
                out_ref[c, x, y] = value
                if first:
                    if y == 0:
                        f2[c, x] = value.astype(BF)
                    if y == 7:
                        f3[c, x] = value.astype(BF)

    plane(0, lambda c, y: xl[c, y].astype(F32), lambda c, y: u_ref[c, 1, y])

    def step(x, carry):
        plane(x, lambda c, y: u_ref[c, x - 1, y], lambda c, y: u_ref[c, x + 1, y])
        return carry

    lax.fori_loop(1, 7, step, 0)
    plane(7, lambda c, y: u_ref[c, 6, y], lambda c, y: xh[c, y].astype(F32))
    if first:
        f0[...] = out_ref[:, 0].astype(BF)
        f1[...] = out_ref[:, 7].astype(BF)
        wp_ref[...] = jnp.dot(onehot(route_ref[...], 128), w_ref[...].astype(BF), preferred_element_type=F32).astype(BF)


def stencil(field, halos, stiffness, mixing, flux=None, route_row=None):
    first = flux is not None
    whole = pl.BlockSpec((3, 8, 8, 8, LANES), lambda i: (0, 0, 0, 0, i))
    face = pl.BlockSpec((3, 8, 8, LANES), lambda i: (0, 0, 0, i))
    panel = pl.BlockSpec((128, LANES), lambda i: (0, i))
    in_specs = [pl.BlockSpec(memory_space=pltpu.SMEM), whole, face, face, face, face,
                pl.BlockSpec((8, 8, 8, 1), lambda i: (0, 0, 0, 0))]
    args = [mixing, field, *halos, stiffness]
    out_specs = [whole]
    out_shape = [jax.ShapeDtypeStruct(field.shape, F32)]
    if first:
        in_specs += [panel, pl.BlockSpec((1, 128), lambda i: (0, 0))]
        args += [flux, route_row]
        out_specs += [panel, panel, face, face, face, face]
        out_shape += [jax.ShapeDtypeStruct((128, WAVES), F32), jax.ShapeDtypeStruct((128, WAVES), BF)]
        out_shape += [jax.ShapeDtypeStruct((3, 8, 8, WAVES), BF)] * 4
    return pl.pallas_call(
        lambda *refs: stencil_kernel(first, *refs),
        grid=(WAVES // LANES,),
        in_specs=in_specs,
        out_specs=out_specs,
        out_shape=out_shape,
        name="stencil_first" if first else "stencil_second",
    )(*args)


def boundary_kernel(first, order_ref, rows_ref, cols_ref, count_ref, *refs):
    chunks = refs[:8]
    single_ref, double_ref, near_ref, extra_ref = refs[8:12]
    refs = refs[12:]
    if first:
        key_ref, out_ref, phi_ref, w_ref, acc_ref = refs
    else:
        out_ref, phi_ref, w_ref, acc_ref = refs
    i = pl.program_id(0)

    @pl.when(i == 0)
    def _():
        for k in range(8):
            at = pl.multiple_of(order_ref[k] * 128, 128)
            phi_ref[pl.ds(at, 128), :] = chunks[k][0]
            w_ref[pl.ds(at, 128), :] = chunks[k][1]

    acc_ref[...] = jnp.dot(single_ref[...], phi_ref[...], preferred_element_type=F32) + jnp.dot(
        double_ref[...], w_ref[...], preferred_element_type=F32
    )
    for k in range(8):
        @pl.when((k < count_ref[0]) & (rows_ref[k] // 2 == i))
        def _():
            row = pl.multiple_of((rows_ref[k] % 2) * 128, 128)
            col = pl.multiple_of(cols_ref[k] * 128, 128)
            acc_ref[pl.ds(row, 128), :] += jnp.dot(
                near_ref[k], phi_ref[pl.ds(col, 128), :], preferred_element_type=F32
            )
    total = acc_ref[...].astype(BF)
    if first:
        m = lax.broadcasted_iota(jnp.int32, (256, 256), 0)
        place = (m // 16) * 8 + m % 8 + 128 * ((m // 8) % 2)
        select = (place == key_ref[...]).astype(F32).astype(BF)
        packed = jnp.dot(select, total, preferred_element_type=F32).astype(BF)
        out_ref[:, pl.ds(pl.multiple_of(i * 16, 16), 16), :] = packed.reshape(16, 16, WAVES)

        @pl.when(i == 7)
        def _():
            out_ref[:, 128:136, :] = extra_ref[...]
    else:
        out_ref[:, 0:128, :] = total.reshape(2, 128, WAVES)
        out_ref[:, 128:136, :] = extra_ref[...]


def boundary(order, near, chunks, single_layer, double_layer, extra, keys=None):
    near_blocks, near_rows, near_cols, near_count = near
    first = keys is not None
    chunk = pl.BlockSpec((2, 128, WAVES), lambda i, *_: (0, 0, 0))
    tile = pl.BlockSpec((256, 1024), lambda i, *_: (i, 0))
    in_specs = [chunk] * 8 + [tile, tile, pl.BlockSpec((8, 128, 128), lambda i, *_: (0, 0, 0))]
    args = [*chunks, single_layer, double_layer, near_blocks, extra]
    if first:
        in_specs += [pl.BlockSpec((16, 8, WAVES), lambda i, *_: (0, 0, 0)),
                     pl.BlockSpec((None, 1, 256), lambda i, *_: (i, 0, 0))]
        args += [keys]
        out_spec = pl.BlockSpec((16, 136, WAVES), lambda i, *_: (0, 0, 0))
    else:
        in_specs += [pl.BlockSpec((2, 8, WAVES), lambda i, *_: (i, 0, 0))]
        out_spec = pl.BlockSpec((2, 136, WAVES), lambda i, *_: (i, 0, 0))
    return pl.pallas_call(
        lambda *refs: boundary_kernel(first, *refs),
        grid_spec=pltpu.PrefetchScalarGridSpec(
            num_scalar_prefetch=4,
            grid=(8,),
            in_specs=in_specs,
            out_specs=out_spec,
            scratch_shapes=[
                pltpu.VMEM((1024, WAVES), BF),
                pltpu.VMEM((1024, WAVES), BF),
                pltpu.VMEM((256, WAVES), F32),
            ],
        ),
        out_shape=jax.ShapeDtypeStruct((16, 136, WAVES), BF),
        name="boundary_first" if first else "boundary_second",
    )(order, near_rows, near_cols, near_count, *args)


def middle_kernel(got_ref, chunk_ref, out_ref):
    total = got_ref[0, 0:128].astype(F32)
    for k in range(1, 16):
        total = total + got_ref[k, 0:128].astype(F32)
    out_ref[0] = (total - 0.5 * chunk_ref[...].astype(F32)).astype(BF)
    out_ref[1] = got_ref[:, 128:136, :].reshape(128, LANES)


def middle(got, chunk):
    return pl.pallas_call(
        middle_kernel,
        grid=(WAVES // LANES,),
        in_specs=[
            pl.BlockSpec((16, 136, LANES), lambda i: (0, 0, i)),
            pl.BlockSpec((None, 128, LANES), lambda i: (1, 0, i)),
        ],
        out_specs=pl.BlockSpec((2, 128, LANES), lambda i: (0, 0, i)),
        out_shape=jax.ShapeDtypeStruct((2, 128, WAVES), BF),
        name="middle",
    )(got, chunk)


def last_kernel(got_ref, w_ref, route_ref, comp_ref, flux_ref, out_ref, mid_ref):
    total = got_ref[0, 0:128].astype(F32)
    for k in range(1, 16):
        total = total + got_ref[k, 0:128].astype(F32)
    flux_ref[...] = total - 0.5 * w_ref[...]
    picker = (lax.broadcasted_iota(jnp.int32, (128, 128), 1) == route_ref[...]).astype(F32).astype(BF)
    mid_ref[...] = jnp.dot(picker, got_ref[:, 128:136, :].reshape(128, LANES), preferred_element_type=F32)
    depth = lax.broadcasted_iota(jnp.int32, (8, LANES), 0)

    def step(x, carry):
        for y in range(8):
            low = mid_ref[pl.ds(x * 8 + y, 1), :]
            high = mid_ref[pl.ds(64 + x * 8 + y, 1), :]
            out_ref[x, y] = comp_ref[x, y] - jnp.where(depth == 0, low, jnp.where(depth == 7, high, 0.0))
        return carry

    lax.fori_loop(0, 8, step, 0)


def last(got, trace, route_column, field):
    comp = pl.BlockSpec((None, 8, 8, 8, LANES), lambda i: (2, 0, 0, 0, i))
    panel = pl.BlockSpec((128, LANES), lambda i: (0, i))
    return pl.pallas_call(
        last_kernel,
        grid=(WAVES // LANES,),
        in_specs=[
            pl.BlockSpec((16, 136, LANES), lambda i: (0, 0, i)),
            panel,
            pl.BlockSpec((128, 1), lambda i: (0, 0)),
            comp,
        ],
        out_specs=[panel, comp],
        out_shape=[jax.ShapeDtypeStruct((128, WAVES), F32), jax.ShapeDtypeStruct(field.shape, F32)],
        scratch_shapes=[pltpu.VMEM((128, LANES), F32)],
        input_output_aliases={3: 1},
        name="last",
    )(got, trace, route_column, field)


def shifted(count, by):
    return [(i, (i + by) % count) for i in range(count)]


def across_rows(chunk):
    row = lax.axis_index("row")
    mine = [chunk] + [lax.ppermute(chunk, "row", shifted(8, k)) for k in (4, 2, 6)]
    beside = [lax.ppermute(one, "row", [(i, i ^ 1) for i in range(8)]) for one in mine]
    order = [(row - k) % 8 for k in (0, 4, 2, 6)]
    order = jnp.stack(order + [one ^ 1 for one in order]).astype(jnp.int32)
    return mine + beside, order


def swap_faces(faces):
    low_x, high_x, low_y, high_y = faces
    up = lambda n: [(i, i + 1) for i in range(n - 1)]
    down = lambda n: [(i + 1, i) for i in range(n - 1)]
    return (
        lax.ppermute(high_x, "row", up(8)),
        lax.ppermute(low_x, "row", down(8)),
        lax.ppermute(high_y, "col", up(16)),
        lax.ppermute(low_y, "col", down(16)),
    )


def local(
    displacement,
    flux,
    stiffness,
    mixing,
    single_layer,
    double_layer,
    near_blocks,
    near_rows,
    near_cols,
    near_counts,
    routes,
):
    near = (near_blocks.reshape(8, 128, 128), near_rows.reshape(8), near_cols.reshape(8), near_counts.reshape(1))
    route_row = routes.reshape(1, 128)
    ends = routes.reshape(2, 64)
    face_row = jnp.concatenate(
        [ends[0][:, None], jnp.full((64, 6), -1, jnp.int32), ends[1][:, None]], axis=1
    ).reshape(1, 512)

    packed = pack(flux, displacement, route_row, face_row)
    got = lax.all_to_all(packed.reshape(16, 8, 2 * WAVES + 128), "col", 0, 0, tiled=True)
    chunk = jnp.stack(
        [got[:, :, :WAVES].reshape(128, WAVES), got[:, :, WAVES : 2 * WAVES].reshape(128, WAVES)], 0
    )
    keys = got[:, 0, 2 * WAVES :].astype(jnp.int32).reshape(8, 2, 128)
    keys = (keys + jnp.array([0, 128], jnp.int32)[None, :, None]).reshape(8, 1, 256)

    faces = [
        displacement[:, 0].astype(BF),
        displacement[:, 7].astype(BF),
        displacement[:, :, 0].astype(BF),
        displacement[:, :, 7].astype(BF),
    ]
    stiff = stiffness[..., None]
    field, trace, outgoing, *faces = stencil(displacement, swap_faces(faces), stiff, mixing, flux, route_row)

    chunks, order = across_rows(chunk)
    sums = boundary(order, near, chunks, single_layer, double_layer, outgoing.reshape(16, 8, WAVES), keys)
    got = lax.all_to_all(sums, "col", 0, 0, tiled=True)
    (field,) = stencil(field, swap_faces(faces), stiff, mixing)
    chunk = middle(got, chunk)

    chunks, order = across_rows(chunk)
    sums = boundary(order, near, chunks, single_layer, double_layer, chunk[0].reshape(16, 8, WAVES))
    got = lax.all_to_all(sums, "col", 0, 0, tiled=True)
    new_flux, field = last(got, trace, routes.reshape(128, 1), field)
    return (field, new_flux)


def solution(mesh):
    return jax.shard_map(
        local,
        mesh=mesh,
        in_specs=(
            P(None, "row", "col", None, None),
            P(("row", "col"), None),
            P("row", "col", None),
            P(),
            P("row", "col"),
            P("row", "col"),
            P("row", "col", None, None),
            P("row", "col"),
            P("row", "col"),
            P("row", "col"),
            P(("row", "col")),
        ),
        out_specs=(P(None, "row", "col", None, None), P(("row", "col"), None)),
        check_vma=False,
    )
```

time: 308 us -> 164 us (0.53)
  matrix products: 52.8 us -> 0 us
  waiting for transfers between devices: 70.8 us -> 21.9 us
  Pallas kernels: 0 us -> 44.5 us
  local copies, waits for them, and re-layouts: 42.5 us -> 14.2 us
  blocking collectives: 57 us -> 34.4 us
  other arithmetic: 15.6 us -> 0.7 us
  between operations: 15.6 us -> 1.72 us
  starting transfers between devices: 49.3 us -> 43.6 us
    all_gather x4 -> x0, blocking collectives: 57 us -> none  [the longest x2 29.2 us: route_panels(): lax.all_gather(swapped[1], 'row', axis=0, tiled=True)]
    dot_general x14 -> x0, matrix products: 52.8 us -> none  [the longest x2 22.5 us: apply_stiffness(): jnp.einsum('ij,jxyzq->ixyzq', mixing, field, precision=lax.Precision.HIGH...]
    pallas_call x0 -> x7, Pallas kernels: none -> 44.5 us  [the longest x2 24.9 us: boundary(): pl.pallas_call(lambda *refs: boundary_kernel(first, *refs), grid_spec=plt...]
    all_to_all x0 -> x1, blocking collectives: none -> 34.4 us  [local(): got = lax.all_to_all(sums, 'col', 0, 0, tiled=True)]
    reduce_scatter x2 -> x0, waiting for transfers between devices: 30.4 us -> none  [apply_once(): lax.psum_scatter(total + near, 'col', scatter_dimension=0, tiled=True)]
    unnamed x89 -> x56, local copies, waits for them, and re-layouts: 21.1 us -> 4.74 us
    all_to_all x4 -> x2, starting transfers between devices: 26 us -> 12.5 us  [the longest x1 8.05 us: local(): lax.all_to_all(packed.reshape(16, 8, 2 * WAVES + 128), 'col', 0, 0, tiled...]
    ppermute x8 -> x22, waiting for transfers between devices: 34.1 us -> 21.8 us  [the longest x2 10.8 us: swap_faces(): lax.ppermute(high_y, 'col', up(16))]
  transfers between devices with their start and end apart: 14 -> 24, of which waited for: 10 -> 7; matrix products, arithmetic and copies ran while one was open for 20% -> 5% of each run, Pallas kernels for 0% -> 7%
where the time goes in v1:
time: 164 us; the launch traced here: 161 us
  Pallas kernels  44.5 us (27%)
  starting transfers between devices  43.6 us (27%)
  blocking collectives  34.4 us (21%)
  waiting for transfers between devices  21.9 us (13%)
  local copies, waits for them, and re-layouts  14.2 us (9%)
  between operations  1.72 us (1%)
    all_to_all x1, blocking collectives, local(): got = lax.all_to_all(sums, 'col', 0, 0, tiled=True)  34.4 us
    pallas_call x2, Pallas kernels, boundary(): pl.pallas_call(lambda *refs: boundary_kernel(first, *refs), grid_spec=plt...  24.9 us
    ppermute x2, waiting for transfers between devices, swap_faces(): lax.ppermute(high_y, 'col', up(16))  10.8 us
    pallas_call x2, Pallas kernels, stencil(): pl.pallas_call(lambda *refs: stencil_kernel(first, *refs), grid=(WAVES //...  10.6 us
    ppermute x2, starting transfers between devices, swap_faces(): lax.ppermute(high_y, 'col', up(16))  8.39 us
    ppermute x6, waiting for transfers between devices, across_rows(): lax.ppermute(chunk, 'row', shifted(8, k))  8.2 us
    all_to_all x1, starting transfers between devices, local(): lax.all_to_all(packed.reshape(16, 8, 2 * WAVES + 128), 'col', 0, 0, tiled...  8.05 us
    ppermute x6, starting transfers between devices, across_rows(): lax.ppermute(chunk, 'row', shifted(8, k))  7.9 us
  transfers between devices with their start and end apart: 24, of which 7 were waited for; matrix products, arithmetic and copies ran while one was open for 5% of the time, Pallas kernels for 7%

profile of v1, /device:TPU:2, one launch (start us, length us, event | category | flops | bytes accessed | tf_op | source)
XLA Modules:
  0.0 161.0 jit_solution(635597035852196144)
XLA Ops:
  0.6 0.8 slice_bitcast_fusion.8
  1.4 0.1 pad.3.clone
  1.5 0.1 pad_add_fusion
  1.6 0.1 copy.29
  1.7 0.7 reshape.85.face_ref
  2.4 2.1 %pack.1 = bf16[128,896]{1,0:T(8,128)(2,1)} custom-call(f32[128,384]{1,0:T(8,128)} %refs_7_.1, f32[3,8,8,8,384]{4,3,2,1,0:T(8,128)} %refs_1_.1, s32[1,128]{1,0:T(1,128)} %bitcast.47, s32[1,512]{1,0:T(1,128)} %reshape.85.face_ref), custom_call_target="tpu_custom_call" | custom-call | tf_op jit(solution)/shard_map/pack/pallas_call | solution.py:29
  4.5 8.0 %all-to-all-start = ((bf16[16,8,896]{2,1,0:T(8,128)(2,1)}), bf16[16,8,896]{2,1,0:T(8,128)(2,1)S(1)}, u32[]{:S(2)}, u32[]{:S(2)}) async-start(bf16[16,8,896]{2,1,0:T(8,128)(2,1)} %bitcast.43), calls=%async_computation | async-start | bytes 458752 | tf_op jit(solution)/shard_map/all_to_all | solution.py:304
  12.5 1.1 slice_bitcast_fusion.2
  13.6 1.9 %collective-permute-start.7 = (bf16[3,8,8,384]{3,2,0,1:T(8,128)(2,1)S(1)}, bf16[3,8,8,384]{3,2,0,1:T(8,128)(2,1)S(1)}, u32[]{:S(2)}, u32[]{:S(2)}) collective-permute-start(bf16[3,8,8,384]{3,2,0,1:T(8,128)(2,1)S(1)} %get-tuple-element.23), channel_id=1, source_target_pairs={{0,16},{16,32},{32,48},{48,64},{64,80},{80,96},{96,112},{1,17},{17... | collective-permute-start | bytes 442376 | tf_op jit(solution)/shard_map/ppermute | solution.py:276
  15.5 3.6 %collective-permute-start.8 = (bf16[3,8,8,384]{3,2,0,1:T(8,128)(2,1)S(1)}, bf16[3,8,8,384]{3,2,0,1:T(8,128)(2,1)S(1)}, u32[]{:S(2)}, u32[]{:S(2)}) collective-permute-start(bf16[3,8,8,384]{3,2,0,1:T(8,128)(2,1)S(1)} %get-tuple-element.22), channel_id=1, source_target_pairs={{16,0},{32,16},{48,32},{64,48},{80,64},{96,80},{112,96},{17,1},{33... | collective-permute-start | bytes 442376 | tf_op jit(solution)/shard_map/ppermute | solution.py:277
  19.2 1.1 slice_bitcast_fusion
  20.3 1.3 collective-permute-start.10
  21.6 4.6 %collective-permute-start.9 = (bf16[3,8,8,384]{3,2,1,0:T(8,128)(2,1)S(1)}, bf16[3,8,8,384]{3,2,1,0:T(8,128)(2,1)S(1)}, u32[]{:S(2)}, u32[]{:S(2)}) collective-permute-start(bf16[3,8,8,384]{3,2,1,0:T(8,128)(2,1)S(1)} %get-tuple-element.21), channel_id=1, source_target_pairs={{0,1},{1,2},{2,3},{3,4},{4,5},{5,6},{6,7},{7,8},{8,9},{9,10},{10,1... | collective-permute-start | bytes 442376 | tf_op jit(solution)/shard_map/ppermute | solution.py:278
  26.2 1.1 copy.33.refs_6_
  28.0 0.7 stack.47.refs_0_
  28.8 0.0 copy-start.1
  28.8 2.2 %collective-permute-start = (bf16[2,128,384]{2,1,0:T(8,128)(2,1)S(1)}, bf16[2,128,384]{2,1,0:T(8,128)(2,1)S(1)}, u32[]{:S(2)}, u32[]{:S(2)}) collective-permute-start(bf16[2,128,384]{2,1,0:T(8,128)(2,1)S(1)} %pad_maximum_fusion.refs_4_.chunk_ref), channel_id=1, source_target_pairs={{0,64},{16,80},{32,96},{48,112},{64,0},{80,16},{96,32},{112,48},{1... | collective-permute-start | bytes 589832 | tf_op jit(solution)/shard_map/ppermute | solution.py:264
  31.0 0.0 collective-permute-done.7
  31.0 0.0 collective-permute-start.1
  31.0 2.0 %collective-permute-start.2 = (bf16[2,128,384]{2,1,0:T(8,128)(2,1)S(1)}, bf16[2,128,384]{2,1,0:T(8,128)(2,1)S(1)}, u32[]{:S(2)}, u32[]{:S(2)}) collective-permute-start(bf16[2,128,384]{2,1,0:T(8,128)(2,1)S(1)} %pad_maximum_fusion.refs_4_.chunk_ref), channel_id=1, source_target_pairs={{0,96},{16,112},{32,0},{48,16},{64,32},{80,48},{96,64},{112,80},{1... | collective-permute-start | bytes 589832 | tf_op jit(solution)/shard_map/ppermute | solution.py:264
  33.0 0.1 broadcast_bitcast_fusion
  33.1 0.7 copy.31.refs_2_
  33.8 0.7 copy.32.refs_3_
  34.5 0.7 copy-done.16
  35.1 0.7 copy-done.17
  35.8 5.4 %stencil_first.1 = (f32[3,8,8,8,384]{4,3,2,1,0:T(8,128)}, f32[128,384]{1,0:T(8,128)}, bf16[128,384]{1,0:T(8,128)(2,1)}, bf16[3,8,8,384]{3,2,1,0:T(8,128)(2,1)}, ...) custom-call(f32[3,3]{1,0:T(4,128)} %refs_0_.3, ...), custom_call_target="tpu_custom_call" | custom-call | tf_op jit(solution)/shard_map/stencil_first/pallas_call | solution.py:110
  41.2 0.1 collective-permute-start.3
  41.3 0.6 collective-permute-start.4
  41.9 0.1 collective-permute-start.5
  42.0 0.4 collective-permute-start.6
  42.4 0.6 convert_add_fusion.refs_16_
  43.0 0.3 collective-permute-done.5.refs_10_
  43.3 0.3 collective-permute-done.6.refs_11_
  43.6 0.0 copy-done.8
  43.7 0.1 copy-done.10
  43.8 0.3 copy-done.12
  44.0 0.3 copy-done.14
  44.3 13.0 %boundary_first.1 = bf16[16,136,384]{2,1,0:T(8,128)(2,1)} custom-call(s32[8]{0:T(128)} %stack.47.refs_0_, s32[8]{0:T(128)} %bitcast.50, s32[8]{0:T(128)} %bitcast.52, s32[1]{0:T(128)} %bitcast.39.refs_3_, bf16[2,128,384]{2,1,0:T(8,128)(2,1)} %copy-done.1, bf16[2,128,384]{2,1,0:T(8,128)(2,1)} %copy-done.2, bf16[2,128,384]{2,1,0:T(8,128)(2,1)} %copy-done.3, ...), custom_call_target="tpu_custom_call" | custom-call | tf_op jit(solution)/shard_map/boundary_first/pallas_call | solution.py:179
  57.3 34.4 %all_to_all.15.got_ref = bf16[16,136,384]{2,1,0:T(8,128)(2,1)} all-to-all(bf16[16,136,384]{2,1,0:T(8,128)(2,1)} %boundary_first.1), channel_id=1, replica_groups=mesh['row'=8,'col'=16] {'col'}, dimensions={0} | all-to-all | bytes 3342336 | tf_op jit(solution)/shard_map/all_to_all | solution.py:322
  91.7 3.0 %middle.1.refs_4_ = bf16[2,128,384]{2,1,0:T(8,128)(2,1)} custom-call(bf16[16,136,384]{2,1,0:T(8,128)(2,1)} %all_to_all.15.got_ref, bf16[2,128,384]{2,1,0:T(8,128)(2,1)} %copy-done.1), custom_call_target="tpu_custom_call" | custom-call | tf_op jit(solution)/shard_map/middle/pallas_call | solution.py:206
  94.7 0.7 collective-permute-start.11
  95.4 3.0 %collective-permute-start.12 = (bf16[2,128,384]{2,1,0:T(8,128)(2,1)}, bf16[2,128,384]{2,1,0:T(8,128)(2,1)S(1)}, u32[]{:S(2)}, u32[]{:S(2)}) collective-permute-start(bf16[2,128,384]{2,1,0:T(8,128)(2,1)} %middle.1.refs_4_), channel_id=1, source_target_pairs={{0,32},{16,48},{32,64},{48,80},{64,96},{80,112},{96,0},{112,16},{1... | collective-permute-start | bytes 589832 | tf_op jit(solution)/shard_map/ppermute | solution.py:264
  98.3 5.8 %collective-permute-done.11.refs_5_ = bf16[2,128,384]{2,1,0:T(8,128)(2,1)S(1)} collective-permute-done((bf16[2,128,384]{2,1,0:T(8,128)(2,1)}, bf16[2,128,384]{2,1,0:T(8,128)(2,1)S(1)}, u32[]{:S(2)}, u32[]{:S(2)}) %collective-permute-start.11) | collective-permute-done | bytes 196640 | tf_op jit(solution)/shard_map/ppermute | solution.py:264
  104.2 0.7 collective-permute-done.12.refs_6_
  104.9 1.7 %collective-permute-done.13.refs_7_ = bf16[2,128,384]{2,1,0:T(8,128)(2,1)S(1)} collective-permute-done((bf16[2,128,384]{2,1,0:T(8,128)(2,1)}, bf16[2,128,384]{2,1,0:T(8,128)(2,1)S(1)}, u32[]{:S(2)}, u32[]{:S(2)}) %collective-permute-start.13) | collective-permute-done | bytes 196640 | tf_op jit(solution)/shard_map/ppermute | solution.py:264
  106.5 1.6 slice_bitcast_fusion.4.refs_15_
  108.2 0.6 copy-done.9
  108.8 0.1 copy-done.11
  108.9 0.1 copy-done.13
  109.0 0.1 copy-done.15
  109.0 11.9 %boundary_second.1 = bf16[16,136,384]{2,1,0:T(8,128)(2,1)} custom-call(s32[8]{0:T(128)} %stack.47.refs_0_, s32[8]{0:T(128)} %bitcast.51, s32[8]{0:T(128)} %bitcast.53, s32[1]{0:T(128)} %bitcast.40.refs_3_, bf16[2,128,384]{2,1,0:T(8,128)(2,1)} %middle.1.refs_4_, bf16[2,128,384]{2,1,0:T(8,128)(2,1)} %copy-done.5, bf16[2,128,384]{2,1,0:T(8,128)(2,1)} %copy-done.6, ...), custom_call_target="tpu_custom_call" | custom-call | tf_op jit(solution)/shard_map/boundary_second/pallas_call | solution.py:179
  121.0 0.0 copy-start.23
  121.0 4.4 %all-to-all-start.2 = ((bf16[16,136,384]{2,1,0:T(8,128)(2,1)}), bf16[16,136,384]{2,1,0:T(8,128)(2,1)S(1)}, u32[]{:S(2)}, u32[]{:S(2)}) async-start(bf16[16,136,384]{2,1,0:T(8,128)(2,1)} %boundary_second.1), calls=%async_computation.2 | async-start | bytes 3342336 | tf_op jit(solution)/shard_map/all_to_all | solution.py:328
  125.4 2.2 %collective-permute-start.18 = (bf16[3,8,8,384]{3,2,1,0:T(8,128)(2,1)S(1)}, bf16[3,8,8,384]{3,2,1,0:T(8,128)(2,1)S(1)}, u32[]{:S(2)}, u32[]{:S(2)}) collective-permute-start(bf16[3,8,8,384]{3,2,1,0:T(8,128)(2,1)S(1)} %copy-done.27), channel_id=1, source_target_pairs={{0,16},{16,32},{32,48},{48,64},{64,80},{80,96},{96,112},{1,17},{17... | collective-permute-start | bytes 442376 | tf_op jit(solution)/shard_map/ppermute | solution.py:276
  127.7 3.3 %collective-permute-start.19 = (bf16[3,8,8,384]{3,2,1,0:T(8,128)(2,1)S(1)}, bf16[3,8,8,384]{3,2,1,0:T(8,128)(2,1)S(1)}, u32[]{:S(2)}, u32[]{:S(2)}) collective-permute-start(bf16[3,8,8,384]{3,2,1,0:T(8,128)(2,1)S(1)} %copy-done.26), channel_id=1, source_target_pairs={{16,0},{32,16},{48,32},{64,48},{80,64},{96,80},{112,96},{17,1},{33... | collective-permute-start | bytes 442376 | tf_op jit(solution)/shard_map/ppermute | solution.py:277
  131.0 3.8 %collective-permute-start.20 = (bf16[3,8,8,384]{3,2,1,0:T(8,128)(2,1)S(1)}, bf16[3,8,8,384]{3,2,1,0:T(8,128)(2,1)S(1)}, u32[]{:S(2)}, u32[]{:S(2)}) collective-permute-start(bf16[3,8,8,384]{3,2,1,0:T(8,128)(2,1)S(1)} %copy-done.25), channel_id=1, source_target_pairs={{0,1},{1,2},{2,3},{3,4},{4,5},{5,6},{6,7},{7,8},{8,9},{9,10},{10,1... | collective-permute-start | bytes 442376 | tf_op jit(solution)/shard_map/ppermute | solution.py:278
  134.9 1.3 collective-permute-start.21
  136.2 0.7 copy.35.route_ref
  136.9 10.8 %collective-permute-done.20.refs_4_ = bf16[3,8,8,384]{3,2,1,0:T(8,128)(2,1)S(1)} collective-permute-done((bf16[3,8,8,384]{3,2,1,0:T(8,128)(2,1)S(1)}, bf16[3,8,8,384]{3,2,1,0:T(8,128)(2,1)S(1)}, u32[]{:S(2)}, u32[]{:S(2)}) %collective-permute-start.20) | collective-permute-done | bytes 147488 | tf_op jit(solution)/shard_map/ppermute | solution.py:278
  147.8 2.2 %collective-permute-done.21.refs_5_ = bf16[3,8,8,384]{3,2,1,0:T(8,128)(2,1)S(1)} collective-permute-done((bf16[3,8,8,384]{3,2,1,0:T(8,128)(2,1)S(1)}, bf16[3,8,8,384]{3,2,1,0:T(8,128)(2,1)S(1)}, u32[]{:S(2)}, u32[]{:S(2)}) %collective-permute-start.21) | collective-permute-done | bytes 147488 | tf_op jit(solution)/shard_map/ppermute | solution.py:279
  150.0 0.7 copy-done.21
  150.6 5.2 %stencil_second.1.comp_ref = f32[3,8,8,8,384]{4,3,2,1,0:T(8,128)} custom-call(f32[3,3]{1,0:T(4,128)} %refs_0_.3, f32[3,8,8,8,384]{4,3,2,1,0:T(8,128)} %get-tuple-element.13.refs_1_, bf16[3,8,8,384]{3,2,1,0:T(8,128)(2,1)} %copy-done.18, bf16[3,8,8,384]{3,2,1,0:T(8,128)(2,1)} %copy-done.19, bf16[3,8,8,384]{3,2,1,0:T(8,128)(2,1)} %copy-done.20, ...), custom_call_target="tpu_custom_call" | custom-call | tf_op jit(solution)/shard_map/stencil_second/pallas_call | solution.py:110
  155.9 1.2 copy-done
  157.1 3.9 %last.1 = (f32[128,384]{1,0:T(8,128)}, f32[3,8,8,8,384]{4,3,2,1,0:T(8,128)}) custom-call(bf16[16,136,384]{2,1,0:T(8,128)(2,1)} %copy-done, f32[128,384]{1,0:T(8,128)} %get-tuple-element.12.w_ref, s32[128,1]{1,0:T(8,128)} %copy.35.route_ref, f32[3,8,8,8,384]{4,3,2,1,0:T(8,128)} %stencil_second.1.comp_ref), custom_call_target="tpu_custom_call", output_to_operand_aliasing={{1}: (3, {})} | custom-call | tf_op jit(solution)/shard_map/last/pallas_call | solution.py:241
  (68 shorter events, 0.2 us)
Async XLA Ops:
  0.6 25.6 %copy-start.22 = (f32[8,8,8]{2,1,0:T(8,128)S(1)}, f32[8,8,8]{2,1,0:T(8,128)}, u32[]{:S(2)}) copy-start(f32[8,8,8]{2,1,0:T(8,128)} %param.14) | copy-start | bytes 6148
  4.5 24.3 %all-to-all-start = ((bf16[16,8,896]{2,1,0:T(8,128)(2,1)}), bf16[16,8,896]{2,1,0:T(8,128)(2,1)S(1)}, u32[]{:S(2)}, u32[]{:S(2)}) async-start(bf16[16,8,896]{2,1,0:T(8,128)(2,1)} %bitcast.43), calls=%async_computation | async-start | bytes 458752 | tf_op jit(solution)/shard_map/all_to_all | solution.py:304
  13.6 17.4 %collective-permute-start.7 = (bf16[3,8,8,384]{3,2,0,1:T(8,128)(2,1)S(1)}, bf16[3,8,8,384]{3,2,0,1:T(8,128)(2,1)S(1)}, u32[]{:S(2)}, u32[]{:S(2)}) collective-permute-start(bf16[3,8,8,384]{3,2,0,1:T(8,128)(2,1)S(1)} %get-tuple-element.23), channel_id=1, source_target_pairs={{0,16},{16,32},{32,48},{48,64},{64,80},{80,96},{96,112},{1,17},{17... | collective-permute-start | bytes 442376 | tf_op jit(solution)/shard_map/ppermute | solution.py:276
  15.5 15.5 %collective-permute-start.8 = (bf16[3,8,8,384]{3,2,0,1:T(8,128)(2,1)S(1)}, bf16[3,8,8,384]{3,2,0,1:T(8,128)(2,1)S(1)}, u32[]{:S(2)}, u32[]{:S(2)}) collective-permute-start(bf16[3,8,8,384]{3,2,0,1:T(8,128)(2,1)S(1)} %get-tuple-element.22), channel_id=1, source_target_pairs={{16,0},{32,16},{48,32},{64,48},{80,64},{96,80},{112,96},{17,1},{33... | collective-permute-start | bytes 442376 | tf_op jit(solution)/shard_map/ppermute | solution.py:277
  20.3 14.2 %collective-permute-start.10 = (bf16[3,8,8,384]{3,2,1,0:T(8,128)(2,1)S(1)}, bf16[3,8,8,384]{3,2,1,0:T(8,128)(2,1)S(1)}, u32[]{:S(2)}, u32[]{:S(2)}) collective-permute-start(bf16[3,8,8,384]{3,2,1,0:T(8,128)(2,1)S(1)} %get-tuple-element.20), channel_id=1, source_target_pairs={{1,0},{2,1},{3,2},{4,3},{5,4},{6,5},{7,6},{8,7},{9,8},{10,9},{11,1... | collective-permute-start | bytes 442376 | tf_op jit(solution)/shard_map/ppermute | solution.py:279
  21.6 12.9 %collective-permute-start.9 = (bf16[3,8,8,384]{3,2,1,0:T(8,128)(2,1)S(1)}, bf16[3,8,8,384]{3,2,1,0:T(8,128)(2,1)S(1)}, u32[]{:S(2)}, u32[]{:S(2)}) collective-permute-start(bf16[3,8,8,384]{3,2,1,0:T(8,128)(2,1)S(1)} %get-tuple-element.21), channel_id=1, source_target_pairs={{0,1},{1,2},{2,3},{3,4},{4,5},{5,6},{6,7},{7,8},{8,9},{9,10},{10,1... | collective-permute-start | bytes 442376 | tf_op jit(solution)/shard_map/ppermute | solution.py:278
  28.8 14.8 %copy-start.1 = (bf16[2,128,384]{2,1,0:T(8,128)(2,1)}, bf16[2,128,384]{2,1,0:T(8,128)(2,1)S(1)}, u32[]{:S(2)}) copy-start(bf16[2,128,384]{2,1,0:T(8,128)(2,1)S(1)} %pad_maximum_fusion.refs_4_.chunk_ref) | copy-start | bytes 589828
  28.8 12.5 %collective-permute-start = (bf16[2,128,384]{2,1,0:T(8,128)(2,1)S(1)}, bf16[2,128,384]{2,1,0:T(8,128)(2,1)S(1)}, u32[]{:S(2)}, u32[]{:S(2)}) collective-permute-start(bf16[2,128,384]{2,1,0:T(8,128)(2,1)S(1)} %pad_maximum_fusion.refs_4_.chunk_ref), channel_id=1, source_target_pairs={{0,64},{16,80},{32,96},{48,112},{64,0},{80,16},{96,32},{112,48},{1... | collective-permute-start | bytes 589832 | tf_op jit(solution)/shard_map/ppermute | solution.py:264
  31.0 10.9 %collective-permute-start.1 = (bf16[2,128,384]{2,1,0:T(8,128)(2,1)S(1)}, bf16[2,128,384]{2,1,0:T(8,128)(2,1)S(1)}, u32[]{:S(2)}, u32[]{:S(2)}) collective-permute-start(bf16[2,128,384]{2,1,0:T(8,128)(2,1)S(1)} %pad_maximum_fusion.refs_4_.chunk_ref), channel_id=1, source_target_pairs={{0,32},{16,48},{32,64},{48,80},{64,96},{80,112},{96,0},{112,16},{1... | collective-permute-start | bytes 589832 | tf_op jit(solution)/shard_map/ppermute | solution.py:264
  31.0 11.0 %collective-permute-start.2 = (bf16[2,128,384]{2,1,0:T(8,128)(2,1)S(1)}, bf16[2,128,384]{2,1,0:T(8,128)(2,1)S(1)}, u32[]{:S(2)}, u32[]{:S(2)}) collective-permute-start(bf16[2,128,384]{2,1,0:T(8,128)(2,1)S(1)} %pad_maximum_fusion.refs_4_.chunk_ref), channel_id=1, source_target_pairs={{0,96},{16,112},{32,0},{48,16},{64,32},{80,48},{96,64},{112,80},{1... | collective-permute-start | bytes 589832 | tf_op jit(solution)/shard_map/ppermute | solution.py:264
  34.5 0.7 copy-start.16
  35.1 0.7 copy-start.17
  41.2 1.8 %collective-permute-start.3 = (bf16[2,128,384]{2,1,0:T(8,128)(2,1)S(1)}, bf16[2,128,384]{2,1,0:T(8,128)(2,1)S(1)}, u32[]{:S(2)}, u32[]{:S(2)}) collective-permute-start(bf16[2,128,384]{2,1,0:T(8,128)(2,1)S(1)} %pad_maximum_fusion.refs_4_.chunk_ref), channel_id=1, source_target_pairs={{0,16},{16,0},{32,48},{48,32},{64,80},{80,64},{96,112},{112,96},{1... | collective-permute-start | bytes 589832 | tf_op jit(solution)/shard_map/ppermute | solution.py:265
  41.3 2.3 %copy-start.2 = (bf16[2,128,384]{2,1,0:T(8,128)(2,1)}, bf16[2,128,384]{2,1,0:T(8,128)(2,1)S(1)}, u32[]{:S(2)}) copy-start(bf16[2,128,384]{2,1,0:T(8,128)(2,1)S(1)} %collective-permute-done.refs_5_) | copy-start | bytes 589828
  41.3 1.7 %collective-permute-start.4 = (bf16[2,128,384]{2,1,0:T(8,128)(2,1)S(1)}, bf16[2,128,384]{2,1,0:T(8,128)(2,1)S(1)}, u32[]{:S(2)}, u32[]{:S(2)}) collective-permute-start(bf16[2,128,384]{2,1,0:T(8,128)(2,1)S(1)} %collective-permute-done.refs_5_), channel_id=1, source_target_pairs={{0,16},{16,0},{32,48},{48,32},{64,80},{80,64},{96,112},{112,96},{1... | collective-permute-start | bytes 589832 | tf_op jit(solution)/shard_map/ppermute | solution.py:265
  41.9 1.7 %copy-start.3 = (bf16[2,128,384]{2,1,0:T(8,128)(2,1)}, bf16[2,128,384]{2,1,0:T(8,128)(2,1)S(1)}, u32[]{:S(2)}) copy-start(bf16[2,128,384]{2,1,0:T(8,128)(2,1)S(1)} %collective-permute-done.1.refs_6_) | copy-start | bytes 589828
  41.9 1.4 collective-permute-start.5
  42.0 1.6 %copy-start.4 = (bf16[2,128,384]{2,1,0:T(8,128)(2,1)}, bf16[2,128,384]{2,1,0:T(8,128)(2,1)S(1)}, u32[]{:S(2)}) copy-start(bf16[2,128,384]{2,1,0:T(8,128)(2,1)S(1)} %collective-permute-done.2.refs_7_) | copy-start | bytes 589828
  42.0 1.6 collective-permute-start.6
  43.0 0.7 copy-start.8
  43.0 0.7 copy-start.10
  43.3 0.7 copy-start.12
  43.6 0.7 copy-start.14
  94.7 9.5 %collective-permute-start.11 = (bf16[2,128,384]{2,1,0:T(8,128)(2,1)}, bf16[2,128,384]{2,1,0:T(8,128)(2,1)S(1)}, u32[]{:S(2)}, u32[]{:S(2)}) collective-permute-start(bf16[2,128,384]{2,1,0:T(8,128)(2,1)} %middle.1.refs_4_), channel_id=1, source_target_pairs={{0,64},{16,80},{32,96},{48,112},{64,0},{80,16},{96,32},{112,48},{1... | collective-permute-start | bytes 589832 | tf_op jit(solution)/shard_map/ppermute | solution.py:264
  95.4 9.5 %collective-permute-start.12 = (bf16[2,128,384]{2,1,0:T(8,128)(2,1)}, bf16[2,128,384]{2,1,0:T(8,128)(2,1)S(1)}, u32[]{:S(2)}, u32[]{:S(2)}) collective-permute-start(bf16[2,128,384]{2,1,0:T(8,128)(2,1)} %middle.1.refs_4_), channel_id=1, source_target_pairs={{0,32},{16,48},{32,64},{48,80},{64,96},{80,112},{96,0},{112,16},{1... | collective-permute-start | bytes 589832 | tf_op jit(solution)/shard_map/ppermute | solution.py:264
  98.3 8.2 %collective-permute-start.13 = (bf16[2,128,384]{2,1,0:T(8,128)(2,1)}, bf16[2,128,384]{2,1,0:T(8,128)(2,1)S(1)}, u32[]{:S(2)}, u32[]{:S(2)}) collective-permute-start(bf16[2,128,384]{2,1,0:T(8,128)(2,1)} %middle.1.refs_4_), channel_id=1, source_target_pairs={{0,96},{16,112},{32,0},{48,16},{64,32},{80,48},{96,64},{112,80},{1... | collective-permute-start | bytes 589832 | tf_op jit(solution)/shard_map/ppermute | solution.py:264
  98.3 9.8 %collective-permute-start.14 = (bf16[2,128,384]{2,1,0:T(8,128)(2,1)}, bf16[2,128,384]{2,1,0:T(8,128)(2,1)S(1)}, u32[]{:S(2)}, u32[]{:S(2)}) collective-permute-start(bf16[2,128,384]{2,1,0:T(8,128)(2,1)} %middle.1.refs_4_), channel_id=1, source_target_pairs={{0,16},{16,0},{32,48},{48,32},{64,80},{80,64},{96,112},{112,96},{1... | collective-permute-start | bytes 589832 | tf_op jit(solution)/shard_map/ppermute | solution.py:265
  104.1 4.1 %copy-start.5 = (bf16[2,128,384]{2,1,0:T(8,128)(2,1)}, bf16[2,128,384]{2,1,0:T(8,128)(2,1)S(1)}, u32[]{:S(2)}) copy-start(bf16[2,128,384]{2,1,0:T(8,128)(2,1)S(1)} %collective-permute-done.11.refs_5_) | copy-start | bytes 589828
  104.2 4.0 %collective-permute-start.15 = (bf16[2,128,384]{2,1,0:T(8,128)(2,1)S(1)}, bf16[2,128,384]{2,1,0:T(8,128)(2,1)S(1)}, u32[]{:S(2)}, u32[]{:S(2)}) collective-permute-start(bf16[2,128,384]{2,1,0:T(8,128)(2,1)S(1)} %collective-permute-done.11.refs_5_), channel_id=1, source_target_pairs={{0,16},{16,0},{32,48},{48,32},{64,80},{80,64},{96,112},{112,96},{1... | collective-permute-start | bytes 589832 | tf_op jit(solution)/shard_map/ppermute | solution.py:265
  104.9 3.4 %copy-start.6 = (bf16[2,128,384]{2,1,0:T(8,128)(2,1)}, bf16[2,128,384]{2,1,0:T(8,128)(2,1)S(1)}, u32[]{:S(2)}) copy-start(bf16[2,128,384]{2,1,0:T(8,128)(2,1)S(1)} %collective-permute-done.12.refs_6_) | copy-start | bytes 589828
  104.9 3.3 %collective-permute-start.16 = (bf16[2,128,384]{2,1,0:T(8,128)(2,1)S(1)}, bf16[2,128,384]{2,1,0:T(8,128)(2,1)S(1)}, u32[]{:S(2)}, u32[]{:S(2)}) collective-permute-start(bf16[2,128,384]{2,1,0:T(8,128)(2,1)S(1)} %collective-permute-done.12.refs_6_), channel_id=1, source_target_pairs={{0,16},{16,0},{32,48},{48,32},{64,80},{80,64},{96,112},{112,96},{1... | collective-permute-start | bytes 589832 | tf_op jit(solution)/shard_map/ppermute | solution.py:265
  106.5 1.7 %copy-start.7 = (bf16[2,128,384]{2,1,0:T(8,128)(2,1)}, bf16[2,128,384]{2,1,0:T(8,128)(2,1)S(1)}, u32[]{:S(2)}) copy-start(bf16[2,128,384]{2,1,0:T(8,128)(2,1)S(1)} %collective-permute-done.13.refs_7_) | copy-start | bytes 589828
  106.5 1.7 %collective-permute-start.17 = (bf16[2,128,384]{2,1,0:T(8,128)(2,1)S(1)}, bf16[2,128,384]{2,1,0:T(8,128)(2,1)S(1)}, u32[]{:S(2)}, u32[]{:S(2)}) collective-permute-start(bf16[2,128,384]{2,1,0:T(8,128)(2,1)S(1)} %collective-permute-done.13.refs_7_), channel_id=1, source_target_pairs={{0,16},{16,0},{32,48},{48,32},{64,80},{80,64},{96,112},{112,96},{1... | collective-permute-start | bytes 589832 | tf_op jit(solution)/shard_map/ppermute | solution.py:265
  108.2 0.7 copy-start.9
  108.2 0.8 copy-start.11
  108.2 0.8 copy-start.13
  108.2 0.8 copy-start.15
  120.9 4.5 %copy-start.27 = (bf16[3,8,8,384]{3,2,1,0:T(8,128)(2,1)S(1)}, bf16[3,8,8,384]{3,2,1,0:T(8,128)(2,1)}, u32[]{:S(2)}) copy-start(bf16[3,8,8,384]{3,2,1,0:T(8,128)(2,1)} %get-tuple-element.14) | copy-start | bytes 442372
  120.9 6.7 %copy-start.26 = (bf16[3,8,8,384]{3,2,1,0:T(8,128)(2,1)S(1)}, bf16[3,8,8,384]{3,2,1,0:T(8,128)(2,1)}, u32[]{:S(2)}) copy-start(bf16[3,8,8,384]{3,2,1,0:T(8,128)(2,1)} %get-tuple-element.15) | copy-start | bytes 442372
  120.9 10.1 %copy-start.25 = (bf16[3,8,8,384]{3,2,1,0:T(8,128)(2,1)S(1)}, bf16[3,8,8,384]{3,2,1,0:T(8,128)(2,1)}, u32[]{:S(2)}) copy-start(bf16[3,8,8,384]{3,2,1,0:T(8,128)(2,1)} %get-tuple-element.16) | copy-start | bytes 442372
  121.0 13.9 %copy-start.24 = (bf16[3,8,8,384]{3,2,1,0:T(8,128)(2,1)S(1)}, bf16[3,8,8,384]{3,2,1,0:T(8,128)(2,1)}, u32[]{:S(2)}) copy-start(bf16[3,8,8,384]{3,2,1,0:T(8,128)(2,1)} %get-tuple-element.17) | copy-start | bytes 442372
  121.0 15.2 %copy-start.23 = (s32[128]{0:T(128)S(1)}, s32[128]{0:T(128)}, u32[]{:S(2)}) copy-start(s32[128]{0:T(128)} %param.22) | copy-start | bytes 1540
  121.0 34.9 %all-to-all-start.2 = ((bf16[16,136,384]{2,1,0:T(8,128)(2,1)}), bf16[16,136,384]{2,1,0:T(8,128)(2,1)S(1)}, u32[]{:S(2)}, u32[]{:S(2)}) async-start(bf16[16,136,384]{2,1,0:T(8,128)(2,1)} %boundary_second.1), calls=%async_computation.2 | async-start | bytes 3342336 | tf_op jit(solution)/shard_map/all_to_all | solution.py:328
  125.4 11.5 %collective-permute-start.18 = (bf16[3,8,8,384]{3,2,1,0:T(8,128)(2,1)S(1)}, bf16[3,8,8,384]{3,2,1,0:T(8,128)(2,1)S(1)}, u32[]{:S(2)}, u32[]{:S(2)}) collective-permute-start(bf16[3,8,8,384]{3,2,1,0:T(8,128)(2,1)S(1)} %copy-done.27), channel_id=1, source_target_pairs={{0,16},{16,32},{32,48},{48,64},{64,80},{80,96},{96,112},{1,17},{17... | collective-permute-start | bytes 442376 | tf_op jit(solution)/shard_map/ppermute | solution.py:276
  127.7 9.3 %collective-permute-start.19 = (bf16[3,8,8,384]{3,2,1,0:T(8,128)(2,1)S(1)}, bf16[3,8,8,384]{3,2,1,0:T(8,128)(2,1)S(1)}, u32[]{:S(2)}, u32[]{:S(2)}) collective-permute-start(bf16[3,8,8,384]{3,2,1,0:T(8,128)(2,1)S(1)} %copy-done.26), channel_id=1, source_target_pairs={{16,0},{32,16},{48,32},{64,48},{80,64},{96,80},{112,96},{17,1},{33... | collective-permute-start | bytes 442376 | tf_op jit(solution)/shard_map/ppermute | solution.py:277
  131.0 16.7 %collective-permute-start.20 = (bf16[3,8,8,384]{3,2,1,0:T(8,128)(2,1)S(1)}, bf16[3,8,8,384]{3,2,1,0:T(8,128)(2,1)S(1)}, u32[]{:S(2)}, u32[]{:S(2)}) collective-permute-start(bf16[3,8,8,384]{3,2,1,0:T(8,128)(2,1)S(1)} %copy-done.25), channel_id=1, source_target_pairs={{0,1},{1,2},{2,3},{3,4},{4,5},{5,6},{6,7},{7,8},{8,9},{9,10},{10,1... | collective-permute-start | bytes 442376 | tf_op jit(solution)/shard_map/ppermute | solution.py:278
  134.9 15.1 %collective-permute-start.21 = (bf16[3,8,8,384]{3,2,1,0:T(8,128)(2,1)S(1)}, bf16[3,8,8,384]{3,2,1,0:T(8,128)(2,1)S(1)}, u32[]{:S(2)}, u32[]{:S(2)}) collective-permute-start(bf16[3,8,8,384]{3,2,1,0:T(8,128)(2,1)S(1)} %copy-done.24), channel_id=1, source_target_pairs={{1,0},{2,1},{3,2},{4,3},{5,4},{6,5},{7,6},{8,7},{9,8},{10,9},{11,1... | collective-permute-start | bytes 442376 | tf_op jit(solution)/shard_map/ppermute | solution.py:279
  136.9 13.1 %copy-start.18 = (bf16[3,8,8,384]{3,2,1,0:T(8,128)(2,1)}, bf16[3,8,8,384]{3,2,1,0:T(8,128)(2,1)S(1)}, u32[]{:S(2)}) copy-start(bf16[3,8,8,384]{3,2,1,0:T(8,128)(2,1)S(1)} %collective-permute-done.18.refs_2_) | copy-start | bytes 442372
  136.9 13.1 %copy-start.19 = (bf16[3,8,8,384]{3,2,1,0:T(8,128)(2,1)}, bf16[3,8,8,384]{3,2,1,0:T(8,128)(2,1)S(1)}, u32[]{:S(2)}) copy-start(bf16[3,8,8,384]{3,2,1,0:T(8,128)(2,1)S(1)} %collective-permute-done.19.refs_3_) | copy-start | bytes 442372
  147.8 2.2 %copy-start.20 = (bf16[3,8,8,384]{3,2,1,0:T(8,128)(2,1)}, bf16[3,8,8,384]{3,2,1,0:T(8,128)(2,1)S(1)}, u32[]{:S(2)}) copy-start(bf16[3,8,8,384]{3,2,1,0:T(8,128)(2,1)S(1)} %collective-permute-done.20.refs_4_) | copy-start | bytes 442372
  150.0 0.7 copy-start.21
  155.9 1.2 copy-start

commit v2 on v1

v2 whole, which is shorter than its diff:
```python
import jax
import jax.numpy as jnp
from jax import lax
from jax.experimental import pallas as pl
from jax.experimental.pallas import tpu as pltpu
from jax.sharding import PartitionSpec as P

BF = jnp.bfloat16
F32 = jnp.float32
WAVES = 384
LANES = 128
ROWS = 512
LIMIT = 24


def onehot(keys, count):
    rows = lax.broadcasted_iota(jnp.int32, (count, keys.shape[1]), 0)
    return (rows == keys).astype(F32).astype(BF)


def pack_kernel(flux_ref, comp_ref, route_ref, out_ref, trace_ref):
    by_panel = onehot(route_ref[...], 128)
    out_ref[:, 0:WAVES] = jnp.dot(by_panel, flux_ref[...].astype(BF), preferred_element_type=F32).astype(BF)

    def step(x, carry):
        for y in range(8):
            trace_ref[pl.ds(x * 8 + y, 1), :] = comp_ref[x, y, 0:1]
            trace_ref[pl.ds(64 + x * 8 + y, 1), :] = comp_ref[x, y, 7:8]
        return carry

    lax.fori_loop(0, 8, step, 0)
    out_ref[:, WAVES : 2 * WAVES] = jnp.dot(
        by_panel, trace_ref[...].astype(BF), preferred_element_type=F32
    ).astype(BF)
    out_ref[:, 2 * WAVES :] = jnp.broadcast_to(route_ref[...].astype(F32), (128, 128)).astype(BF)


def pack(flux, field, route_row):
    return pl.pallas_call(
        pack_kernel,
        grid=(1,),
        in_specs=[
            pl.BlockSpec((128, WAVES), lambda i: (0, 0)),
            pl.BlockSpec((None, 8, 8, 8, WAVES), lambda i: (2, 0, 0, 0, 0)),
            pl.BlockSpec((1, 128), lambda i: (0, 0)),
        ],
        out_specs=pl.BlockSpec((128, 2 * WAVES + 128), lambda i: (0, 0)),
        out_shape=jax.ShapeDtypeStruct((128, 2 * WAVES + 128), BF),
        scratch_shapes=[pltpu.VMEM((128, WAVES), F32)],
        compiler_params=pltpu.CompilerParams(vmem_limit_bytes=8 << 20),
        name="pack",
    )(in_hbm(flux), in_hbm(field), route_row)


def stencil_kernel(first, side_ref, mix_ref, *refs):
    if first:
        u_ref, sib, far, even, odd, st_ref, flux_ref, route_ref, out_ref, w_ref, wp_ref, f_sib, f_far, f_even, f_odd = refs
    else:
        u_ref, sib, far, even, odd, st_ref, out_ref = refs
    row_even = side_ref[0] == 0
    col_even = side_ref[1] == 0

    def low_x(c, y):
        return jnp.where(row_even, far[c, y], sib[c, y]).astype(F32)

    def high_x(c, y):
        return jnp.where(row_even, sib[c, y], far[c, y]).astype(F32)

    def low_y(c, x):
        return jnp.where(col_even, odd[c, x], even[c, x]).astype(F32)

    def high_y(c, x):
        return jnp.where(col_even, even[c, x], odd[c, x]).astype(F32)

    depth = lax.broadcasted_iota(jnp.int32, (8, LANES), 0)
    bottom = depth == 0
    top = depth == 7
    mix = [[mix_ref[i, j] for j in range(3)] for i in range(3)]

    def plane(x, below, above):
        for y in range(8):
            cell = [u_ref[c, x, y] for c in range(3)]
            stiff = jnp.broadcast_to(st_ref[x, y], (8, LANES))
            for c in range(3):
                u = cell[c]
                total = below(c, y) + above(c, y)
                total = total + (u_ref[c, x, y - 1] if y > 0 else low_y(c, x))
                total = total + (u_ref[c, x, y + 1] if y < 7 else high_y(c, x))
                total = total + jnp.where(bottom, 0.0, pltpu.roll(u, 1, 0))
                total = total + jnp.where(top, 0.0, pltpu.roll(u, 7, 0))
                mixed = mix[c][0] * cell[0] + mix[c][1] * cell[1] + mix[c][2] * cell[2]
                value = stiff * (u - total * (1.0 / 6.0)) + mixed
                if first and c == 2:
                    low = flux_ref[pl.ds(x * 8 + y, 1), :]
                    high = flux_ref[pl.ds(64 + x * 8 + y, 1), :]
                    value = value - jnp.where(bottom, low, jnp.where(top, high, 0.0))
                    w_ref[pl.ds(x * 8 + y, 1), :] = value[0:1]
                    w_ref[pl.ds(64 + x * 8 + y, 1), :] = value[7:8]
                out_ref[c, x, y] = value

    plane(0, low_x, lambda c, y: u_ref[c, 1, y])

    def step(x, carry):
        plane(x, lambda c, y: u_ref[c, x - 1, y], lambda c, y: u_ref[c, x + 1, y])
        return carry

    lax.fori_loop(1, 7, step, 0)
    plane(7, lambda c, y: u_ref[c, 6, y], high_x)
    if first:
        f_sib[...] = jnp.where(row_even, out_ref[:, 7], out_ref[:, 0]).astype(BF)
        f_far[...] = jnp.where(row_even, out_ref[:, 0], out_ref[:, 7]).astype(BF)
        f_even[...] = jnp.where(col_even, out_ref[:, :, 7], out_ref[:, :, 0]).astype(BF)
        f_odd[...] = jnp.where(col_even, out_ref[:, :, 0], out_ref[:, :, 7]).astype(BF)
        wp_ref[...] = jnp.dot(onehot(route_ref[...], 128), w_ref[...].astype(BF), preferred_element_type=F32).astype(BF)


def stencil(side, field, halos, stiffness, mixing, flux=None, route_row=None):
    first = flux is not None
    whole = pl.BlockSpec((3, 8, 8, 8, LANES), lambda i: (0, 0, 0, 0, i))
    face = pl.BlockSpec((3, 8, 8, LANES), lambda i: (0, 0, 0, i))
    panel = pl.BlockSpec((128, LANES), lambda i: (0, i))
    in_specs = [pl.BlockSpec(memory_space=pltpu.SMEM)] * 2 + [whole, face, face, face, face,
                pl.BlockSpec((8, 8, 8, 1), lambda i: (0, 0, 0, 0))]
    args = [side, mixing, in_hbm(field), *halos, stiffness]
    out_specs = [whole]
    out_shape = [pltpu.HBM(field.shape, F32)]
    if first:
        in_specs += [panel, pl.BlockSpec((1, 128), lambda i: (0, 0))]
        args += [flux, route_row]
        out_specs += [panel, panel, face, face, face, face]
        out_shape += [jax.ShapeDtypeStruct((128, WAVES), F32), jax.ShapeDtypeStruct((128, WAVES), BF)]
        out_shape += [jax.ShapeDtypeStruct((3, 8, 8, WAVES), BF)] * 4
    return pl.pallas_call(
        lambda *refs: stencil_kernel(first, *refs),
        grid=(WAVES // LANES,),
        in_specs=in_specs,
        out_specs=out_specs,
        out_shape=out_shape,
        compiler_params=pltpu.CompilerParams(vmem_limit_bytes=8 << 20),
        name="stencil_first" if first else "stencil_second",
    )(*args)


def boundary_kernel(first, order_ref, rows_ref, cols_ref, count_ref, *refs):
    chunks = refs[:8]
    single_ref, double_ref, near_ref = refs[8:11]
    extra_ref, *keys, out_ref, single_buf, double_buf, phi_ref, w_ref, acc_ref, sems = refs[11:]
    copies = []
    for i in range(2048 // ROWS):
        part = pl.ds(i * ROWS, ROWS)
        copies.append((
            pltpu.make_async_copy(single_ref.at[part], single_buf.at[part], sems.at[0, i]),
            pltpu.make_async_copy(double_ref.at[part], double_buf.at[part], sems.at[1, i]),
        ))
    for pair in copies:
        pair[0].start()
        pair[1].start()
    for k in range(8):
        at = pl.multiple_of(order_ref[k] * 128, 128)
        phi_ref[pl.ds(at, 128), :] = chunks[k][0]
        w_ref[pl.ds(at, 128), :] = chunks[k][1]
    m = lax.broadcasted_iota(jnp.int32, (256, 256), 0)
    place = (m // 16) * 8 + m % 8 + 128 * ((m // 8) % 2)

    for i in range(2048 // ROWS):
        part = pl.ds(i * ROWS, ROWS)
        copies[i][0].wait()
        far = jnp.dot(single_buf[part, :], phi_ref[...], preferred_element_type=F32)
        copies[i][1].wait()
        acc_ref[...] = far + jnp.dot(double_buf[part, :], w_ref[...], preferred_element_type=F32)

        def add_near(k, carry, i=i):
            @pl.when((k < count_ref[0]) & (rows_ref[k] // (ROWS // 128) == i))
            def _():
                row = pl.multiple_of((rows_ref[k] % (ROWS // 128)) * 128, 128)
                col = pl.multiple_of(cols_ref[k] * 128, 128)
                acc_ref[pl.ds(row, 128), :] += jnp.dot(
                    near_ref[k], phi_ref[pl.ds(col, 128), :], preferred_element_type=F32
                )

            return carry

        lax.fori_loop(0, 8, add_near, 0)
        total = acc_ref[...].astype(BF)
        if first:
            for p in range(ROWS // 256):
                pair = i * (ROWS // 256) + p
                select = (place == keys[0][pair]).astype(F32).astype(BF)
                packed = jnp.dot(select, total[p * 256 : p * 256 + 256], preferred_element_type=F32).astype(BF)
                out_ref[:, pair * 16 : pair * 16 + 16, :] = packed.reshape(16, 16, WAVES)
        else:
            owners = ROWS // 128
            out_ref[i * owners : (i + 1) * owners, 0:128, :] = total.reshape(owners, 128, WAVES)
    out_ref[:, 128:136, :] = extra_ref[...]


def boundary(order, near, chunks, single_layer, double_layer, extra, *keys):
    near_blocks, near_rows, near_cols, near_count = near
    first = len(keys) > 0
    vmem = pl.BlockSpec(memory_space=pltpu.VMEM)
    hbm = pl.BlockSpec(memory_space=pltpu.HBM)
    matrix = pltpu.VMEM((2048, 1024), BF)
    return pl.pallas_call(
        lambda *refs: boundary_kernel(first, *refs),
        in_specs=[pl.BlockSpec(memory_space=pltpu.SMEM)] * 4 + [vmem] * 8 + [hbm, hbm] + [vmem] * (2 + len(keys)),
        out_specs=vmem,
        out_shape=jax.ShapeDtypeStruct((16, 136, WAVES), BF),
        scratch_shapes=[
            matrix,
            matrix,
            pltpu.VMEM((1024, WAVES), BF),
            pltpu.VMEM((1024, WAVES), BF),
            pltpu.VMEM((ROWS, WAVES), F32),
            pltpu.SemaphoreType.DMA((2, 2048 // ROWS)),
        ],
        compiler_params=pltpu.CompilerParams(vmem_limit_bytes=LIMIT << 20),
        name="boundary_first" if first else "boundary_second",
    )(order, near_rows, near_cols, near_count, *chunks, in_hbm(single_layer), in_hbm(double_layer), near_blocks, extra, *keys)


def faces_kernel(side_ref, low_x, high_x, low_y, high_y, sib, far, even, odd):
    row_even = side_ref[0] == 0
    col_even = side_ref[1] == 0
    sib[...] = jnp.where(row_even, high_x[...], low_x[...]).astype(BF)
    far[...] = jnp.where(row_even, low_x[...], high_x[...]).astype(BF)
    even[...] = jnp.where(col_even, high_y[...], low_y[...]).astype(BF)
    odd[...] = jnp.where(col_even, low_y[...], high_y[...]).astype(BF)


def faces_of(side, field):
    across = lambda at: pl.BlockSpec((3, None, 8, 8, WAVES), lambda i: (0, at, 0, 0, 0))
    along = lambda at: pl.BlockSpec((3, 8, None, 8, WAVES), lambda i: (0, 0, at, 0, 0))
    out = pl.BlockSpec((3, 8, 8, WAVES), lambda i: (0, 0, 0, 0))
    return pl.pallas_call(
        faces_kernel,
        grid=(1,),
        in_specs=[pl.BlockSpec(memory_space=pltpu.SMEM), across(0), across(7), along(0), along(7)],
        out_specs=[out] * 4,
        out_shape=[jax.ShapeDtypeStruct((3, 8, 8, WAVES), BF)] * 4,
        compiler_params=pltpu.CompilerParams(vmem_limit_bytes=8 << 20),
        name="faces",
    )(side, *[in_hbm(field)] * 4)


def middle_kernel(got_ref, chunk_ref, out_ref):
    total = got_ref[0, 0:128].astype(F32)
    for k in range(1, 16):
        total = total + got_ref[k, 0:128].astype(F32)
    out_ref[0] = (total - 0.5 * chunk_ref[...].astype(F32)).astype(BF)
    out_ref[1] = got_ref[:, 128:136, :].reshape(128, LANES)


def middle(got, chunk):
    return pl.pallas_call(
        middle_kernel,
        grid=(WAVES // LANES,),
        in_specs=[
            pl.BlockSpec((16, 136, LANES), lambda i: (0, 0, i)),
            pl.BlockSpec((None, 128, LANES), lambda i: (1, 0, i)),
        ],
        out_specs=pl.BlockSpec((2, 128, LANES), lambda i: (0, 0, i)),
        out_shape=jax.ShapeDtypeStruct((2, 128, WAVES), BF),
        compiler_params=pltpu.CompilerParams(vmem_limit_bytes=8 << 20),
        name="middle",
    )(got, chunk)


def last_kernel(got_ref, w_ref, route_ref, comp_ref, flux_ref, out_ref, mid_ref):
    total = got_ref[0, 0:128].astype(F32)
    for k in range(1, 16):
        total = total + got_ref[k, 0:128].astype(F32)
    flux_ref[...] = total - 0.5 * w_ref[...]
    picker = (lax.broadcasted_iota(jnp.int32, (128, 128), 1) == route_ref[...]).astype(F32).astype(BF)
    mid_ref[...] = jnp.dot(picker, got_ref[:, 128:136, :].reshape(128, LANES), preferred_element_type=F32)
    depth = lax.broadcasted_iota(jnp.int32, (8, LANES), 0)

    def step(x, carry):
        for y in range(8):
            low = mid_ref[pl.ds(x * 8 + y, 1), :]
            high = mid_ref[pl.ds(64 + x * 8 + y, 1), :]
            out_ref[x, y] = comp_ref[x, y] - jnp.where(depth == 0, low, jnp.where(depth == 7, high, 0.0))
        return carry

    lax.fori_loop(0, 8, step, 0)


def last(got, trace, route_column, field):
    comp = pl.BlockSpec((None, 8, 8, 8, LANES), lambda i: (2, 0, 0, 0, i))
    panel = pl.BlockSpec((128, LANES), lambda i: (0, i))
    return pl.pallas_call(
        last_kernel,
        grid=(WAVES // LANES,),
        in_specs=[
            pl.BlockSpec((16, 136, LANES), lambda i: (0, 0, i)),
            panel,
            pl.BlockSpec((128, 1), lambda i: (0, 0)),
            comp,
        ],
        out_specs=[panel, comp],
        out_shape=[jax.ShapeDtypeStruct((128, WAVES), F32), jax.ShapeDtypeStruct(field.shape, F32)],
        scratch_shapes=[pltpu.VMEM((128, LANES), F32)],
        input_output_aliases={3: 1},
        compiler_params=pltpu.CompilerParams(vmem_limit_bytes=8 << 20),
        name="last",
    )(got, trace, route_column, in_hbm(field))


def shifted(count, by):
    return [(i, (i + by) % count) for i in range(count)]


def in_hbm(array):
    return pltpu.with_memory_space_constraint(array, pltpu.HBM)


def swapped(count, bits):
    return [(i, i ^ bits) for i in range(count)]


def across_rows(chunk):
    mine = [chunk] + [lax.ppermute(chunk, "row", swapped(8, k)) for k in (4, 2, 6)]
    beside = [lax.ppermute(one, "row", swapped(8, 1)) for one in mine]
    order = lax.axis_index("row") ^ jnp.array([0, 4, 2, 6, 1, 5, 3, 7], jnp.int32)
    return mine + beside, order


def swap_faces(sib, far, even, odd):
    across = lambda count: [pair for i in range(1, count - 1, 2) for pair in ((i, i + 1), (i + 1, i))]
    return (
        lax.ppermute(sib, "row", swapped(8, 1)),
        lax.ppermute(far, "row", across(8)),
        lax.ppermute(even, "col", swapped(16, 1)),
        lax.ppermute(odd, "col", across(16)),
    )


def after(value, *others):
    return lax.optimization_barrier((value, *others))[0]


def local(
    displacement,
    flux,
    stiffness,
    mixing,
    single_layer,
    double_layer,
    near_blocks,
    near_rows,
    near_cols,
    near_counts,
    routes,
):
    near = (near_blocks.reshape(8, 128, 128), near_rows.reshape(8), near_cols.reshape(8), near_counts.reshape(1))
    route_row = routes.reshape(1, 128)
    side = jnp.stack([lax.axis_index("row") % 2, lax.axis_index("col") % 2]).astype(jnp.int32)
    stiff = stiffness[..., None]

    packed = pack(flux, displacement, route_row)
    got = lax.all_to_all(packed.reshape(16, 8, 2 * WAVES + 128), "col", 0, 0, tiled=True)
    halos = swap_faces(*faces_of(side, displacement))
    chunk = jnp.stack(
        [got[:, :, :WAVES].reshape(128, WAVES), got[:, :, WAVES : 2 * WAVES].reshape(128, WAVES)], 0
    )
    keys = got[:, 0, 2 * WAVES :].astype(jnp.int32).reshape(8, 2, 128)
    keys = (keys + jnp.array([0, 128], jnp.int32)[None, :, None]).reshape(8, 1, 256)

    field, trace, outgoing, *faces = stencil(side, displacement, halos, stiff, mixing, flux, route_row)
    chunks, order = across_rows(chunk)
    sums = boundary(order, near, chunks, single_layer, double_layer, outgoing.reshape(16, 8, WAVES), keys)
    got = lax.all_to_all(sums, "col", 0, 0, tiled=True)
    halos = swap_faces(*after(faces, sums))
    chunk = middle(after(got, halos), chunk)

    chunks, order = across_rows(chunk)
    sums = boundary(order, near, chunks, single_layer, double_layer, chunk[0].reshape(16, 8, WAVES))
    got = lax.all_to_all(sums, "col", 0, 0, tiled=True)
    (field,) = stencil(side, field, after(halos, sums), stiff, mixing)
    new_flux, field = last(after(got, field), trace, routes.reshape(128, 1), field)
    return (field, new_flux)


def solution(mesh):
    return jax.shard_map(
        local,
        mesh=mesh,
        in_specs=(
            P(None, "row", "col", None, None),
            P(("row", "col"), None),
            P("row", "col", None),
            P(),
            P("row", "col"),
            P("row", "col"),
            P("row", "col", None, None),
            P("row", "col"),
            P("row", "col"),
            P("row", "col"),
            P(("row", "col")),
        ),
        out_specs=(P(None, "row", "col", None, None), P(("row", "col"), None)),
        check_vma=False,
    )
```

time: 164 us -> 145 us (0.88)
  waiting for transfers between devices: 21.9 us -> 60.8 us
  blocking collectives: 34.4 us -> 0 us
  local copies, waits for them, and re-layouts: 14.2 us -> 0.72 us
  Pallas kernels: 44.5 us -> 39.3 us
  starting transfers between devices: 43.6 us -> 41 us
    all_to_all x1 -> x0, blocking collectives: 34.4 us -> none  [local(): got = lax.all_to_all(sums, 'col', 0, 0, tiled=True)]
    all_to_all x1 -> x2, waiting for transfers between devices: 0.01 us -> 22.8 us  [local(): got = lax.all_to_all(sums, 'col', 0, 0, tiled=True)]
    ppermute x22, starting transfers between devices: 31.2 us -> 22.5 us  [the longest x6 8.35 us: across_rows(): lax.ppermute(chunk, 'row', swapped(8, k))]
    ppermute x22, waiting for transfers between devices: 21.8 us -> 30.2 us  [the longest x2 16.9 us: swap_faces(): lax.ppermute(even, 'col', swapped(16, 1))]
    all_to_all x1 -> x2, starting transfers between devices: 4.42 us -> 12.3 us  [local(): got = lax.all_to_all(sums, 'col', 0, 0, tiled=True)]
    all_to_all x1, waiting for transfers between devices: 0.01 us -> 7.82 us  [local(): lax.all_to_all(packed.reshape(16, 8, 2 * WAVES + 128), 'col', 0, 0, tiled...]
    unnamed x56 -> x16, local copies, waits for them, and re-layouts: 4.74 us -> 0.05 us
    pallas_call x1, Pallas kernels: 2.96 us -> 0.63 us  [middle(): pl.pallas_call(middle_kernel, grid=(WAVES // LANES,), in_specs=[pl.BlockS...]
  transfers between devices with their start and end apart: 24 -> 25, of which waited for: 7 -> 14; matrix products, arithmetic and copies ran while one was open for 5% -> 0% of each run, Pallas kernels for 7% -> 9%
where the time goes in v2:
time: 145 us; the launch traced here: 144 us
  waiting for transfers between devices  60.8 us (42%)
  starting transfers between devices  41 us (28%)
  Pallas kernels  39.3 us (27%)
  between operations  1.6 us (1%)
    all_to_all x2, waiting for transfers between devices, local(): got = lax.all_to_all(sums, 'col', 0, 0, tiled=True)  22.8 us
    pallas_call x2, Pallas kernels, boundary(): pl.pallas_call(lambda *refs: boundary_kernel(first, *refs), in_specs=[pl....  21.6 us
    ppermute x2, waiting for transfers between devices, swap_faces(): lax.ppermute(even, 'col', swapped(16, 1))  16.9 us
    all_to_all x2, starting transfers between devices, local(): got = lax.all_to_all(sums, 'col', 0, 0, tiled=True)  12.3 us
    pallas_call x2, Pallas kernels, stencil(): pl.pallas_call(lambda *refs: stencil_kernel(first, *refs), grid=(WAVES //...  9.72 us
    ppermute x6, waiting for transfers between devices, across_rows(): lax.ppermute(chunk, 'row', swapped(8, k))  8.58 us
    ppermute x6, starting transfers between devices, across_rows(): lax.ppermute(chunk, 'row', swapped(8, k))  8.35 us
    all_to_all x1, waiting for transfers between devices, local(): lax.all_to_all(packed.reshape(16, 8, 2 * WAVES + 128), 'col', 0, 0, tiled...  7.82 us
  transfers between devices with their start and end apart: 25, of which 14 were waited for; matrix products, arithmetic and copies ran while one was open for 0% of the time, Pallas kernels for 9%

profile of v2, /device:TPU:2, one launch (start us, length us, event | category | flops | bytes accessed | tf_op | source)
XLA Modules:
  0.0 143.6 jit_solution(625307789716691387)
XLA Ops:
  0.6 0.1 pad_add_fusion.side_ref.refs_0_
  0.7 1.4 faces.1
  2.1 0.0 copy-start.6
  2.1 0.0 copy-start.7
  2.1 0.0 copy-start.1
  2.1 0.0 copy-start.2
  2.1 0.8 collective-permute-start.10
  3.0 0.1 collective-permute-start.7
  3.0 2.4 %collective-permute-start.8 = (bf16[3,8,8,384]{3,2,1,0:T(8,128)(2,1)S(1)}, bf16[3,8,8,384]{3,2,1,0:T(8,128)(2,1)S(1)}, u32[]{:S(2)}, u32[]{:S(2)}) collective-permute-start(bf16[3,8,8,384]{3,2,1,0:T(8,128)(2,1)S(1)} %get-tuple-element.26), channel_id=1, source_target_pairs={{16,32},{32,16},{48,64},{64,48},{80,96},{96,80},{17,33},{33,17},{4... | collective-permute-start | bytes 442376 | tf_op jit(solution)/shard_map/ppermute | solution.py:331
  5.5 5.3 %collective-permute-start.9 = (bf16[3,8,8,384]{3,2,1,0:T(8,128)(2,1)S(1)}, bf16[3,8,8,384]{3,2,1,0:T(8,128)(2,1)S(1)}, u32[]{:S(2)}, u32[]{:S(2)}) collective-permute-start(bf16[3,8,8,384]{3,2,1,0:T(8,128)(2,1)S(1)} %get-tuple-element.27), channel_id=1, source_target_pairs={{0,1},{1,0},{2,3},{3,2},{4,5},{5,4},{6,7},{7,6},{8,9},{9,8},{10,11... | collective-permute-start | bytes 442376 | tf_op jit(solution)/shard_map/ppermute | solution.py:332
  10.7 2.5 %pack.1 = bf16[128,896]{1,0:T(8,128)(2,1)} custom-call(f32[128,384]{1,0:T(8,128)} %refs_8_.1, f32[3,8,8,8,384]{4,3,2,1,0:T(8,128)} %refs_2_.1, s32[1,128]{1,0:T(1,128)S(1)} %bitcast.26), custom_call_target="tpu_custom_call" | custom-call | tf_op jit(solution)/shard_map/pack/pallas_call | solution.py:39
  13.3 6.2 %all-to-all-start = ((bf16[16,8,896]{2,1,0:T(8,128)(2,1)}), bf16[16,8,896]{2,1,0:T(8,128)(2,1)S(1)}, u32[]{:S(2)}, u32[]{:S(2)}) async-start(bf16[16,8,896]{2,1,0:T(8,128)(2,1)} %bitcast.4), calls=%async_computation | async-start | bytes 458752 | tf_op jit(solution)/shard_map/all_to_all | solution.py:360
  19.5 0.0 copy-start
  19.5 0.0 copy-start.4
  19.5 0.0 copy-start.5
  19.6 0.4 copy.18.refs_7_
  20.7 0.1 broadcast_bitcast_fusion
  20.7 7.8 %all-to-all-done = bf16[16,8,896]{2,1,0:T(8,128)(2,1)S(1)} async-done(((bf16[16,8,896]{2,1,0:T(8,128)(2,1)}), bf16[16,8,896]{2,1,0:T(8,128)(2,1)S(1)}, u32[]{:S(2)}, u32[]{:S(2)}) %all-to-all-start) | async-done | bytes 229408 | tf_op jit(solution)/shard_map/all_to_all | solution.py:360
  28.6 1.7 %collective-permute-start = (bf16[2,128,384]{2,1,0:T(8,128)(2,1)S(1)}, bf16[2,128,384]{2,1,0:T(8,128)(2,1)S(1)}, u32[]{:S(2)}, u32[]{:S(2)}) collective-permute-start(bf16[2,128,384]{2,1,0:T(8,128)(2,1)S(1)} %pad_maximum_fusion.refs_4_.chunk_ref), channel_id=1, source_target_pairs={{0,64},{16,80},{32,96},{48,112},{64,0},{80,16},{96,32},{112,48},{1... | collective-permute-start | bytes 589832 | tf_op jit(solution)/shard_map/ppermute | solution.py:321
  30.3 0.0 collective-permute-done.10.refs_6_
  30.3 1.6 %collective-permute-start.1 = (bf16[2,128,384]{2,1,0:T(8,128)(2,1)S(1)}, bf16[2,128,384]{2,1,0:T(8,128)(2,1)S(1)}, u32[]{:S(2)}, u32[]{:S(2)}) collective-permute-start(bf16[2,128,384]{2,1,0:T(8,128)(2,1)S(1)} %pad_maximum_fusion.refs_4_.chunk_ref), channel_id=1, source_target_pairs={{0,32},{16,48},{32,0},{48,16},{64,96},{80,112},{96,64},{112,80},{1... | collective-permute-start | bytes 589832 | tf_op jit(solution)/shard_map/ppermute | solution.py:321
  32.0 0.0 collective-permute-done.7.refs_3_
  32.0 0.8 collective-permute-start.2
  32.8 0.0 collective-permute-done.8.refs_4_
  32.8 0.0 collective-permute-done.9.refs_5_
  32.8 5.0 %stencil_first.1 = (f32[3,8,8,8,384]{4,3,2,1,0:T(8,128)}, f32[128,384]{1,0:T(8,128)S(1)}, bf16[128,384]{1,0:T(8,128)(2,1)S(1)}, bf16[3,8,8,384]{3,2,1,0:T(8,128)...) custom-call(s32[2]{0:T(128)S(1)} %pad_add_fusion.side_ref.refs_0_, ...), custom_call_target="tpu_custom_call" | custom-call | tf_op jit(solution)/shard_map/stencil_first/pallas_call | solution.py:133
  37.8 0.0 collective-permute-start.3
  37.8 0.1 collective-permute-done.refs_5_
  38.0 0.5 collective-permute-start.4
  38.4 1.4 collective-permute-done.1.refs_6_
  39.8 0.5 collective-permute-done.2.refs_7_
  40.3 0.0 collective-permute-start.6
  40.3 0.0 collective-permute-done.4.refs_9_
  40.4 0.9 collective-permute-done.5.refs_10_
  41.2 0.5 collective-permute-done.6.refs_11_
  41.8 11.3 %boundary_first.1 = bf16[16,136,384]{2,1,0:T(8,128)(2,1)} custom-call(s32[8]{0:T(128)S(1)} %broadcast_xor_fusion.refs_0_, s32[8]{0:T(128)S(1)} %bitcast.29, s32[8]{0:T(128)S(1)} %bitcast.31, s32[1]{0:T(128)} %bitcast.21.refs_3_, bf16[2,128,384]{2,1,0:T(8,128)(2,1)S(1)} %pad_maximum_fusion.refs_4_.chunk_ref, ...), custom_call_target="tpu_custom_call" | custom-call | tf_op jit(solution)/shard_map/boundary_first/pallas_call | solution.py:203
  53.1 4.5 %all-to-all-start.1 = ((bf16[16,136,384]{2,1,0:T(8,128)(2,1)}), bf16[16,136,384]{2,1,0:T(8,128)(2,1)S(1)}, u32[]{:S(2)}, u32[]{:S(2)}) async-start(bf16[16,136,384]{2,1,0:T(8,128)(2,1)} %boundary_first.1), calls=%async_computation.1 | async-start | bytes 3342336 | tf_op jit(solution)/shard_map/all_to_all | solution.py:371
  57.6 0.1 collective-permute-start.11
  57.7 1.9 %collective-permute-start.12 = (bf16[3,8,8,384]{3,2,1,0:T(8,128)(2,1)}, bf16[3,8,8,384]{3,2,1,0:T(8,128)(2,1)S(1)}, u32[]{:S(2)}, u32[]{:S(2)}) collective-permute-start(bf16[3,8,8,384]{3,2,1,0:T(8,128)(2,1)} %get-tuple-element.35), channel_id=1, source_target_pairs={{16,32},{32,16},{48,64},{64,48},{80,96},{96,80},{17,33},{33,17},{4... | collective-permute-start | bytes 442376 | tf_op jit(solution)/shard_map/ppermute | solution.py:331
  59.7 1.9 %collective-permute-start.13 = (bf16[3,8,8,384]{3,2,1,0:T(8,128)(2,1)S(1)}, bf16[3,8,8,384]{3,2,1,0:T(8,128)(2,1)S(1)}, u32[]{:S(2)}, u32[]{:S(2)}) collective-permute-start(bf16[3,8,8,384]{3,2,1,0:T(8,128)(2,1)S(1)} %get-tuple-element.36), channel_id=1, source_target_pairs={{0,1},{1,0},{2,3},{3,2},{4,5},{5,4},{6,7},{7,6},{8,9},{9,8},{10,11... | collective-permute-start | bytes 442376 | tf_op jit(solution)/shard_map/ppermute | solution.py:332
  61.6 0.7 collective-permute-start.14
  62.3 2.1 %collective-permute-done.12.refs_4_ = bf16[3,8,8,384]{3,2,1,0:T(8,128)(2,1)S(1)} collective-permute-done((bf16[3,8,8,384]{3,2,1,0:T(8,128)(2,1)}, bf16[3,8,8,384]{3,2,1,0:T(8,128)(2,1)S(1)}, u32[]{:S(2)}, u32[]{:S(2)}) %collective-permute-start.12) | collective-permute-done | bytes 147488 | tf_op jit(solution)/shard_map/ppermute | solution.py:331
  64.4 16.8 %collective-permute-done.13.refs_5_ = bf16[3,8,8,384]{3,2,1,0:T(8,128)(2,1)S(1)} collective-permute-done((bf16[3,8,8,384]{3,2,1,0:T(8,128)(2,1)S(1)}, bf16[3,8,8,384]{3,2,1,0:T(8,128)(2,1)S(1)}, u32[]{:S(2)}, u32[]{:S(2)}) %collective-permute-start.13) | collective-permute-done | bytes 147488 | tf_op jit(solution)/shard_map/ppermute | solution.py:332
  81.2 0.0 collective-permute-done.14.refs_6_
  81.3 1.9 %all-to-all-done.1.got_ref = bf16[16,136,384]{2,1,0:T(8,128)(2,1)S(1)} async-done(((bf16[16,136,384]{2,1,0:T(8,128)(2,1)}), bf16[16,136,384]{2,1,0:T(8,128)(2,1)S(1)}, u32[]{:S(2)}, u32[]{:S(2)}) %all-to-all-start.1) | async-done | bytes 1671200 | tf_op jit(solution)/shard_map/all_to_all | solution.py:371
  83.2 0.6 middle.1.refs_4_
  83.8 0.9 collective-permute-start.15
  84.8 1.8 %collective-permute-start.16 = (bf16[2,128,384]{2,1,0:T(8,128)(2,1)S(1)}, bf16[2,128,384]{2,1,0:T(8,128)(2,1)S(1)}, u32[]{:S(2)}, u32[]{:S(2)}) collective-permute-start(bf16[2,128,384]{2,1,0:T(8,128)(2,1)S(1)} %middle.1.refs_4_), channel_id=1, source_target_pairs={{0,32},{16,48},{32,0},{48,16},{64,96},{80,112},{96,64},{112,80},{1... | collective-permute-start | bytes 589832 | tf_op jit(solution)/shard_map/ppermute | solution.py:321
  86.6 1.4 collective-permute-start.17
  88.0 0.0 collective-permute-start.18
  88.0 4.4 %collective-permute-done.15.refs_5_ = bf16[2,128,384]{2,1,0:T(8,128)(2,1)S(1)} collective-permute-done((bf16[2,128,384]{2,1,0:T(8,128)(2,1)S(1)}, bf16[2,128,384]{2,1,0:T(8,128)(2,1)S(1)}, u32[]{:S(2)}, u32[]{:S(2)}) %collective-permute-start.15) | collective-permute-done | bytes 196640 | tf_op jit(solution)/shard_map/ppermute | solution.py:321
  92.4 0.0 collective-permute-start.19
  92.4 2.2 %collective-permute-done.16.refs_6_ = bf16[2,128,384]{2,1,0:T(8,128)(2,1)S(1)} collective-permute-done((bf16[2,128,384]{2,1,0:T(8,128)(2,1)S(1)}, bf16[2,128,384]{2,1,0:T(8,128)(2,1)S(1)}, u32[]{:S(2)}, u32[]{:S(2)}) %collective-permute-start.16) | collective-permute-done | bytes 196640 | tf_op jit(solution)/shard_map/ppermute | solution.py:321
  94.6 0.0 collective-permute-start.20
  94.6 0.5 collective-permute-start.21
  95.1 0.0 collective-permute-done.19.refs_9_
  95.1 0.9 collective-permute-done.20.refs_10_
  96.0 0.3 collective-permute-done.21.refs_11_
  96.3 10.3 %boundary_second.1 = bf16[16,136,384]{2,1,0:T(8,128)(2,1)} custom-call(s32[8]{0:T(128)S(1)} %broadcast_xor_fusion.refs_0_, s32[8]{0:T(128)S(1)} %bitcast.30, s32[8]{0:T(128)S(1)} %bitcast.32, s32[1]{0:T(128)} %bitcast.22.refs_3_, bf16[2,128,384]{2,1,0:T(8,128)(2,1)S(1)} %middle.1.refs_4_, bf16[2,128,384]{2,1,0:T(8,128)(2,1)S(1)} %collective-permute-done.15.refs_5_, ...), custom_call_target="tpu_custom_call" | custom-call | tf_op jit(solution)/shard_map/boundary_second/pallas_call | solution.py:203
  106.6 7.8 %all-to-all-start.2 = ((bf16[16,136,384]{2,1,0:T(8,128)(2,1)}), bf16[16,136,384]{2,1,0:T(8,128)(2,1)S(1)}, u32[]{:S(2)}, u32[]{:S(2)}) async-start(bf16[16,136,384]{2,1,0:T(8,128)(2,1)} %boundary_second.1), calls=%async_computation.2 | async-start | bytes 3342336 | tf_op jit(solution)/shard_map/all_to_all | solution.py:377
  114.4 0.1 copy.20.route_ref
  114.5 4.7 %stencil_second.1.comp_ref = f32[3,8,8,8,384]{4,3,2,1,0:T(8,128)} custom-call(s32[2]{0:T(128)S(1)} %pad_add_fusion.side_ref.refs_0_, f32[3,3]{1,0:T(4,128)S(1)} %copy-done.2, f32[3,8,8,8,384]{4,3,2,1,0:T(8,128)} %get-tuple-element.39.refs_2_, bf16[3,8,8,384]{3,2,1,0:T(8,128)(2,1)S(1)} %collective-permute-done.11.refs_3_, ...), custom_call_target="tpu_custom_call" | custom-call | tf_op jit(solution)/shard_map/stencil_second/pallas_call | solution.py:133
  119.2 20.9 %all-to-all-done.2.got_ref = bf16[16,136,384]{2,1,0:T(8,128)(2,1)S(1)} async-done(((bf16[16,136,384]{2,1,0:T(8,128)(2,1)}), bf16[16,136,384]{2,1,0:T(8,128)(2,1)S(1)}, u32[]{:S(2)}, u32[]{:S(2)}) %all-to-all-start.2) | async-done | bytes 1671200 | tf_op jit(solution)/shard_map/all_to_all | solution.py:377
  140.1 3.5 %last.1 = (f32[128,384]{1,0:T(8,128)}, f32[3,8,8,8,384]{4,3,2,1,0:T(8,128)}) custom-call(bf16[16,136,384]{2,1,0:T(8,128)(2,1)S(1)} %all-to-all-done.2.got_ref, f32[128,384]{1,0:T(8,128)S(1)} %get-tuple-element.45.w_ref, s32[128,1]{1,0:T(8,128)S(1)} %copy.20.route_ref, f32[3,8,8,8,384]{4,3,2,1,0:T(8,128)} %stencil_second.1.comp_ref), custom_call_target="tpu_custom_call", output_to_operand_aliasing={{1}: (3, {})} | custom-call | tf_op jit(solution)/shard_map/last/pallas_call | solution.py:290
  (21 shorter events, 0.1 us)
Async XLA Ops:
  0.7 10.0 %copy-start.3 = (s32[128]{0:T(128)S(1)}, s32[128]{0:T(128)}, u32[]{:S(2)}) copy-start(s32[128]{0:T(128)} %param.24) | copy-start | bytes 1540
  2.1 17.5 %copy-start.6 = (f32[8,8,8]{2,1,0:T(8,128)S(1)}, f32[8,8,8]{2,1,0:T(8,128)}, u32[]{:S(2)}) copy-start(f32[8,8,8]{2,1,0:T(8,128)} %param.16) | copy-start | bytes 6148
  2.1 30.7 %copy-start.7 = (s32[8]{0:T(128)S(1)}, s32[8]{0:T(128)}, u32[]{:S(2)}) copy-start(s32[8]{0:T(128)} %constant.32.clone) | copy-start | bytes 100
  2.1 30.7 %copy-start.1 = (f32[128,384]{1,0:T(8,128)S(1)}, f32[128,384]{1,0:T(8,128)}, u32[]{:S(2)}) copy-start(f32[128,384]{1,0:T(8,128)} %refs_8_.1) | copy-start | bytes 589828
  2.1 30.7 %copy-start.2 = (f32[3,3]{1,0:T(4,128)S(1)}, f32[3,3]{1,0:T(4,128)}, u32[]{:S(2)}) copy-start(f32[3,3]{1,0:T(4,128)} %refs_1_.3) | copy-start | bytes 112
  2.1 28.2 %collective-permute-start.10 = (bf16[3,8,8,384]{3,2,1,0:T(8,128)(2,1)S(1)}, bf16[3,8,8,384]{3,2,1,0:T(8,128)(2,1)S(1)}, u32[]{:S(2)}, u32[]{:S(2)}) collective-permute-start(bf16[3,8,8,384]{3,2,1,0:T(8,128)(2,1)S(1)} %get-tuple-element.28), channel_id=1, source_target_pairs={{1,2},{2,1},{3,4},{4,3},{5,6},{6,5},{7,8},{8,7},{9,10},{10,9},{11,... | collective-permute-start | bytes 442376 | tf_op jit(solution)/shard_map/ppermute | solution.py:333
  3.0 29.0 %collective-permute-start.7 = (bf16[3,8,8,384]{3,2,1,0:T(8,128)(2,1)S(1)}, bf16[3,8,8,384]{3,2,1,0:T(8,128)(2,1)S(1)}, u32[]{:S(2)}, u32[]{:S(2)}) collective-permute-start(bf16[3,8,8,384]{3,2,1,0:T(8,128)(2,1)S(1)} %get-tuple-element.25), channel_id=1, source_target_pairs={{0,16},{16,0},{32,48},{48,32},{64,80},{80,64},{96,112},{112,96},{1... | collective-permute-start | bytes 442376 | tf_op jit(solution)/shard_map/ppermute | solution.py:330
  3.0 29.7 %collective-permute-start.8 = (bf16[3,8,8,384]{3,2,1,0:T(8,128)(2,1)S(1)}, bf16[3,8,8,384]{3,2,1,0:T(8,128)(2,1)S(1)}, u32[]{:S(2)}, u32[]{:S(2)}) collective-permute-start(bf16[3,8,8,384]{3,2,1,0:T(8,128)(2,1)S(1)} %get-tuple-element.26), channel_id=1, source_target_pairs={{16,32},{32,16},{48,64},{64,48},{80,96},{96,80},{17,33},{33,17},{4... | collective-permute-start | bytes 442376 | tf_op jit(solution)/shard_map/ppermute | solution.py:331
  5.5 27.3 %collective-permute-start.9 = (bf16[3,8,8,384]{3,2,1,0:T(8,128)(2,1)S(1)}, bf16[3,8,8,384]{3,2,1,0:T(8,128)(2,1)S(1)}, u32[]{:S(2)}, u32[]{:S(2)}) collective-permute-start(bf16[3,8,8,384]{3,2,1,0:T(8,128)(2,1)S(1)} %get-tuple-element.27), channel_id=1, source_target_pairs={{0,1},{1,0},{2,3},{3,2},{4,5},{5,4},{6,7},{7,6},{8,9},{9,8},{10,11... | collective-permute-start | bytes 442376 | tf_op jit(solution)/shard_map/ppermute | solution.py:332
  13.3 15.3 %all-to-all-start = ((bf16[16,8,896]{2,1,0:T(8,128)(2,1)}), bf16[16,8,896]{2,1,0:T(8,128)(2,1)S(1)}, u32[]{:S(2)}, u32[]{:S(2)}) async-start(bf16[16,8,896]{2,1,0:T(8,128)(2,1)} %bitcast.4), calls=%async_computation | async-start | bytes 458752 | tf_op jit(solution)/shard_map/all_to_all | solution.py:360
  19.5 22.3 %copy-start = (bf16[8,1,128,128]{3,2,1,0:T(8,128)(2,1)S(1)}, bf16[8,1,128,128]{3,2,1,0:T(8,128)(2,1)}, u32[]{:S(2)}) copy-start(bf16[8,1,128,128]{3,2,1,0:T(8,128)(2,1)} %param.20) | copy-start | bytes 786436
  19.5 22.2 %copy-start.4 = (s32[8,1]{0,1:T(1,128)S(1)}, s32[8,1]{0,1:T(1,128)}, u32[]{:S(2)}) copy-start(s32[8,1]{0,1:T(1,128)} %param.21) | copy-start | bytes 100
  19.5 22.2 %copy-start.5 = (s32[8,1]{0,1:T(1,128)S(1)}, s32[8,1]{0,1:T(1,128)}, u32[]{:S(2)}) copy-start(s32[8,1]{0,1:T(1,128)} %param.22) | copy-start | bytes 100
  28.6 9.4 %collective-permute-start = (bf16[2,128,384]{2,1,0:T(8,128)(2,1)S(1)}, bf16[2,128,384]{2,1,0:T(8,128)(2,1)S(1)}, u32[]{:S(2)}, u32[]{:S(2)}) collective-permute-start(bf16[2,128,384]{2,1,0:T(8,128)(2,1)S(1)} %pad_maximum_fusion.refs_4_.chunk_ref), channel_id=1, source_target_pairs={{0,64},{16,80},{32,96},{48,112},{64,0},{80,16},{96,32},{112,48},{1... | collective-permute-start | bytes 589832 | tf_op jit(solution)/shard_map/ppermute | solution.py:321
  30.3 9.4 %collective-permute-start.1 = (bf16[2,128,384]{2,1,0:T(8,128)(2,1)S(1)}, bf16[2,128,384]{2,1,0:T(8,128)(2,1)S(1)}, u32[]{:S(2)}, u32[]{:S(2)}) collective-permute-start(bf16[2,128,384]{2,1,0:T(8,128)(2,1)S(1)} %pad_maximum_fusion.refs_4_.chunk_ref), channel_id=1, source_target_pairs={{0,32},{16,48},{32,0},{48,16},{64,96},{80,112},{96,64},{112,80},{1... | collective-permute-start | bytes 589832 | tf_op jit(solution)/shard_map/ppermute | solution.py:321
  32.0 8.4 %collective-permute-start.2 = (bf16[2,128,384]{2,1,0:T(8,128)(2,1)S(1)}, bf16[2,128,384]{2,1,0:T(8,128)(2,1)S(1)}, u32[]{:S(2)}, u32[]{:S(2)}) collective-permute-start(bf16[2,128,384]{2,1,0:T(8,128)(2,1)S(1)} %pad_maximum_fusion.refs_4_.chunk_ref), channel_id=1, source_target_pairs={{0,96},{16,112},{32,64},{48,80},{64,32},{80,48},{96,0},{112,16},{1... | collective-permute-start | bytes 589832 | tf_op jit(solution)/shard_map/ppermute | solution.py:321
  37.8 2.5 %collective-permute-start.3 = (bf16[2,128,384]{2,1,0:T(8,128)(2,1)S(1)}, bf16[2,128,384]{2,1,0:T(8,128)(2,1)S(1)}, u32[]{:S(2)}, u32[]{:S(2)}) collective-permute-start(bf16[2,128,384]{2,1,0:T(8,128)(2,1)S(1)} %pad_maximum_fusion.refs_4_.chunk_ref), channel_id=1, source_target_pairs={{0,16},{16,0},{32,48},{48,32},{64,80},{80,64},{96,112},{112,96},{1... | collective-permute-start | bytes 589832 | tf_op jit(solution)/shard_map/ppermute | solution.py:322
  38.0 2.4 %collective-permute-start.4 = (bf16[2,128,384]{2,1,0:T(8,128)(2,1)S(1)}, bf16[2,128,384]{2,1,0:T(8,128)(2,1)S(1)}, u32[]{:S(2)}, u32[]{:S(2)}) collective-permute-start(bf16[2,128,384]{2,1,0:T(8,128)(2,1)S(1)} %collective-permute-done.refs_5_), channel_id=1, source_target_pairs={{0,16},{16,0},{32,48},{48,32},{64,80},{80,64},{96,112},{112,96},{1... | collective-permute-start | bytes 589832 | tf_op jit(solution)/shard_map/ppermute | solution.py:322
  39.8 1.4 %collective-permute-start.5 = (bf16[2,128,384]{2,1,0:T(8,128)(2,1)S(1)}, bf16[2,128,384]{2,1,0:T(8,128)(2,1)S(1)}, u32[]{:S(2)}, u32[]{:S(2)}) collective-permute-start(bf16[2,128,384]{2,1,0:T(8,128)(2,1)S(1)} %collective-permute-done.1.refs_6_), channel_id=1, source_target_pairs={{0,16},{16,0},{32,48},{48,32},{64,80},{80,64},{96,112},{112,96},{1... | collective-permute-start | bytes 589832 | tf_op jit(solution)/shard_map/ppermute | solution.py:322
  40.3 1.4 %collective-permute-start.6 = (bf16[2,128,384]{2,1,0:T(8,128)(2,1)S(1)}, bf16[2,128,384]{2,1,0:T(8,128)(2,1)S(1)}, u32[]{:S(2)}, u32[]{:S(2)}) collective-permute-start(bf16[2,128,384]{2,1,0:T(8,128)(2,1)S(1)} %collective-permute-done.2.refs_7_), channel_id=1, source_target_pairs={{0,16},{16,0},{32,48},{48,32},{64,80},{80,64},{96,112},{112,96},{1... | collective-permute-start | bytes 589832 | tf_op jit(solution)/shard_map/ppermute | solution.py:322
  53.1 30.1 %all-to-all-start.1 = ((bf16[16,136,384]{2,1,0:T(8,128)(2,1)}), bf16[16,136,384]{2,1,0:T(8,128)(2,1)S(1)}, u32[]{:S(2)}, u32[]{:S(2)}) async-start(bf16[16,136,384]{2,1,0:T(8,128)(2,1)} %boundary_first.1), calls=%async_computation.1 | async-start | bytes 3342336 | tf_op jit(solution)/shard_map/all_to_all | solution.py:371
  57.6 4.6 %collective-permute-start.11 = (bf16[3,8,8,384]{3,2,1,0:T(8,128)(2,1)}, bf16[3,8,8,384]{3,2,1,0:T(8,128)(2,1)S(1)}, u32[]{:S(2)}, u32[]{:S(2)}) collective-permute-start(bf16[3,8,8,384]{3,2,1,0:T(8,128)(2,1)} %get-tuple-element.34), channel_id=1, source_target_pairs={{0,16},{16,0},{32,48},{48,32},{64,80},{80,64},{96,112},{112,96},{1... | collective-permute-start | bytes 442376 | tf_op jit(solution)/shard_map/ppermute | solution.py:330
  57.7 6.7 %collective-permute-start.12 = (bf16[3,8,8,384]{3,2,1,0:T(8,128)(2,1)}, bf16[3,8,8,384]{3,2,1,0:T(8,128)(2,1)S(1)}, u32[]{:S(2)}, u32[]{:S(2)}) collective-permute-start(bf16[3,8,8,384]{3,2,1,0:T(8,128)(2,1)} %get-tuple-element.35), channel_id=1, source_target_pairs={{16,32},{32,16},{48,64},{64,48},{80,96},{96,80},{17,33},{33,17},{4... | collective-permute-start | bytes 442376 | tf_op jit(solution)/shard_map/ppermute | solution.py:331
  59.7 21.6 %collective-permute-start.13 = (bf16[3,8,8,384]{3,2,1,0:T(8,128)(2,1)S(1)}, bf16[3,8,8,384]{3,2,1,0:T(8,128)(2,1)S(1)}, u32[]{:S(2)}, u32[]{:S(2)}) collective-permute-start(bf16[3,8,8,384]{3,2,1,0:T(8,128)(2,1)S(1)} %get-tuple-element.36), channel_id=1, source_target_pairs={{0,1},{1,0},{2,3},{3,2},{4,5},{5,4},{6,7},{7,6},{8,9},{9,8},{10,11... | collective-permute-start | bytes 442376 | tf_op jit(solution)/shard_map/ppermute | solution.py:332
  61.6 19.7 %collective-permute-start.14 = (bf16[3,8,8,384]{3,2,1,0:T(8,128)(2,1)S(1)}, bf16[3,8,8,384]{3,2,1,0:T(8,128)(2,1)S(1)}, u32[]{:S(2)}, u32[]{:S(2)}) collective-permute-start(bf16[3,8,8,384]{3,2,1,0:T(8,128)(2,1)S(1)} %get-tuple-element.37), channel_id=1, source_target_pairs={{1,2},{2,1},{3,4},{4,3},{5,6},{6,5},{7,8},{8,7},{9,10},{10,9},{11,... | collective-permute-start | bytes 442376 | tf_op jit(solution)/shard_map/ppermute | solution.py:333
  83.8 8.6 %collective-permute-start.15 = (bf16[2,128,384]{2,1,0:T(8,128)(2,1)S(1)}, bf16[2,128,384]{2,1,0:T(8,128)(2,1)S(1)}, u32[]{:S(2)}, u32[]{:S(2)}) collective-permute-start(bf16[2,128,384]{2,1,0:T(8,128)(2,1)S(1)} %middle.1.refs_4_), channel_id=1, source_target_pairs={{0,64},{16,80},{32,96},{48,112},{64,0},{80,16},{96,32},{112,48},{1... | collective-permute-start | bytes 589832 | tf_op jit(solution)/shard_map/ppermute | solution.py:321
  84.8 9.8 %collective-permute-start.16 = (bf16[2,128,384]{2,1,0:T(8,128)(2,1)S(1)}, bf16[2,128,384]{2,1,0:T(8,128)(2,1)S(1)}, u32[]{:S(2)}, u32[]{:S(2)}) collective-permute-start(bf16[2,128,384]{2,1,0:T(8,128)(2,1)S(1)} %middle.1.refs_4_), channel_id=1, source_target_pairs={{0,32},{16,48},{32,0},{48,16},{64,96},{80,112},{96,64},{112,80},{1... | collective-permute-start | bytes 589832 | tf_op jit(solution)/shard_map/ppermute | solution.py:321
  86.6 8.0 %collective-permute-start.17 = (bf16[2,128,384]{2,1,0:T(8,128)(2,1)S(1)}, bf16[2,128,384]{2,1,0:T(8,128)(2,1)S(1)}, u32[]{:S(2)}, u32[]{:S(2)}) collective-permute-start(bf16[2,128,384]{2,1,0:T(8,128)(2,1)S(1)} %middle.1.refs_4_), channel_id=1, source_target_pairs={{0,96},{16,112},{32,64},{48,80},{64,32},{80,48},{96,0},{112,16},{1... | collective-permute-start | bytes 589832 | tf_op jit(solution)/shard_map/ppermute | solution.py:321
  88.0 7.1 %collective-permute-start.18 = (bf16[2,128,384]{2,1,0:T(8,128)(2,1)S(1)}, bf16[2,128,384]{2,1,0:T(8,128)(2,1)S(1)}, u32[]{:S(2)}, u32[]{:S(2)}) collective-permute-start(bf16[2,128,384]{2,1,0:T(8,128)(2,1)S(1)} %middle.1.refs_4_), channel_id=1, source_target_pairs={{0,16},{16,0},{32,48},{48,32},{64,80},{80,64},{96,112},{112,96},{1... | collective-permute-start | bytes 589832 | tf_op jit(solution)/shard_map/ppermute | solution.py:322
  92.4 2.7 %collective-permute-start.19 = (bf16[2,128,384]{2,1,0:T(8,128)(2,1)S(1)}, bf16[2,128,384]{2,1,0:T(8,128)(2,1)S(1)}, u32[]{:S(2)}, u32[]{:S(2)}) collective-permute-start(bf16[2,128,384]{2,1,0:T(8,128)(2,1)S(1)} %collective-permute-done.15.refs_5_), channel_id=1, source_target_pairs={{0,16},{16,0},{32,48},{48,32},{64,80},{80,64},{96,112},{112,96},{1... | collective-permute-start | bytes 589832 | tf_op jit(solution)/shard_map/ppermute | solution.py:322
  94.6 1.4 %collective-permute-start.20 = (bf16[2,128,384]{2,1,0:T(8,128)(2,1)S(1)}, bf16[2,128,384]{2,1,0:T(8,128)(2,1)S(1)}, u32[]{:S(2)}, u32[]{:S(2)}) collective-permute-start(bf16[2,128,384]{2,1,0:T(8,128)(2,1)S(1)} %collective-permute-done.16.refs_6_), channel_id=1, source_target_pairs={{0,16},{16,0},{32,48},{48,32},{64,80},{80,64},{96,112},{112,96},{1... | collective-permute-start | bytes 589832 | tf_op jit(solution)/shard_map/ppermute | solution.py:322
  94.6 1.7 %collective-permute-start.21 = (bf16[2,128,384]{2,1,0:T(8,128)(2,1)S(1)}, bf16[2,128,384]{2,1,0:T(8,128)(2,1)S(1)}, u32[]{:S(2)}, u32[]{:S(2)}) collective-permute-start(bf16[2,128,384]{2,1,0:T(8,128)(2,1)S(1)} %collective-permute-done.17.refs_7_), channel_id=1, source_target_pairs={{0,16},{16,0},{32,48},{48,32},{64,80},{80,64},{96,112},{112,96},{1... | collective-permute-start | bytes 589832 | tf_op jit(solution)/shard_map/ppermute | solution.py:322
  106.6 33.6 %all-to-all-start.2 = ((bf16[16,136,384]{2,1,0:T(8,128)(2,1)}), bf16[16,136,384]{2,1,0:T(8,128)(2,1)S(1)}, u32[]{:S(2)}, u32[]{:S(2)}) async-start(bf16[16,136,384]{2,1,0:T(8,128)(2,1)} %boundary_second.1), calls=%async_computation.2 | async-start | bytes 3342336 | tf_op jit(solution)/shard_map/all_to_all | solution.py:377

commit v3 on v2

--- a/solution.py
+++ b/solution.py
@@ -10,7 +10,7 @@
 WAVES = 384
 LANES = 128
 ROWS = 512
-LIMIT = 24
+LIMIT = 12
 
 
 def onehot(keys, count):
@@ -141,20 +141,34 @@
     )(*args)
 
 
+def stage_kernel(side_ref, single_hbm, double_hbm, single_ref, double_ref, sems):
+    copies = [
+        pltpu.make_async_copy(single_hbm, single_ref, sems.at[0]),
+        pltpu.make_async_copy(double_hbm, double_ref, sems.at[1]),
+    ]
+    for copy in copies:
+        copy.start()
+    for copy in copies:
+        copy.wait()
+
+
+def stage(side, single_layer, double_layer):
+    hbm = pl.BlockSpec(memory_space=pltpu.HBM)
+    return pl.pallas_call(
+        stage_kernel,
+        in_specs=[pl.BlockSpec(memory_space=pltpu.SMEM), hbm, hbm],
+        out_specs=[pl.BlockSpec(memory_space=pltpu.VMEM)] * 2,
+        out_shape=[pltpu.VMEM((2048, 1024), BF)] * 2,
+        scratch_shapes=[pltpu.SemaphoreType.DMA((2,))],
+        compiler_params=pltpu.CompilerParams(vmem_limit_bytes=10 << 20),
+        name="stage",
+    )(side, in_hbm(single_layer), in_hbm(double_layer))
+
+
 def boundary_kernel(first, order_ref, rows_ref, cols_ref, count_ref, *refs):
     chunks = refs[:8]
     single_ref, double_ref, near_ref = refs[8:11]
-    extra_ref, *keys, out_ref, single_buf, double_buf, phi_ref, w_ref, acc_ref, sems = refs[11:]
-    copies = []
-    for i in range(2048 // ROWS):
-        part = pl.ds(i * ROWS, ROWS)
-        copies.append((
-            pltpu.make_async_copy(single_ref.at[part], single_buf.at[part], sems.at[0, i]),
-            pltpu.make_async_copy(double_ref.at[part], double_buf.at[part], sems.at[1, i]),
-        ))
-    for pair in copies:
-        pair[0].start()
-        pair[1].start()
+    extra_ref, *keys, out_ref, phi_ref, w_ref, acc_ref = refs[11:]
     for k in range(8):
         at = pl.multiple_of(order_ref[k] * 128, 128)
         phi_ref[pl.ds(at, 128), :] = chunks[k][0]
@@ -164,10 +178,9 @@
 
     for i in range(2048 // ROWS):
         part = pl.ds(i * ROWS, ROWS)
-        copies[i][0].wait()
-        far = jnp.dot(single_buf[part, :], phi_ref[...], preferred_element_type=F32)
-        copies[i][1].wait()
-        acc_ref[...] = far + jnp.dot(double_buf[part, :], w_ref[...], preferred_element_type=F32)
+        acc_ref[...] = jnp.dot(single_ref[part, :], phi_ref[...], preferred_element_type=F32) + jnp.dot(
+            double_ref[part, :], w_ref[...], preferred_element_type=F32
+        )
 
         def add_near(k, carry, i=i):
             @pl.when((k < count_ref[0]) & (rows_ref[k] // (ROWS // 128) == i))
@@ -194,28 +207,23 @@
     out_ref[:, 128:136, :] = extra_ref[...]
 
 
-def boundary(order, near, chunks, single_layer, double_layer, extra, *keys):
+def boundary(order, near, chunks, matrices, extra, *keys):
     near_blocks, near_rows, near_cols, near_count = near
     first = len(keys) > 0
     vmem = pl.BlockSpec(memory_space=pltpu.VMEM)
-    hbm = pl.BlockSpec(memory_space=pltpu.HBM)
-    matrix = pltpu.VMEM((2048, 1024), BF)
     return pl.pallas_call(
         lambda *refs: boundary_kernel(first, *refs),
-        in_specs=[pl.BlockSpec(memory_space=pltpu.SMEM)] * 4 + [vmem] * 8 + [hbm, hbm] + [vmem] * (2 + len(keys)),
+        in_specs=[pl.BlockSpec(memory_space=pltpu.SMEM)] * 4 + [vmem] * (12 + len(keys)),
         out_specs=vmem,
         out_shape=jax.ShapeDtypeStruct((16, 136, WAVES), BF),
         scratch_shapes=[
-            matrix,
-            matrix,
             pltpu.VMEM((1024, WAVES), BF),
             pltpu.VMEM((1024, WAVES), BF),
             pltpu.VMEM((ROWS, WAVES), F32),
-            pltpu.SemaphoreType.DMA((2, 2048 // ROWS)),
         ],
         compiler_params=pltpu.CompilerParams(vmem_limit_bytes=LIMIT << 20),
         name="boundary_first" if first else "boundary_second",
-    )(order, near_rows, near_cols, near_count, *chunks, in_hbm(single_layer), in_hbm(double_layer), near_blocks, extra, *keys)
+    )(order, near_rows, near_cols, near_count, *chunks, *matrices, near_blocks, extra, *keys)
 
 
 def faces_kernel(side_ref, low_x, high_x, low_y, high_y, sib, far, even, odd):
@@ -359,21 +367,24 @@
     packed = pack(flux, displacement, route_row)
     got = lax.all_to_all(packed.reshape(16, 8, 2 * WAVES + 128), "col", 0, 0, tiled=True)
     halos = swap_faces(*faces_of(side, displacement))
+    field, trace, outgoing, *faces = stencil(side, displacement, halos, stiff, mixing, flux, route_row)
+    got = after(got, outgoing)
     chunk = jnp.stack(
         [got[:, :, :WAVES].reshape(128, WAVES), got[:, :, WAVES : 2 * WAVES].reshape(128, WAVES)], 0
     )
     keys = got[:, 0, 2 * WAVES :].astype(jnp.int32).reshape(8, 2, 128)
     keys = (keys + jnp.array([0, 128], jnp.int32)[None, :, None]).reshape(8, 1, 256)
 
-    field, trace, outgoing, *faces = stencil(side, displacement, halos, stiff, mixing, flux, route_row)
+    matrices = stage(after(side, chunk), single_layer, double_layer)
     chunks, order = across_rows(chunk)
-    sums = boundary(order, near, chunks, single_layer, double_layer, outgoing.reshape(16, 8, WAVES), keys)
+    sums = boundary(order, near, chunks, matrices, outgoing.reshape(16, 8, WAVES), keys)
     got = lax.all_to_all(sums, "col", 0, 0, tiled=True)
     halos = swap_faces(*after(faces, sums))
     chunk = middle(after(got, halos), chunk)
+    matrices = stage(after(side, chunk), single_layer, double_layer)
 
     chunks, order = across_rows(chunk)
-    sums = boundary(order, near, chunks, single_layer, double_layer, chunk[0].reshape(16, 8, WAVES))
+    sums = boundary(order, near, chunks, matrices, chunk[0].reshape(16, 8, WAVES))
     got = lax.all_to_all(sums, "col", 0, 0, tiled=True)
     (field,) = stencil(side, field, after(halos, sums), stiff, mixing)
     new_flux, field = last(after(got, field), trace, routes.reshape(128, 1), field)

time: 145 us -> 142 us (0.979)
  waiting for transfers between devices: 60.8 us -> 53.4 us
  Pallas kernels: 39.3 us -> 42 us
  starting transfers between devices: 41 us -> 42.7 us
    pallas_call x0 -> x2, Pallas kernels: none -> 8.05 us  [stage(): pl.pallas_call(stage_kernel, in_specs=[pl.BlockSpec(memory_space=pltpu.SM...]
    pallas_call x2, Pallas kernels: 21.6 us -> 16.3 us  [boundary(): pl.pallas_call(lambda *refs: boundary_kernel(first, *refs), in_specs=[pl....]
    all_to_all x1, waiting for transfers between devices: 7.82 us -> 2.58 us  [local(): lax.all_to_all(packed.reshape(16, 8, 2 * WAVES + 128), 'col', 0, 0, tiled...]
    ppermute x2, starting transfers between devices: 7.19 us -> 4.03 us  [swap_faces(): lax.ppermute(even, 'col', swapped(16, 1))]
    all_to_all x1, starting transfers between devices: 6.24 us -> 9.2 us  [local(): lax.all_to_all(packed.reshape(16, 8, 2 * WAVES + 128), 'col', 0, 0, tiled...]
    ppermute x6, waiting for transfers between devices: 8.58 us -> 5.88 us  [across_rows(): lax.ppermute(chunk, 'row', swapped(8, k))]
    all_to_all x2, starting transfers between devices: 12.3 us -> 14.3 us  [local(): got = lax.all_to_all(sums, 'col', 0, 0, tiled=True)]
  transfers between devices with their start and end apart: 25 -> 25, of which waited for: 14 -> 12; matrix products, arithmetic and copies ran while one was open for 0% -> 0% of each run, Pallas kernels for 9% -> 14%
where the time goes in v3:
time: 142 us; the launch traced here: 141 us
  waiting for transfers between devices  53.4 us (38%)
  starting transfers between devices  42.7 us (30%)
  Pallas kernels  42 us (30%)
  between operations  1.61 us (1%)
    all_to_all x2, waiting for transfers between devices, local(): got = lax.all_to_all(sums, 'col', 0, 0, tiled=True)  23.4 us
    ppermute x2, waiting for transfers between devices, swap_faces(): lax.ppermute(even, 'col', swapped(16, 1))  17 us
    pallas_call x2, Pallas kernels, boundary(): pl.pallas_call(lambda *refs: boundary_kernel(first, *refs), in_specs=[pl....  16.3 us
    all_to_all x2, starting transfers between devices, local(): got = lax.all_to_all(sums, 'col', 0, 0, tiled=True)  14.3 us
    pallas_call x2, Pallas kernels, stencil(): pl.pallas_call(lambda *refs: stencil_kernel(first, *refs), grid=(WAVES //...  9.69 us
    all_to_all x1, starting transfers between devices, local(): lax.all_to_all(packed.reshape(16, 8, 2 * WAVES + 128), 'col', 0, 0, tiled...  9.2 us
    ppermute x6, starting transfers between devices, across_rows(): lax.ppermute(chunk, 'row', swapped(8, k))  8.35 us
    pallas_call x2, Pallas kernels, stage(): pl.pallas_call(stage_kernel, in_specs=[pl.BlockSpec(memory_space=pltpu.SM...  8.05 us
  transfers between devices with their start and end apart: 25, of which 12 were waited for; matrix products, arithmetic and copies ran while one was open for 0% of the time, Pallas kernels for 14%

profile of v3, /device:TPU:2, one launch (start us, length us, event | category | flops | bytes accessed | tf_op | source)
XLA Modules:
  0.0 140.5 jit_solution(13512821124429687680)
XLA Ops:
  0.6 0.1 pad_add_fusion.side_ref.refs_0_
  0.7 1.4 faces.1
  2.1 0.0 copy-start.6
  2.1 0.0 copy-start.1
  2.1 0.0 copy-start.2
  2.1 0.1 collective-permute-start
  2.2 2.4 %collective-permute-start.1 = (bf16[3,8,8,384]{3,2,1,0:T(8,128)(2,1)S(1)}, bf16[3,8,8,384]{3,2,1,0:T(8,128)(2,1)S(1)}, u32[]{:S(2)}, u32[]{:S(2)}) collective-permute-start(bf16[3,8,8,384]{3,2,1,0:T(8,128)(2,1)S(1)} %get-tuple-element.33), channel_id=1, source_target_pairs={{16,32},{32,16},{48,64},{64,48},{80,96},{96,80},{17,33},{33,17},{4... | collective-permute-start | bytes 442376 | tf_op jit(solution)/shard_map/ppermute | solution.py:339
  4.7 2.1 %collective-permute-start.2 = (bf16[3,8,8,384]{3,2,1,0:T(8,128)(2,1)S(1)}, bf16[3,8,8,384]{3,2,1,0:T(8,128)(2,1)S(1)}, u32[]{:S(2)}, u32[]{:S(2)}) collective-permute-start(bf16[3,8,8,384]{3,2,1,0:T(8,128)(2,1)S(1)} %get-tuple-element.34), channel_id=1, source_target_pairs={{0,1},{1,0},{2,3},{3,2},{4,5},{5,4},{6,7},{7,6},{8,9},{9,8},{10,11... | collective-permute-start | bytes 442376 | tf_op jit(solution)/shard_map/ppermute | solution.py:340
  6.8 0.7 collective-permute-start.3
  7.4 2.5 %pack.1 = bf16[128,896]{1,0:T(8,128)(2,1)} custom-call(f32[128,384]{1,0:T(8,128)} %refs_8_.1, f32[3,8,8,8,384]{4,3,2,1,0:T(8,128)} %refs_2_.1, s32[1,128]{1,0:T(1,128)S(1)} %bitcast.26), custom_call_target="tpu_custom_call" | custom-call | tf_op jit(solution)/shard_map/pack/pallas_call | solution.py:39
  10.0 9.2 %all-to-all-start = ((bf16[16,8,896]{2,1,0:T(8,128)(2,1)}), bf16[16,8,896]{2,1,0:T(8,128)(2,1)S(1)}, u32[]{:S(2)}, u32[]{:S(2)}) async-start(bf16[16,8,896]{2,1,0:T(8,128)(2,1)} %bitcast.4), calls=%async_computation | async-start | bytes 458752 | tf_op jit(solution)/shard_map/all_to_all | solution.py:368
  19.2 0.0 copy-start.7
  19.2 0.4 copy.18.refs_7_
  20.3 0.1 broadcast_bitcast_fusion
  20.4 0.0 collective-permute-done.refs_3_
  20.4 0.0 collective-permute-done.1.refs_4_
  20.4 0.0 collective-permute-done.2.refs_5_
  20.4 4.9 %stencil_first.1 = (f32[3,8,8,8,384]{4,3,2,1,0:T(8,128)}, f32[128,384]{1,0:T(8,128)S(1)}, bf16[128,384]{1,0:T(8,128)(2,1)S(1)}, bf16[3,8,8,384]{3,2,1,0:T(8,128)...) custom-call(s32[2]{0:T(128)S(1)} %pad_add_fusion.side_ref.refs_0_, ...), custom_call_target="tpu_custom_call" | custom-call | tf_op jit(solution)/shard_map/stencil_first/pallas_call | solution.py:133
  25.4 2.6 %all-to-all-done = bf16[16,8,896]{2,1,0:T(8,128)(2,1)S(1)} async-done(((bf16[16,8,896]{2,1,0:T(8,128)(2,1)}), bf16[16,8,896]{2,1,0:T(8,128)(2,1)S(1)}, u32[]{:S(2)}, u32[]{:S(2)}) %all-to-all-start) | async-done | bytes 229408 | tf_op jit(solution)/shard_map/all_to_all | solution.py:368
  28.0 1.3 collective-permute-start.6
  29.3 0.8 collective-permute-start.4
  30.1 2.1 %collective-permute-start.5 = (bf16[2,128,384]{2,1,0:T(8,128)(2,1)S(1)}, bf16[2,128,384]{2,1,0:T(8,128)(2,1)S(1)}, u32[]{:S(2)}, u32[]{:S(2)}) collective-permute-start(bf16[2,128,384]{2,1,0:T(8,128)(2,1)S(1)} %pad_maximum_fusion.refs_4_.chunk_ref), channel_id=1, source_target_pairs={{0,32},{16,48},{32,0},{48,16},{64,96},{80,112},{96,64},{112,80},{1... | collective-permute-start | bytes 589832 | tf_op jit(solution)/shard_map/ppermute | solution.py:329
  32.2 0.0 collective-permute-start.7
  32.2 0.0 copy-start
  32.2 0.0 copy-start.4
  32.2 0.0 copy-start.5
  32.2 4.0 %stage.2 = (bf16[2048,1024]{1,0:T(8,128)(2,1)S(1)}, bf16[2048,1024]{1,0:T(8,128)(2,1)S(1)}) custom-call(s32[2]{0:T(128)S(1)} %pad_add_fusion.side_ref.refs_0_, bf16[2048,1024]{1,0:T(8,128)(2,1)} %single_hbm.3, bf16[2048,1024]{1,0:T(8,128)(2,1)} %double_hbm.3), custom_call_target="tpu_custom_call" | custom-call | tf_op jit(solution)/shard_map/stage/pallas_call | solution.py:157
  36.3 1.1 collective-permute-done.6.refs_7_
  37.4 0.0 collective-permute-start.10
  37.4 0.8 collective-permute-done.4.refs_5_
  38.2 1.6 %collective-permute-done.5.refs_6_ = bf16[2,128,384]{2,1,0:T(8,128)(2,1)S(1)} collective-permute-done((bf16[2,128,384]{2,1,0:T(8,128)(2,1)S(1)}, bf16[2,128,384]{2,1,0:T(8,128)(2,1)S(1)}, u32[]{:S(2)}, u32[]{:S(2)}) %collective-permute-start.5) | collective-permute-done | bytes 196640 | tf_op jit(solution)/shard_map/ppermute | solution.py:329
  39.8 0.0 collective-permute-start.9
  39.8 0.0 collective-permute-done.10.refs_11_
  39.8 0.0 collective-permute-done.8.refs_9_
  39.8 1.4 collective-permute-done.9.refs_10_
  41.2 8.4 %boundary_first.1 = bf16[16,136,384]{2,1,0:T(8,128)(2,1)} custom-call(s32[8]{0:T(128)S(1)} %broadcast_xor_fusion.refs_0_, s32[8]{0:T(128)S(1)} %bitcast.29, s32[8]{0:T(128)S(1)} %bitcast.31, s32[1]{0:T(128)} %bitcast.21.refs_3_, bf16[2,128,384]{2,1,0:T(8,128)(2,1)S(1)} %pad_maximum_fusion.refs_4_.chunk_ref, ...), custom_call_target="tpu_custom_call" | custom-call | tf_op jit(solution)/shard_map/boundary_first/pallas_call | solution.py:214
  49.7 6.4 %all-to-all-start.1 = ((bf16[16,136,384]{2,1,0:T(8,128)(2,1)}), bf16[16,136,384]{2,1,0:T(8,128)(2,1)S(1)}, u32[]{:S(2)}, u32[]{:S(2)}) async-start(bf16[16,136,384]{2,1,0:T(8,128)(2,1)} %boundary_first.1), calls=%async_computation.1 | async-start | bytes 3342336 | tf_op jit(solution)/shard_map/all_to_all | solution.py:381
  56.0 0.1 collective-permute-start.11
  56.1 2.4 %collective-permute-start.12 = (bf16[3,8,8,384]{3,2,1,0:T(8,128)(2,1)}, bf16[3,8,8,384]{3,2,1,0:T(8,128)(2,1)S(1)}, u32[]{:S(2)}, u32[]{:S(2)}) collective-permute-start(bf16[3,8,8,384]{3,2,1,0:T(8,128)(2,1)} %get-tuple-element.46), channel_id=1, source_target_pairs={{16,32},{32,16},{48,64},{64,48},{80,96},{96,80},{17,33},{33,17},{4... | collective-permute-start | bytes 442376 | tf_op jit(solution)/shard_map/ppermute | solution.py:339
  58.5 1.9 %collective-permute-start.13 = (bf16[3,8,8,384]{3,2,1,0:T(8,128)(2,1)S(1)}, bf16[3,8,8,384]{3,2,1,0:T(8,128)(2,1)S(1)}, u32[]{:S(2)}, u32[]{:S(2)}) collective-permute-start(bf16[3,8,8,384]{3,2,1,0:T(8,128)(2,1)S(1)} %get-tuple-element.47), channel_id=1, source_target_pairs={{0,1},{1,0},{2,3},{3,2},{4,5},{5,4},{6,7},{7,6},{8,9},{9,8},{10,11... | collective-permute-start | bytes 442376 | tf_op jit(solution)/shard_map/ppermute | solution.py:340
  60.5 0.7 collective-permute-start.14
  61.1 0.0 collective-permute-done.11.refs_3_
  61.1 1.7 %collective-permute-done.12.refs_4_ = bf16[3,8,8,384]{3,2,1,0:T(8,128)(2,1)S(1)} collective-permute-done((bf16[3,8,8,384]{3,2,1,0:T(8,128)(2,1)}, bf16[3,8,8,384]{3,2,1,0:T(8,128)(2,1)S(1)}, u32[]{:S(2)}, u32[]{:S(2)}) %collective-permute-start.12) | collective-permute-done | bytes 147488 | tf_op jit(solution)/shard_map/ppermute | solution.py:339
  62.8 17.0 %collective-permute-done.13.refs_5_ = bf16[3,8,8,384]{3,2,1,0:T(8,128)(2,1)S(1)} collective-permute-done((bf16[3,8,8,384]{3,2,1,0:T(8,128)(2,1)S(1)}, bf16[3,8,8,384]{3,2,1,0:T(8,128)(2,1)S(1)}, u32[]{:S(2)}, u32[]{:S(2)}) %collective-permute-start.13) | collective-permute-done | bytes 147488 | tf_op jit(solution)/shard_map/ppermute | solution.py:340
  79.8 0.0 collective-permute-done.14.refs_6_
  79.8 2.1 %all-to-all-done.1.got_ref = bf16[16,136,384]{2,1,0:T(8,128)(2,1)S(1)} async-done(((bf16[16,136,384]{2,1,0:T(8,128)(2,1)}), bf16[16,136,384]{2,1,0:T(8,128)(2,1)S(1)}, u32[]{:S(2)}, u32[]{:S(2)}) %all-to-all-start.1) | async-done | bytes 1671200 | tf_op jit(solution)/shard_map/all_to_all | solution.py:381
  81.9 0.6 middle.1.refs_4_
  82.5 0.4 collective-permute-start.15
  83.0 1.8 %collective-permute-start.16 = (bf16[2,128,384]{2,1,0:T(8,128)(2,1)S(1)}, bf16[2,128,384]{2,1,0:T(8,128)(2,1)S(1)}, u32[]{:S(2)}, u32[]{:S(2)}) collective-permute-start(bf16[2,128,384]{2,1,0:T(8,128)(2,1)S(1)} %middle.1.refs_4_), channel_id=1, source_target_pairs={{0,32},{16,48},{32,0},{48,16},{64,96},{80,112},{96,64},{112,80},{1... | collective-permute-start | bytes 589832 | tf_op jit(solution)/shard_map/ppermute | solution.py:329
  84.8 1.9 %collective-permute-start.17 = (bf16[2,128,384]{2,1,0:T(8,128)(2,1)S(1)}, bf16[2,128,384]{2,1,0:T(8,128)(2,1)S(1)}, u32[]{:S(2)}, u32[]{:S(2)}) collective-permute-start(bf16[2,128,384]{2,1,0:T(8,128)(2,1)S(1)} %middle.1.refs_4_), channel_id=1, source_target_pairs={{0,96},{16,112},{32,64},{48,80},{64,32},{80,48},{96,0},{112,16},{1... | collective-permute-start | bytes 589832 | tf_op jit(solution)/shard_map/ppermute | solution.py:329
  86.7 0.0 collective-permute-start.18
  86.7 4.0 %stage.3 = (bf16[2048,1024]{1,0:T(8,128)(2,1)S(1)}, bf16[2048,1024]{1,0:T(8,128)(2,1)S(1)}) custom-call(s32[2]{0:T(128)S(1)} %pad_add_fusion.side_ref.refs_0_, bf16[2048,1024]{1,0:T(8,128)(2,1)} %single_hbm.3, bf16[2048,1024]{1,0:T(8,128)(2,1)} %double_hbm.3), custom_call_target="tpu_custom_call" | custom-call | tf_op jit(solution)/shard_map/stage/pallas_call | solution.py:157
  90.7 0.8 collective-permute-done.15.refs_5_
  91.6 0.0 collective-permute-start.19
  91.6 0.5 collective-permute-start.20
  92.1 1.6 %collective-permute-done.17.refs_7_ = bf16[2,128,384]{2,1,0:T(8,128)(2,1)S(1)} collective-permute-done((bf16[2,128,384]{2,1,0:T(8,128)(2,1)S(1)}, bf16[2,128,384]{2,1,0:T(8,128)(2,1)S(1)}, u32[]{:S(2)}, u32[]{:S(2)}) %collective-permute-start.17) | collective-permute-done | bytes 196640 | tf_op jit(solution)/shard_map/ppermute | solution.py:329
  93.6 0.0 collective-permute-start.21
  93.7 1.4 collective-permute-done.21.refs_11_
  95.1 7.8 %boundary_second.1 = bf16[16,136,384]{2,1,0:T(8,128)(2,1)} custom-call(s32[8]{0:T(128)S(1)} %broadcast_xor_fusion.refs_0_, s32[8]{0:T(128)S(1)} %bitcast.30, s32[8]{0:T(128)S(1)} %bitcast.32, s32[1]{0:T(128)} %bitcast.22.refs_3_, bf16[2,128,384]{2,1,0:T(8,128)(2,1)S(1)} %middle.1.refs_4_, bf16[2,128,384]{2,1,0:T(8,128)(2,1)S(1)} %collective-permute-done.15.refs_5_, ...), custom_call_target="tpu_custom_call" | custom-call | tf_op jit(solution)/shard_map/boundary_second/pallas_call | solution.py:214
  102.9 7.9 %all-to-all-start.2 = ((bf16[16,136,384]{2,1,0:T(8,128)(2,1)}), bf16[16,136,384]{2,1,0:T(8,128)(2,1)S(1)}, u32[]{:S(2)}, u32[]{:S(2)}) async-start(bf16[16,136,384]{2,1,0:T(8,128)(2,1)} %boundary_second.1), calls=%async_computation.2 | async-start | bytes 3342336 | tf_op jit(solution)/shard_map/all_to_all | solution.py:388
  110.8 0.1 copy.20.route_ref
  111.0 4.7 %stencil_second.1.comp_ref = f32[3,8,8,8,384]{4,3,2,1,0:T(8,128)} custom-call(s32[2]{0:T(128)S(1)} %pad_add_fusion.side_ref.refs_0_, f32[3,3]{1,0:T(4,128)S(1)} %copy-done.2, f32[3,8,8,8,384]{4,3,2,1,0:T(8,128)} %get-tuple-element.53.refs_2_, bf16[3,8,8,384]{3,2,1,0:T(8,128)(2,1)S(1)} %collective-permute-done.11.refs_3_, ...), custom_call_target="tpu_custom_call" | custom-call | tf_op jit(solution)/shard_map/stencil_second/pallas_call | solution.py:133
  115.7 21.3 %all-to-all-done.2.got_ref = bf16[16,136,384]{2,1,0:T(8,128)(2,1)S(1)} async-done(((bf16[16,136,384]{2,1,0:T(8,128)(2,1)}), bf16[16,136,384]{2,1,0:T(8,128)(2,1)S(1)}, u32[]{:S(2)}, u32[]{:S(2)}) %all-to-all-start.2) | async-done | bytes 1671200 | tf_op jit(solution)/shard_map/all_to_all | solution.py:388
  137.0 3.5 %last.1 = (f32[128,384]{1,0:T(8,128)}, f32[3,8,8,8,384]{4,3,2,1,0:T(8,128)}) custom-call(bf16[16,136,384]{2,1,0:T(8,128)(2,1)S(1)} %all-to-all-done.2.got_ref, f32[128,384]{1,0:T(8,128)S(1)} %get-tuple-element.59.w_ref, s32[128,1]{1,0:T(8,128)S(1)} %copy.20.route_ref, f32[3,8,8,8,384]{4,3,2,1,0:T(8,128)} %stencil_second.1.comp_ref), custom_call_target="tpu_custom_call", output_to_operand_aliasing={{1}: (3, {})} | custom-call | tf_op jit(solution)/shard_map/last/pallas_call | solution.py:298
  (23 shorter events, 0.1 us)
Async XLA Ops:
  0.7 6.7 %copy-start.3 = (s32[128]{0:T(128)S(1)}, s32[128]{0:T(128)}, u32[]{:S(2)}) copy-start(s32[128]{0:T(128)} %param.24) | copy-start | bytes 1540
  2.1 17.1 %copy-start.6 = (f32[8,8,8]{2,1,0:T(8,128)S(1)}, f32[8,8,8]{2,1,0:T(8,128)}, u32[]{:S(2)}) copy-start(f32[8,8,8]{2,1,0:T(8,128)} %param.16) | copy-start | bytes 6148
  2.1 18.3 %copy-start.1 = (f32[128,384]{1,0:T(8,128)S(1)}, f32[128,384]{1,0:T(8,128)}, u32[]{:S(2)}) copy-start(f32[128,384]{1,0:T(8,128)} %refs_8_.1) | copy-start | bytes 589828
  2.1 18.3 %copy-start.2 = (f32[3,3]{1,0:T(4,128)S(1)}, f32[3,3]{1,0:T(4,128)}, u32[]{:S(2)}) copy-start(f32[3,3]{1,0:T(4,128)} %refs_1_.3) | copy-start | bytes 112
  2.1 18.2 %collective-permute-start = (bf16[3,8,8,384]{3,2,1,0:T(8,128)(2,1)S(1)}, bf16[3,8,8,384]{3,2,1,0:T(8,128)(2,1)S(1)}, u32[]{:S(2)}, u32[]{:S(2)}) collective-permute-start(bf16[3,8,8,384]{3,2,1,0:T(8,128)(2,1)S(1)} %get-tuple-element.32), channel_id=1, source_target_pairs={{0,16},{16,0},{32,48},{48,32},{64,80},{80,64},{96,112},{112,96},{1... | collective-permute-start | bytes 442376 | tf_op jit(solution)/shard_map/ppermute | solution.py:338
  2.2 18.1 %collective-permute-start.1 = (bf16[3,8,8,384]{3,2,1,0:T(8,128)(2,1)S(1)}, bf16[3,8,8,384]{3,2,1,0:T(8,128)(2,1)S(1)}, u32[]{:S(2)}, u32[]{:S(2)}) collective-permute-start(bf16[3,8,8,384]{3,2,1,0:T(8,128)(2,1)S(1)} %get-tuple-element.33), channel_id=1, source_target_pairs={{16,32},{32,16},{48,64},{64,48},{80,96},{96,80},{17,33},{33,17},{4... | collective-permute-start | bytes 442376 | tf_op jit(solution)/shard_map/ppermute | solution.py:339
  4.7 15.7 %collective-permute-start.2 = (bf16[3,8,8,384]{3,2,1,0:T(8,128)(2,1)S(1)}, bf16[3,8,8,384]{3,2,1,0:T(8,128)(2,1)S(1)}, u32[]{:S(2)}, u32[]{:S(2)}) collective-permute-start(bf16[3,8,8,384]{3,2,1,0:T(8,128)(2,1)S(1)} %get-tuple-element.34), channel_id=1, source_target_pairs={{0,1},{1,0},{2,3},{3,2},{4,5},{5,4},{6,7},{7,6},{8,9},{9,8},{10,11... | collective-permute-start | bytes 442376 | tf_op jit(solution)/shard_map/ppermute | solution.py:340
  6.8 13.6 %collective-permute-start.3 = (bf16[3,8,8,384]{3,2,1,0:T(8,128)(2,1)S(1)}, bf16[3,8,8,384]{3,2,1,0:T(8,128)(2,1)S(1)}, u32[]{:S(2)}, u32[]{:S(2)}) collective-permute-start(bf16[3,8,8,384]{3,2,1,0:T(8,128)(2,1)S(1)} %get-tuple-element.35), channel_id=1, source_target_pairs={{1,2},{2,1},{3,4},{4,3},{5,6},{6,5},{7,8},{8,7},{9,10},{10,9},{11,... | collective-permute-start | bytes 442376 | tf_op jit(solution)/shard_map/ppermute | solution.py:341
  10.0 18.0 %all-to-all-start = ((bf16[16,8,896]{2,1,0:T(8,128)(2,1)}), bf16[16,8,896]{2,1,0:T(8,128)(2,1)S(1)}, u32[]{:S(2)}, u32[]{:S(2)}) async-start(bf16[16,8,896]{2,1,0:T(8,128)(2,1)} %bitcast.4), calls=%async_computation | async-start | bytes 458752 | tf_op jit(solution)/shard_map/all_to_all | solution.py:368
  19.2 13.0 %copy-start.7 = (s32[8]{0:T(128)S(1)}, s32[8]{0:T(128)}, u32[]{:S(2)}) copy-start(s32[8]{0:T(128)} %constant.32.clone) | copy-start | bytes 100
  28.0 9.4 %collective-permute-start.6 = (bf16[2,128,384]{2,1,0:T(8,128)(2,1)S(1)}, bf16[2,128,384]{2,1,0:T(8,128)(2,1)S(1)}, u32[]{:S(2)}, u32[]{:S(2)}) collective-permute-start(bf16[2,128,384]{2,1,0:T(8,128)(2,1)S(1)} %pad_maximum_fusion.refs_4_.chunk_ref), channel_id=1, source_target_pairs={{0,96},{16,112},{32,64},{48,80},{64,32},{80,48},{96,0},{112,16},{1... | collective-permute-start | bytes 589832 | tf_op jit(solution)/shard_map/ppermute | solution.py:329
  29.3 8.9 %collective-permute-start.4 = (bf16[2,128,384]{2,1,0:T(8,128)(2,1)S(1)}, bf16[2,128,384]{2,1,0:T(8,128)(2,1)S(1)}, u32[]{:S(2)}, u32[]{:S(2)}) collective-permute-start(bf16[2,128,384]{2,1,0:T(8,128)(2,1)S(1)} %pad_maximum_fusion.refs_4_.chunk_ref), channel_id=1, source_target_pairs={{0,64},{16,80},{32,96},{48,112},{64,0},{80,16},{96,32},{112,48},{1... | collective-permute-start | bytes 589832 | tf_op jit(solution)/shard_map/ppermute | solution.py:329
  30.1 9.7 %collective-permute-start.5 = (bf16[2,128,384]{2,1,0:T(8,128)(2,1)S(1)}, bf16[2,128,384]{2,1,0:T(8,128)(2,1)S(1)}, u32[]{:S(2)}, u32[]{:S(2)}) collective-permute-start(bf16[2,128,384]{2,1,0:T(8,128)(2,1)S(1)} %pad_maximum_fusion.refs_4_.chunk_ref), channel_id=1, source_target_pairs={{0,32},{16,48},{32,0},{48,16},{64,96},{80,112},{96,64},{112,80},{1... | collective-permute-start | bytes 589832 | tf_op jit(solution)/shard_map/ppermute | solution.py:329
  32.2 7.6 %collective-permute-start.7 = (bf16[2,128,384]{2,1,0:T(8,128)(2,1)S(1)}, bf16[2,128,384]{2,1,0:T(8,128)(2,1)S(1)}, u32[]{:S(2)}, u32[]{:S(2)}) collective-permute-start(bf16[2,128,384]{2,1,0:T(8,128)(2,1)S(1)} %pad_maximum_fusion.refs_4_.chunk_ref), channel_id=1, source_target_pairs={{0,16},{16,0},{32,48},{48,32},{64,80},{80,64},{96,112},{112,96},{1... | collective-permute-start | bytes 589832 | tf_op jit(solution)/shard_map/ppermute | solution.py:330
  32.2 9.0 %copy-start = (bf16[8,1,128,128]{3,2,1,0:T(8,128)(2,1)S(1)}, bf16[8,1,128,128]{3,2,1,0:T(8,128)(2,1)}, u32[]{:S(2)}) copy-start(bf16[8,1,128,128]{3,2,1,0:T(8,128)(2,1)} %param.20) | copy-start | bytes 786436
  32.2 9.0 %copy-start.4 = (s32[8,1]{0,1:T(1,128)S(1)}, s32[8,1]{0,1:T(1,128)}, u32[]{:S(2)}) copy-start(s32[8,1]{0,1:T(1,128)} %param.21) | copy-start | bytes 100
  32.2 9.0 %copy-start.5 = (s32[8,1]{0,1:T(1,128)S(1)}, s32[8,1]{0,1:T(1,128)}, u32[]{:S(2)}) copy-start(s32[8,1]{0,1:T(1,128)} %param.22) | copy-start | bytes 100
  37.4 2.4 %collective-permute-start.10 = (bf16[2,128,384]{2,1,0:T(8,128)(2,1)S(1)}, bf16[2,128,384]{2,1,0:T(8,128)(2,1)S(1)}, u32[]{:S(2)}, u32[]{:S(2)}) collective-permute-start(bf16[2,128,384]{2,1,0:T(8,128)(2,1)S(1)} %collective-permute-done.6.refs_7_), channel_id=1, source_target_pairs={{0,16},{16,0},{32,48},{48,32},{64,80},{80,64},{96,112},{112,96},{1... | collective-permute-start | bytes 589832 | tf_op jit(solution)/shard_map/ppermute | solution.py:330
  38.2 1.6 %collective-permute-start.8 = (bf16[2,128,384]{2,1,0:T(8,128)(2,1)S(1)}, bf16[2,128,384]{2,1,0:T(8,128)(2,1)S(1)}, u32[]{:S(2)}, u32[]{:S(2)}) collective-permute-start(bf16[2,128,384]{2,1,0:T(8,128)(2,1)S(1)} %collective-permute-done.4.refs_5_), channel_id=1, source_target_pairs={{0,16},{16,0},{32,48},{48,32},{64,80},{80,64},{96,112},{112,96},{1... | collective-permute-start | bytes 589832 | tf_op jit(solution)/shard_map/ppermute | solution.py:330
  39.8 1.4 %collective-permute-start.9 = (bf16[2,128,384]{2,1,0:T(8,128)(2,1)S(1)}, bf16[2,128,384]{2,1,0:T(8,128)(2,1)S(1)}, u32[]{:S(2)}, u32[]{:S(2)}) collective-permute-start(bf16[2,128,384]{2,1,0:T(8,128)(2,1)S(1)} %collective-permute-done.5.refs_6_), channel_id=1, source_target_pairs={{0,16},{16,0},{32,48},{48,32},{64,80},{80,64},{96,112},{112,96},{1... | collective-permute-start | bytes 589832 | tf_op jit(solution)/shard_map/ppermute | solution.py:330
  49.7 32.2 %all-to-all-start.1 = ((bf16[16,136,384]{2,1,0:T(8,128)(2,1)}), bf16[16,136,384]{2,1,0:T(8,128)(2,1)S(1)}, u32[]{:S(2)}, u32[]{:S(2)}) async-start(bf16[16,136,384]{2,1,0:T(8,128)(2,1)} %boundary_first.1), calls=%async_computation.1 | async-start | bytes 3342336 | tf_op jit(solution)/shard_map/all_to_all | solution.py:381
  56.0 5.1 %collective-permute-start.11 = (bf16[3,8,8,384]{3,2,1,0:T(8,128)(2,1)}, bf16[3,8,8,384]{3,2,1,0:T(8,128)(2,1)S(1)}, u32[]{:S(2)}, u32[]{:S(2)}) collective-permute-start(bf16[3,8,8,384]{3,2,1,0:T(8,128)(2,1)} %get-tuple-element.45), channel_id=1, source_target_pairs={{0,16},{16,0},{32,48},{48,32},{64,80},{80,64},{96,112},{112,96},{1... | collective-permute-start | bytes 442376 | tf_op jit(solution)/shard_map/ppermute | solution.py:338
  56.1 6.7 %collective-permute-start.12 = (bf16[3,8,8,384]{3,2,1,0:T(8,128)(2,1)}, bf16[3,8,8,384]{3,2,1,0:T(8,128)(2,1)S(1)}, u32[]{:S(2)}, u32[]{:S(2)}) collective-permute-start(bf16[3,8,8,384]{3,2,1,0:T(8,128)(2,1)} %get-tuple-element.46), channel_id=1, source_target_pairs={{16,32},{32,16},{48,64},{64,48},{80,96},{96,80},{17,33},{33,17},{4... | collective-permute-start | bytes 442376 | tf_op jit(solution)/shard_map/ppermute | solution.py:339
  58.5 21.3 %collective-permute-start.13 = (bf16[3,8,8,384]{3,2,1,0:T(8,128)(2,1)S(1)}, bf16[3,8,8,384]{3,2,1,0:T(8,128)(2,1)S(1)}, u32[]{:S(2)}, u32[]{:S(2)}) collective-permute-start(bf16[3,8,8,384]{3,2,1,0:T(8,128)(2,1)S(1)} %get-tuple-element.47), channel_id=1, source_target_pairs={{0,1},{1,0},{2,3},{3,2},{4,5},{5,4},{6,7},{7,6},{8,9},{9,8},{10,11... | collective-permute-start | bytes 442376 | tf_op jit(solution)/shard_map/ppermute | solution.py:340
  60.5 19.4 %collective-permute-start.14 = (bf16[3,8,8,384]{3,2,1,0:T(8,128)(2,1)S(1)}, bf16[3,8,8,384]{3,2,1,0:T(8,128)(2,1)S(1)}, u32[]{:S(2)}, u32[]{:S(2)}) collective-permute-start(bf16[3,8,8,384]{3,2,1,0:T(8,128)(2,1)S(1)} %get-tuple-element.48), channel_id=1, source_target_pairs={{1,2},{2,1},{3,4},{4,3},{5,6},{6,5},{7,8},{8,7},{9,10},{10,9},{11,... | collective-permute-start | bytes 442376 | tf_op jit(solution)/shard_map/ppermute | solution.py:341
  82.5 9.0 %collective-permute-start.15 = (bf16[2,128,384]{2,1,0:T(8,128)(2,1)S(1)}, bf16[2,128,384]{2,1,0:T(8,128)(2,1)S(1)}, u32[]{:S(2)}, u32[]{:S(2)}) collective-permute-start(bf16[2,128,384]{2,1,0:T(8,128)(2,1)S(1)} %middle.1.refs_4_), channel_id=1, source_target_pairs={{0,64},{16,80},{32,96},{48,112},{64,0},{80,16},{96,32},{112,48},{1... | collective-permute-start | bytes 589832 | tf_op jit(solution)/shard_map/ppermute | solution.py:329
  83.0 8.6 %collective-permute-start.16 = (bf16[2,128,384]{2,1,0:T(8,128)(2,1)S(1)}, bf16[2,128,384]{2,1,0:T(8,128)(2,1)S(1)}, u32[]{:S(2)}, u32[]{:S(2)}) collective-permute-start(bf16[2,128,384]{2,1,0:T(8,128)(2,1)S(1)} %middle.1.refs_4_), channel_id=1, source_target_pairs={{0,32},{16,48},{32,0},{48,16},{64,96},{80,112},{96,64},{112,80},{1... | collective-permute-start | bytes 589832 | tf_op jit(solution)/shard_map/ppermute | solution.py:329
  84.8 8.9 %collective-permute-start.17 = (bf16[2,128,384]{2,1,0:T(8,128)(2,1)S(1)}, bf16[2,128,384]{2,1,0:T(8,128)(2,1)S(1)}, u32[]{:S(2)}, u32[]{:S(2)}) collective-permute-start(bf16[2,128,384]{2,1,0:T(8,128)(2,1)S(1)} %middle.1.refs_4_), channel_id=1, source_target_pairs={{0,96},{16,112},{32,64},{48,80},{64,32},{80,48},{96,0},{112,16},{1... | collective-permute-start | bytes 589832 | tf_op jit(solution)/shard_map/ppermute | solution.py:329
  86.7 7.0 %collective-permute-start.18 = (bf16[2,128,384]{2,1,0:T(8,128)(2,1)S(1)}, bf16[2,128,384]{2,1,0:T(8,128)(2,1)S(1)}, u32[]{:S(2)}, u32[]{:S(2)}) collective-permute-start(bf16[2,128,384]{2,1,0:T(8,128)(2,1)S(1)} %middle.1.refs_4_), channel_id=1, source_target_pairs={{0,16},{16,0},{32,48},{48,32},{64,80},{80,64},{96,112},{112,96},{1... | collective-permute-start | bytes 589832 | tf_op jit(solution)/shard_map/ppermute | solution.py:330
  91.6 2.1 %collective-permute-start.19 = (bf16[2,128,384]{2,1,0:T(8,128)(2,1)S(1)}, bf16[2,128,384]{2,1,0:T(8,128)(2,1)S(1)}, u32[]{:S(2)}, u32[]{:S(2)}) collective-permute-start(bf16[2,128,384]{2,1,0:T(8,128)(2,1)S(1)} %collective-permute-done.15.refs_5_), channel_id=1, source_target_pairs={{0,16},{16,0},{32,48},{48,32},{64,80},{80,64},{96,112},{112,96},{1... | collective-permute-start | bytes 589832 | tf_op jit(solution)/shard_map/ppermute | solution.py:330
  91.6 2.1 %collective-permute-start.20 = (bf16[2,128,384]{2,1,0:T(8,128)(2,1)S(1)}, bf16[2,128,384]{2,1,0:T(8,128)(2,1)S(1)}, u32[]{:S(2)}, u32[]{:S(2)}) collective-permute-start(bf16[2,128,384]{2,1,0:T(8,128)(2,1)S(1)} %collective-permute-done.16.refs_6_), channel_id=1, source_target_pairs={{0,16},{16,0},{32,48},{48,32},{64,80},{80,64},{96,112},{112,96},{1... | collective-permute-start | bytes 589832 | tf_op jit(solution)/shard_map/ppermute | solution.py:330
  93.6 1.4 %collective-permute-start.21 = (bf16[2,128,384]{2,1,0:T(8,128)(2,1)S(1)}, bf16[2,128,384]{2,1,0:T(8,128)(2,1)S(1)}, u32[]{:S(2)}, u32[]{:S(2)}) collective-permute-start(bf16[2,128,384]{2,1,0:T(8,128)(2,1)S(1)} %collective-permute-done.17.refs_7_), channel_id=1, source_target_pairs={{0,16},{16,0},{32,48},{48,32},{64,80},{80,64},{96,112},{112,96},{1... | collective-permute-start | bytes 589832 | tf_op jit(solution)/shard_map/ppermute | solution.py:330
  102.9 34.1 %all-to-all-start.2 = ((bf16[16,136,384]{2,1,0:T(8,128)(2,1)}), bf16[16,136,384]{2,1,0:T(8,128)(2,1)S(1)}, u32[]{:S(2)}, u32[]{:S(2)}) async-start(bf16[16,136,384]{2,1,0:T(8,128)(2,1)} %boundary_second.1), calls=%async_computation.2 | async-start | bytes 3342336 | tf_op jit(solution)/shard_map/all_to_all | solution.py:388

commit v4 on v3

--- a/solution.py
+++ b/solution.py
@@ -56,7 +56,7 @@
     if first:
         u_ref, sib, far, even, odd, st_ref, flux_ref, route_ref, out_ref, w_ref, wp_ref, f_sib, f_far, f_even, f_odd = refs
     else:
-        u_ref, sib, far, even, odd, st_ref, out_ref = refs
+        u_ref, sib, far, even, odd, st_ref, out_ref, comp_ref = refs
     row_even = side_ref[0] == 0
     col_even = side_ref[1] == 0
 
@@ -96,7 +96,10 @@
                     value = value - jnp.where(bottom, low, jnp.where(top, high, 0.0))
                     w_ref[pl.ds(x * 8 + y, 1), :] = value[0:1]
                     w_ref[pl.ds(64 + x * 8 + y, 1), :] = value[7:8]
-                out_ref[c, x, y] = value
+                if first or c < 2:
+                    out_ref[c, x, y] = value
+                else:
+                    comp_ref[x, y] = value
 
     plane(0, low_x, lambda c, y: u_ref[c, 1, y])
 
@@ -122,8 +125,11 @@
     in_specs = [pl.BlockSpec(memory_space=pltpu.SMEM)] * 2 + [whole, face, face, face, face,
                 pl.BlockSpec((8, 8, 8, 1), lambda i: (0, 0, 0, 0))]
     args = [side, mixing, in_hbm(field), *halos, stiffness]
-    out_specs = [whole]
+    out_specs = [whole if first else pl.BlockSpec((2, 8, 8, 8, LANES), lambda i: (0, 0, 0, 0, i))]
     out_shape = [pltpu.HBM(field.shape, F32)]
+    if not first:
+        out_specs += [pl.BlockSpec((8, 8, 8, LANES), lambda i: (0, 0, 0, i))]
+        out_shape += [jax.ShapeDtypeStruct(field.shape[1:], F32)]
     if first:
         in_specs += [panel, pl.BlockSpec((1, 128), lambda i: (0, 0))]
         args += [flux, route_row]
@@ -273,44 +279,52 @@
     )(got, chunk)
 
 
-def last_kernel(got_ref, w_ref, route_ref, comp_ref, flux_ref, out_ref, mid_ref):
-    total = got_ref[0, 0:128].astype(F32)
-    for k in range(1, 16):
-        total = total + got_ref[k, 0:128].astype(F32)
-    flux_ref[...] = total - 0.5 * w_ref[...]
+def last_kernel(got_ref, w_ref, route_ref, comp_ref, _, flux_ref, field_ref, mid_ref, new_ref, sems):
     picker = (lax.broadcasted_iota(jnp.int32, (128, 128), 1) == route_ref[...]).astype(F32).astype(BF)
-    mid_ref[...] = jnp.dot(picker, got_ref[:, 128:136, :].reshape(128, LANES), preferred_element_type=F32)
-    depth = lax.broadcasted_iota(jnp.int32, (8, LANES), 0)
-
-    def step(x, carry):
-        for y in range(8):
-            low = mid_ref[pl.ds(x * 8 + y, 1), :]
-            high = mid_ref[pl.ds(64 + x * 8 + y, 1), :]
-            out_ref[x, y] = comp_ref[x, y] - jnp.where(depth == 0, low, jnp.where(depth == 7, high, 0.0))
-        return carry
-
-    lax.fori_loop(0, 8, step, 0)
-
-
-def last(got, trace, route_column, field):
-    comp = pl.BlockSpec((None, 8, 8, 8, LANES), lambda i: (2, 0, 0, 0, i))
-    panel = pl.BlockSpec((128, LANES), lambda i: (0, i))
+    mid_ref[...] = jnp.dot(picker, got_ref[:, 128:136, :].reshape(128, WAVES), preferred_element_type=F32)
+    depth = lax.broadcasted_iota(jnp.int32, (8, WAVES), 0)
+    copies = []
+    for half in range(2):
+
+        def step(x, carry):
+            for y in range(8):
+                low = mid_ref[pl.ds(x * 8 + y, 1), :]
+                high = mid_ref[pl.ds(64 + x * 8 + y, 1), :]
+                new_ref[x, y] = comp_ref[x, y] - jnp.where(depth == 0, low, jnp.where(depth == 7, high, 0.0))
+            return carry
+
+        lax.fori_loop(half * 4, half * 4 + 4, step, 0)
+        part = pl.ds(half * 4, 4)
+        copy = pltpu.make_async_copy(new_ref.at[part], field_ref.at[2, part], sems.at[half])
+        copy.start()
+        copies.append(copy)
+    for row in range(0, 128, 32):
+        part = slice(row, row + 32)
+        total = got_ref[0, part].astype(F32)
+        for k in range(1, 16):
+            total = total + got_ref[k, part].astype(F32)
+        flux_ref[part, :] = total - 0.5 * w_ref[part, :]
+    for copy in copies:
+        copy.wait()
+
+
+def last(got, trace, route_column, comp, field):
+    vmem = pl.BlockSpec(memory_space=pltpu.VMEM)
+    hbm = pl.BlockSpec(memory_space=pltpu.HBM)
     return pl.pallas_call(
         last_kernel,
-        grid=(WAVES // LANES,),
-        in_specs=[
-            pl.BlockSpec((16, 136, LANES), lambda i: (0, 0, i)),
-            panel,
-            pl.BlockSpec((128, 1), lambda i: (0, 0)),
-            comp,
+        in_specs=[vmem, vmem, vmem, vmem, hbm],
+        out_specs=[vmem, hbm],
+        out_shape=[jax.ShapeDtypeStruct((128, WAVES), F32), jax.ShapeDtypeStruct(field.shape, F32)],
+        scratch_shapes=[
+            pltpu.VMEM((128, WAVES), F32),
+            pltpu.VMEM((8, 8, 8, WAVES), F32),
+            pltpu.SemaphoreType.DMA((2,)),
         ],
-        out_specs=[panel, comp],
-        out_shape=[jax.ShapeDtypeStruct((128, WAVES), F32), jax.ShapeDtypeStruct(field.shape, F32)],
-        scratch_shapes=[pltpu.VMEM((128, LANES), F32)],
-        input_output_aliases={3: 1},
+        input_output_aliases={4: 1},
         compiler_params=pltpu.CompilerParams(vmem_limit_bytes=8 << 20),
         name="last",
-    )(got, trace, route_column, in_hbm(field))
+    )(got, trace, route_column, comp, in_hbm(field))
 
 
 def shifted(count, by):
@@ -386,8 +400,8 @@
     chunks, order = across_rows(chunk)
     sums = boundary(order, near, chunks, matrices, chunk[0].reshape(16, 8, WAVES))
     got = lax.all_to_all(sums, "col", 0, 0, tiled=True)
-    (field,) = stencil(side, field, after(halos, sums), stiff, mixing)
-    new_flux, field = last(after(got, field), trace, routes.reshape(128, 1), field)
+    field, comp = stencil(side, field, after(halos, sums), stiff, mixing)
+    new_flux, field = last(after(got, comp), trace, routes.reshape(128, 1), comp, field)
     return (field, new_flux)
 
 

time: 142 us -> 140 us (0.986)
  waiting for transfers between devices: 53.4 us -> 51.6 us
    all_to_all x2, waiting for transfers between devices: 23.4 us -> 20.9 us  [local(): got = lax.all_to_all(sums, 'col', 0, 0, tiled=True)]
    pallas_call x1, Pallas kernels: 3.47 us -> 1.92 us  [last(): pl.pallas_call(last_kernel, in_specs=[vmem, vmem, vmem, vmem, hbm], out_s...]
where the time goes in v4:
time: 140 us; the launch traced here: 139 us
  waiting for transfers between devices  51.6 us (37%)
  starting transfers between devices  43.4 us (31%)
  Pallas kernels  40.6 us (29%)
  between operations  1.8 us (1%)
  local copies, waits for them, and re-layouts  1.64 us (1%)
    all_to_all x2, waiting for transfers between devices, local(): got = lax.all_to_all(sums, 'col', 0, 0, tiled=True)  20.9 us
    ppermute x2, waiting for transfers between devices, swap_faces(): lax.ppermute(even, 'col', swapped(16, 1))  17 us
    pallas_call x2, Pallas kernels, boundary(): pl.pallas_call(lambda *refs: boundary_kernel(first, *refs), in_specs=[pl....  16.6 us
    all_to_all x2, starting transfers between devices, local(): got = lax.all_to_all(sums, 'col', 0, 0, tiled=True)  14.7 us
    pallas_call x2, Pallas kernels, stencil(): pl.pallas_call(lambda *refs: stencil_kernel(first, *refs), grid=(WAVES //...  9.5 us
    all_to_all x1, starting transfers between devices, local(): lax.all_to_all(packed.reshape(16, 8, 2 * WAVES + 128), 'col', 0, 0, tiled...  9.2 us
    ppermute x6, starting transfers between devices, across_rows(): lax.ppermute(chunk, 'row', swapped(8, k))  8.35 us
    pallas_call x2, Pallas kernels, stage(): pl.pallas_call(stage_kernel, in_specs=[pl.BlockSpec(memory_space=pltpu.SM...  8.05 us
  transfers between devices with their start and end apart: 25, of which 12 were waited for; matrix products, arithmetic and copies ran while one was open for 0% of the time, Pallas kernels for 14%

profile of v4, /device:TPU:2, one launch (start us, length us, event | category | flops | bytes accessed | tf_op | source)
XLA Modules:
  0.0 139.2 jit_solution(7310215178357960471)
XLA Ops:
  0.6 0.1 pad_add_fusion.side_ref.refs_0_
  0.7 1.4 faces.1
  2.1 0.0 copy-start.11
  2.1 0.0 copy-start.1
  2.1 0.0 copy-start.4
  2.1 0.1 collective-permute-start
  2.2 2.4 %collective-permute-start.1 = (bf16[3,8,8,384]{3,2,1,0:T(8,128)(2,1)S(1)}, bf16[3,8,8,384]{3,2,1,0:T(8,128)(2,1)S(1)}, u32[]{:S(2)}, u32[]{:S(2)}) collective-permute-start(bf16[3,8,8,384]{3,2,1,0:T(8,128)(2,1)S(1)} %get-tuple-element.35), channel_id=1, source_target_pairs={{16,32},{32,16},{48,64},{64,48},{80,96},{96,80},{17,33},{33,17},{4... | collective-permute-start | bytes 442376 | tf_op jit(solution)/shard_map/ppermute | solution.py:353
  4.7 2.1 %collective-permute-start.2 = (bf16[3,8,8,384]{3,2,1,0:T(8,128)(2,1)S(1)}, bf16[3,8,8,384]{3,2,1,0:T(8,128)(2,1)S(1)}, u32[]{:S(2)}, u32[]{:S(2)}) collective-permute-start(bf16[3,8,8,384]{3,2,1,0:T(8,128)(2,1)S(1)} %get-tuple-element.36), channel_id=1, source_target_pairs={{0,1},{1,0},{2,3},{3,2},{4,5},{5,4},{6,7},{7,6},{8,9},{9,8},{10,11... | collective-permute-start | bytes 442376 | tf_op jit(solution)/shard_map/ppermute | solution.py:354
  6.8 0.7 collective-permute-start.3
  7.4 2.5 %pack.1 = bf16[128,896]{1,0:T(8,128)(2,1)} custom-call(f32[128,384]{1,0:T(8,128)} %refs_8_.1, f32[3,8,8,8,384]{4,3,2,1,0:T(8,128)} %refs_2_.1, s32[1,128]{1,0:T(1,128)S(1)} %bitcast.26), custom_call_target="tpu_custom_call" | custom-call | tf_op jit(solution)/shard_map/pack/pallas_call | solution.py:39
  10.0 9.2 %all-to-all-start = ((bf16[16,8,896]{2,1,0:T(8,128)(2,1)}), bf16[16,8,896]{2,1,0:T(8,128)(2,1)S(1)}, u32[]{:S(2)}, u32[]{:S(2)}) async-start(bf16[16,8,896]{2,1,0:T(8,128)(2,1)} %bitcast.4), calls=%async_computation | async-start | bytes 458752 | tf_op jit(solution)/shard_map/all_to_all | solution.py:382
  19.2 0.0 copy-start.12
  19.2 0.4 copy.18.refs_7_
  20.3 0.1 broadcast_bitcast_fusion
  20.4 0.0 collective-permute-done.refs_3_
  20.4 0.0 collective-permute-done.1.refs_4_
  20.4 0.0 collective-permute-done.2.refs_5_
  20.4 0.0 collective-permute-done.3.refs_6_
  20.4 4.9 %stencil_first.1 = (f32[3,8,8,8,384]{4,3,2,1,0:T(8,128)}, f32[128,384]{1,0:T(8,128)S(1)}, bf16[128,384]{1,0:T(8,128)(2,1)S(1)}, bf16[3,8,8,384]{3,2,1,0:T(8,128)...) custom-call(s32[2]{0:T(128)S(1)} %pad_add_fusion.side_ref.refs_0_, ...), custom_call_target="tpu_custom_call" | custom-call | tf_op jit(solution)/shard_map/stencil_first/pallas_call | solution.py:139
  25.4 2.6 %all-to-all-done = bf16[16,8,896]{2,1,0:T(8,128)(2,1)S(1)} async-done(((bf16[16,8,896]{2,1,0:T(8,128)(2,1)}), bf16[16,8,896]{2,1,0:T(8,128)(2,1)S(1)}, u32[]{:S(2)}, u32[]{:S(2)}) %all-to-all-start) | async-done | bytes 229408 | tf_op jit(solution)/shard_map/all_to_all | solution.py:382
  28.0 1.3 collective-permute-start.6
  29.3 0.8 collective-permute-start.4
  30.1 2.1 %collective-permute-start.5 = (bf16[2,128,384]{2,1,0:T(8,128)(2,1)S(1)}, bf16[2,128,384]{2,1,0:T(8,128)(2,1)S(1)}, u32[]{:S(2)}, u32[]{:S(2)}) collective-permute-start(bf16[2,128,384]{2,1,0:T(8,128)(2,1)S(1)} %pad_maximum_fusion.refs_4_.chunk_ref), channel_id=1, source_target_pairs={{0,32},{16,48},{32,0},{48,16},{64,96},{80,112},{96,64},{112,80},{1... | collective-permute-start | bytes 589832 | tf_op jit(solution)/shard_map/ppermute | solution.py:343
  32.2 0.0 collective-permute-start.7
  32.2 0.0 copy-start
  32.2 0.0 copy-start.6
  32.2 0.0 copy-start.7
  32.2 4.0 %stage.2 = (bf16[2048,1024]{1,0:T(8,128)(2,1)S(1)}, bf16[2048,1024]{1,0:T(8,128)(2,1)S(1)}) custom-call(s32[2]{0:T(128)S(1)} %pad_add_fusion.side_ref.refs_0_, bf16[2048,1024]{1,0:T(8,128)(2,1)} %single_hbm.3, bf16[2048,1024]{1,0:T(8,128)(2,1)} %double_hbm.3), custom_call_target="tpu_custom_call" | custom-call | tf_op jit(solution)/shard_map/stage/pallas_call | solution.py:163
  36.3 1.1 collective-permute-done.6.refs_7_
  37.4 0.8 collective-permute-done.4.refs_5_
  38.2 0.0 collective-permute-start.8
  38.2 1.6 %collective-permute-done.5.refs_6_ = bf16[2,128,384]{2,1,0:T(8,128)(2,1)S(1)} collective-permute-done((bf16[2,128,384]{2,1,0:T(8,128)(2,1)S(1)}, bf16[2,128,384]{2,1,0:T(8,128)(2,1)S(1)}, u32[]{:S(2)}, u32[]{:S(2)}) %collective-permute-start.5) | collective-permute-done | bytes 196640 | tf_op jit(solution)/shard_map/ppermute | solution.py:343
  39.8 0.0 collective-permute-done.7.refs_8_
  39.8 1.4 collective-permute-done.9.refs_10_
  41.2 8.6 %boundary_first.1 = bf16[16,136,384]{2,1,0:T(8,128)(2,1)} custom-call(s32[8]{0:T(128)S(1)} %broadcast_xor_fusion.refs_0_, s32[8]{0:T(128)S(1)} %bitcast.29, s32[8]{0:T(128)S(1)} %bitcast.31, s32[1]{0:T(128)} %bitcast.21.refs_3_, bf16[2,128,384]{2,1,0:T(8,128)(2,1)S(1)} %pad_maximum_fusion.refs_4_.chunk_ref, ...), custom_call_target="tpu_custom_call" | custom-call | tf_op jit(solution)/shard_map/boundary_first/pallas_call | solution.py:220
  49.8 5.9 %all-to-all-start.1 = ((bf16[16,136,384]{2,1,0:T(8,128)(2,1)}), bf16[16,136,384]{2,1,0:T(8,128)(2,1)S(1)}, u32[]{:S(2)}, u32[]{:S(2)}) async-start(bf16[16,136,384]{2,1,0:T(8,128)(2,1)} %boundary_first.1), calls=%async_computation.1 | async-start | bytes 3342336 | tf_op jit(solution)/shard_map/all_to_all | solution.py:395
  55.7 0.6 collective-permute-start.11
  56.3 2.2 %collective-permute-start.12 = (bf16[3,8,8,384]{3,2,1,0:T(8,128)(2,1)}, bf16[3,8,8,384]{3,2,1,0:T(8,128)(2,1)S(1)}, u32[]{:S(2)}, u32[]{:S(2)}) collective-permute-start(bf16[3,8,8,384]{3,2,1,0:T(8,128)(2,1)} %get-tuple-element.48), channel_id=1, source_target_pairs={{16,32},{32,16},{48,64},{64,48},{80,96},{96,80},{17,33},{33,17},{4... | collective-permute-start | bytes 442376 | tf_op jit(solution)/shard_map/ppermute | solution.py:353
  58.5 1.9 %collective-permute-start.13 = (bf16[3,8,8,384]{3,2,1,0:T(8,128)(2,1)}, bf16[3,8,8,384]{3,2,1,0:T(8,128)(2,1)S(1)}, u32[]{:S(2)}, u32[]{:S(2)}) collective-permute-start(bf16[3,8,8,384]{3,2,1,0:T(8,128)(2,1)} %copy-done.10), channel_id=1, source_target_pairs={{0,1},{1,0},{2,3},{3,2},{4,5},{5,4},{6,7},{7,6},{8,9},{9,8},{10,11... | collective-permute-start | bytes 442376 | tf_op jit(solution)/shard_map/ppermute | solution.py:354
  60.4 0.7 collective-permute-start.14
  61.1 1.9 %collective-permute-done.12.refs_4_ = bf16[3,8,8,384]{3,2,1,0:T(8,128)(2,1)S(1)} collective-permute-done((bf16[3,8,8,384]{3,2,1,0:T(8,128)(2,1)}, bf16[3,8,8,384]{3,2,1,0:T(8,128)(2,1)S(1)}, u32[]{:S(2)}, u32[]{:S(2)}) %collective-permute-start.12) | collective-permute-done | bytes 147488 | tf_op jit(solution)/shard_map/ppermute | solution.py:353
  62.9 17.0 %collective-permute-done.13.refs_5_ = bf16[3,8,8,384]{3,2,1,0:T(8,128)(2,1)S(1)} collective-permute-done((bf16[3,8,8,384]{3,2,1,0:T(8,128)(2,1)}, bf16[3,8,8,384]{3,2,1,0:T(8,128)(2,1)S(1)}, u32[]{:S(2)}, u32[]{:S(2)}) %collective-permute-start.13) | collective-permute-done | bytes 147488 | tf_op jit(solution)/shard_map/ppermute | solution.py:354
  80.0 1.8 %all-to-all-done.1.got_ref = bf16[16,136,384]{2,1,0:T(8,128)(2,1)S(1)} async-done(((bf16[16,136,384]{2,1,0:T(8,128)(2,1)}), bf16[16,136,384]{2,1,0:T(8,128)(2,1)S(1)}, u32[]{:S(2)}, u32[]{:S(2)}) %all-to-all-start.1) | async-done | bytes 1671200 | tf_op jit(solution)/shard_map/all_to_all | solution.py:395
  81.7 0.6 middle.1.refs_4_
  82.4 0.7 collective-permute-start.15
  83.1 2.3 %collective-permute-start.16 = (bf16[2,128,384]{2,1,0:T(8,128)(2,1)S(1)}, bf16[2,128,384]{2,1,0:T(8,128)(2,1)S(1)}, u32[]{:S(2)}, u32[]{:S(2)}) collective-permute-start(bf16[2,128,384]{2,1,0:T(8,128)(2,1)S(1)} %middle.1.refs_4_), channel_id=1, source_target_pairs={{0,32},{16,48},{32,0},{48,16},{64,96},{80,112},{96,64},{112,80},{1... | collective-permute-start | bytes 589832 | tf_op jit(solution)/shard_map/ppermute | solution.py:343
  85.4 1.2 collective-permute-start.17
  86.6 0.0 collective-permute-start.18
  86.6 4.0 %stage.3 = (bf16[2048,1024]{1,0:T(8,128)(2,1)S(1)}, bf16[2048,1024]{1,0:T(8,128)(2,1)S(1)}) custom-call(s32[2]{0:T(128)S(1)} %pad_add_fusion.side_ref.refs_0_, bf16[2048,1024]{1,0:T(8,128)(2,1)} %single_hbm.3, bf16[2048,1024]{1,0:T(8,128)(2,1)} %double_hbm.3), custom_call_target="tpu_custom_call" | custom-call | tf_op jit(solution)/shard_map/stage/pallas_call | solution.py:163
  90.6 1.2 collective-permute-done.15.refs_5_
  91.8 0.0 collective-permute-start.19
  91.8 0.0 collective-permute-done.16.refs_6_
  91.8 0.5 collective-permute-start.20
  92.3 1.7 %collective-permute-done.17.refs_7_ = bf16[2,128,384]{2,1,0:T(8,128)(2,1)S(1)} collective-permute-done((bf16[2,128,384]{2,1,0:T(8,128)(2,1)S(1)}, bf16[2,128,384]{2,1,0:T(8,128)(2,1)S(1)}, u32[]{:S(2)}, u32[]{:S(2)}) %collective-permute-start.17) | collective-permute-done | bytes 196640 | tf_op jit(solution)/shard_map/ppermute | solution.py:343
  94.0 0.0 collective-permute-start.21
  94.1 0.0 collective-permute-done.18.refs_8_
  94.1 1.4 %collective-permute-done.21.refs_11_ = bf16[2,128,384]{2,1,0:T(8,128)(2,1)S(1)} collective-permute-done((bf16[2,128,384]{2,1,0:T(8,128)(2,1)S(1)}, bf16[2,128,384]{2,1,0:T(8,128)(2,1)S(1)}, u32[]{:S(2)}, u32[]{:S(2)}) %collective-permute-start.21) | collective-permute-done | bytes 196640 | tf_op jit(solution)/shard_map/ppermute | solution.py:344
  95.5 8.0 %boundary_second.1 = bf16[16,136,384]{2,1,0:T(8,128)(2,1)} custom-call(s32[8]{0:T(128)S(1)} %broadcast_xor_fusion.refs_0_, s32[8]{0:T(128)S(1)} %bitcast.30, s32[8]{0:T(128)S(1)} %bitcast.32, s32[1]{0:T(128)} %bitcast.22.refs_3_, bf16[2,128,384]{2,1,0:T(8,128)(2,1)S(1)} %middle.1.refs_4_, bf16[2,128,384]{2,1,0:T(8,128)(2,1)S(1)} %collective-permute-done.15.refs_5_, ...), custom_call_target="tpu_custom_call" | custom-call | tf_op jit(solution)/shard_map/boundary_second/pallas_call | solution.py:220
  103.5 8.9 %all-to-all-start.2 = ((bf16[16,136,384]{2,1,0:T(8,128)(2,1)}), bf16[16,136,384]{2,1,0:T(8,128)(2,1)S(1)}, u32[]{:S(2)}, u32[]{:S(2)}) async-start(bf16[16,136,384]{2,1,0:T(8,128)(2,1)} %boundary_second.1), calls=%async_computation.2 | async-start | bytes 3342336 | tf_op jit(solution)/shard_map/all_to_all | solution.py:402
  112.4 0.1 copy.20.route_ref
  112.5 0.9 copy-done.3
  113.4 4.6 %stencil_second.1 = (f32[3,8,8,8,384]{4,3,2,1,0:T(8,128)}, f32[8,8,8,384]{3,2,1,0:T(8,128)S(1)}) custom-call(s32[2]{0:T(128)S(1)} %pad_add_fusion.side_ref.refs_0_, f32[3,3]{1,0:T(4,128)S(1)} %copy-done.4, f32[3,8,8,8,384]{4,3,2,1,0:T(8,128)} %get-tuple-element.55.refs_2_, bf16[3,8,8,384]{3,2,1,0:T(8,128)(2,1)S(1)} %collective-permute-done.11.refs_3_, ...), custom_call_target="tpu_custom_call" | custom-call | tf_op jit(solution)/shard_map/stencil_second/pallas_call | solution.py:139
  118.0 19.1 %all-to-all-done.2.got_ref = bf16[16,136,384]{2,1,0:T(8,128)(2,1)S(1)} async-done(((bf16[16,136,384]{2,1,0:T(8,128)(2,1)}), bf16[16,136,384]{2,1,0:T(8,128)(2,1)S(1)}, u32[]{:S(2)}, u32[]{:S(2)}) %all-to-all-start.2) | async-done | bytes 1671200 | tf_op jit(solution)/shard_map/all_to_all | solution.py:402
  137.1 1.9 %last.1 = (f32[128,384]{1,0:T(8,128)}, f32[3,8,8,8,384]{4,3,2,1,0:T(8,128)}) custom-call(bf16[16,136,384]{2,1,0:T(8,128)(2,1)S(1)} %all-to-all-done.2.got_ref, f32[128,384]{1,0:T(8,128)S(1)} %get-tuple-element.62.w_ref, s32[128,1]{1,0:T(8,128)S(1)} %copy.20.route_ref, ...), custom_call_target="tpu_custom_call", output_to_operand_aliasing={{1}: (4, {})} | custom-call | tf_op jit(solution)/shard_map/last/pallas_call | solution.py:314
  (33 shorter events, 0.1 us)
Async XLA Ops:
  0.7 6.7 %copy-start.5 = (s32[128]{0:T(128)S(1)}, s32[128]{0:T(128)}, u32[]{:S(2)}) copy-start(s32[128]{0:T(128)} %param.24) | copy-start | bytes 1540
  2.1 17.1 %copy-start.11 = (f32[8,8,8]{2,1,0:T(8,128)S(1)}, f32[8,8,8]{2,1,0:T(8,128)}, u32[]{:S(2)}) copy-start(f32[8,8,8]{2,1,0:T(8,128)} %param.16) | copy-start | bytes 6148
  2.1 18.3 %copy-start.1 = (f32[128,384]{1,0:T(8,128)S(1)}, f32[128,384]{1,0:T(8,128)}, u32[]{:S(2)}) copy-start(f32[128,384]{1,0:T(8,128)} %refs_8_.1) | copy-start | bytes 589828
  2.1 18.3 %copy-start.4 = (f32[3,3]{1,0:T(4,128)S(1)}, f32[3,3]{1,0:T(4,128)}, u32[]{:S(2)}) copy-start(f32[3,3]{1,0:T(4,128)} %refs_1_.3) | copy-start | bytes 112
  2.1 18.2 %collective-permute-start = (bf16[3,8,8,384]{3,2,1,0:T(8,128)(2,1)S(1)}, bf16[3,8,8,384]{3,2,1,0:T(8,128)(2,1)S(1)}, u32[]{:S(2)}, u32[]{:S(2)}) collective-permute-start(bf16[3,8,8,384]{3,2,1,0:T(8,128)(2,1)S(1)} %get-tuple-element.34), channel_id=1, source_target_pairs={{0,16},{16,0},{32,48},{48,32},{64,80},{80,64},{96,112},{112,96},{1... | collective-permute-start | bytes 442376 | tf_op jit(solution)/shard_map/ppermute | solution.py:352
  2.2 18.1 %collective-permute-start.1 = (bf16[3,8,8,384]{3,2,1,0:T(8,128)(2,1)S(1)}, bf16[3,8,8,384]{3,2,1,0:T(8,128)(2,1)S(1)}, u32[]{:S(2)}, u32[]{:S(2)}) collective-permute-start(bf16[3,8,8,384]{3,2,1,0:T(8,128)(2,1)S(1)} %get-tuple-element.35), channel_id=1, source_target_pairs={{16,32},{32,16},{48,64},{64,48},{80,96},{96,80},{17,33},{33,17},{4... | collective-permute-start | bytes 442376 | tf_op jit(solution)/shard_map/ppermute | solution.py:353
  4.7 15.7 %collective-permute-start.2 = (bf16[3,8,8,384]{3,2,1,0:T(8,128)(2,1)S(1)}, bf16[3,8,8,384]{3,2,1,0:T(8,128)(2,1)S(1)}, u32[]{:S(2)}, u32[]{:S(2)}) collective-permute-start(bf16[3,8,8,384]{3,2,1,0:T(8,128)(2,1)S(1)} %get-tuple-element.36), channel_id=1, source_target_pairs={{0,1},{1,0},{2,3},{3,2},{4,5},{5,4},{6,7},{7,6},{8,9},{9,8},{10,11... | collective-permute-start | bytes 442376 | tf_op jit(solution)/shard_map/ppermute | solution.py:354
  6.8 13.6 %collective-permute-start.3 = (bf16[3,8,8,384]{3,2,1,0:T(8,128)(2,1)S(1)}, bf16[3,8,8,384]{3,2,1,0:T(8,128)(2,1)S(1)}, u32[]{:S(2)}, u32[]{:S(2)}) collective-permute-start(bf16[3,8,8,384]{3,2,1,0:T(8,128)(2,1)S(1)} %get-tuple-element.37), channel_id=1, source_target_pairs={{1,2},{2,1},{3,4},{4,3},{5,6},{6,5},{7,8},{8,7},{9,10},{10,9},{11,... | collective-permute-start | bytes 442376 | tf_op jit(solution)/shard_map/ppermute | solution.py:355
  10.0 18.0 %all-to-all-start = ((bf16[16,8,896]{2,1,0:T(8,128)(2,1)}), bf16[16,8,896]{2,1,0:T(8,128)(2,1)S(1)}, u32[]{:S(2)}, u32[]{:S(2)}) async-start(bf16[16,8,896]{2,1,0:T(8,128)(2,1)} %bitcast.4), calls=%async_computation | async-start | bytes 458752 | tf_op jit(solution)/shard_map/all_to_all | solution.py:382
  19.2 13.0 %copy-start.12 = (s32[8]{0:T(128)S(1)}, s32[8]{0:T(128)}, u32[]{:S(2)}) copy-start(s32[8]{0:T(128)} %constant.32.clone) | copy-start | bytes 100
  25.4 10.9 %copy-start.8 = (bf16[3,8,8,384]{3,2,1,0:T(8,128)(2,1)}, bf16[3,8,8,384]{3,2,1,0:T(8,128)(2,1)S(1)}, u32[]{:S(2)}) copy-start(bf16[3,8,8,384]{3,2,1,0:T(8,128)(2,1)S(1)} %get-tuple-element.50) | copy-start | bytes 442372
  25.4 24.5 %copy-start.10 = (bf16[3,8,8,384]{3,2,1,0:T(8,128)(2,1)}, bf16[3,8,8,384]{3,2,1,0:T(8,128)(2,1)S(1)}, u32[]{:S(2)}) copy-start(bf16[3,8,8,384]{3,2,1,0:T(8,128)(2,1)S(1)} %get-tuple-element.49) | copy-start | bytes 442372
  28.0 9.4 %collective-permute-start.6 = (bf16[2,128,384]{2,1,0:T(8,128)(2,1)S(1)}, bf16[2,128,384]{2,1,0:T(8,128)(2,1)S(1)}, u32[]{:S(2)}, u32[]{:S(2)}) collective-permute-start(bf16[2,128,384]{2,1,0:T(8,128)(2,1)S(1)} %pad_maximum_fusion.refs_4_.chunk_ref), channel_id=1, source_target_pairs={{0,96},{16,112},{32,64},{48,80},{64,32},{80,48},{96,0},{112,16},{1... | collective-permute-start | bytes 589832 | tf_op jit(solution)/shard_map/ppermute | solution.py:343
  29.3 8.9 %collective-permute-start.4 = (bf16[2,128,384]{2,1,0:T(8,128)(2,1)S(1)}, bf16[2,128,384]{2,1,0:T(8,128)(2,1)S(1)}, u32[]{:S(2)}, u32[]{:S(2)}) collective-permute-start(bf16[2,128,384]{2,1,0:T(8,128)(2,1)S(1)} %pad_maximum_fusion.refs_4_.chunk_ref), channel_id=1, source_target_pairs={{0,64},{16,80},{32,96},{48,112},{64,0},{80,16},{96,32},{112,48},{1... | collective-permute-start | bytes 589832 | tf_op jit(solution)/shard_map/ppermute | solution.py:343
  30.1 9.7 %collective-permute-start.5 = (bf16[2,128,384]{2,1,0:T(8,128)(2,1)S(1)}, bf16[2,128,384]{2,1,0:T(8,128)(2,1)S(1)}, u32[]{:S(2)}, u32[]{:S(2)}) collective-permute-start(bf16[2,128,384]{2,1,0:T(8,128)(2,1)S(1)} %pad_maximum_fusion.refs_4_.chunk_ref), channel_id=1, source_target_pairs={{0,32},{16,48},{32,0},{48,16},{64,96},{80,112},{96,64},{112,80},{1... | collective-permute-start | bytes 589832 | tf_op jit(solution)/shard_map/ppermute | solution.py:343
  32.2 7.6 %collective-permute-start.7 = (bf16[2,128,384]{2,1,0:T(8,128)(2,1)S(1)}, bf16[2,128,384]{2,1,0:T(8,128)(2,1)S(1)}, u32[]{:S(2)}, u32[]{:S(2)}) collective-permute-start(bf16[2,128,384]{2,1,0:T(8,128)(2,1)S(1)} %pad_maximum_fusion.refs_4_.chunk_ref), channel_id=1, source_target_pairs={{0,16},{16,0},{32,48},{48,32},{64,80},{80,64},{96,112},{112,96},{1... | collective-permute-start | bytes 589832 | tf_op jit(solution)/shard_map/ppermute | solution.py:344
  32.2 9.0 %copy-start = (bf16[8,1,128,128]{3,2,1,0:T(8,128)(2,1)S(1)}, bf16[8,1,128,128]{3,2,1,0:T(8,128)(2,1)}, u32[]{:S(2)}) copy-start(bf16[8,1,128,128]{3,2,1,0:T(8,128)(2,1)} %param.20) | copy-start | bytes 786436
  32.2 9.0 %copy-start.6 = (s32[8,1]{0,1:T(1,128)S(1)}, s32[8,1]{0,1:T(1,128)}, u32[]{:S(2)}) copy-start(s32[8,1]{0,1:T(1,128)} %param.21) | copy-start | bytes 100
  32.2 9.0 %copy-start.7 = (s32[8,1]{0,1:T(1,128)S(1)}, s32[8,1]{0,1:T(1,128)}, u32[]{:S(2)}) copy-start(s32[8,1]{0,1:T(1,128)} %param.22) | copy-start | bytes 100
  37.4 2.4 %collective-permute-start.10 = (bf16[2,128,384]{2,1,0:T(8,128)(2,1)S(1)}, bf16[2,128,384]{2,1,0:T(8,128)(2,1)S(1)}, u32[]{:S(2)}, u32[]{:S(2)}) collective-permute-start(bf16[2,128,384]{2,1,0:T(8,128)(2,1)S(1)} %collective-permute-done.6.refs_7_), channel_id=1, source_target_pairs={{0,16},{16,0},{32,48},{48,32},{64,80},{80,64},{96,112},{112,96},{1... | collective-permute-start | bytes 589832 | tf_op jit(solution)/shard_map/ppermute | solution.py:344
  38.2 1.6 %collective-permute-start.8 = (bf16[2,128,384]{2,1,0:T(8,128)(2,1)S(1)}, bf16[2,128,384]{2,1,0:T(8,128)(2,1)S(1)}, u32[]{:S(2)}, u32[]{:S(2)}) collective-permute-start(bf16[2,128,384]{2,1,0:T(8,128)(2,1)S(1)} %collective-permute-done.4.refs_5_), channel_id=1, source_target_pairs={{0,16},{16,0},{32,48},{48,32},{64,80},{80,64},{96,112},{112,96},{1... | collective-permute-start | bytes 589832 | tf_op jit(solution)/shard_map/ppermute | solution.py:344
  39.8 1.4 %collective-permute-start.9 = (bf16[2,128,384]{2,1,0:T(8,128)(2,1)S(1)}, bf16[2,128,384]{2,1,0:T(8,128)(2,1)S(1)}, u32[]{:S(2)}, u32[]{:S(2)}) collective-permute-start(bf16[2,128,384]{2,1,0:T(8,128)(2,1)S(1)} %collective-permute-done.5.refs_6_), channel_id=1, source_target_pairs={{0,16},{16,0},{32,48},{48,32},{64,80},{80,64},{96,112},{112,96},{1... | collective-permute-start | bytes 589832 | tf_op jit(solution)/shard_map/ppermute | solution.py:344
  49.8 10.6 %copy-start.9 = (bf16[3,8,8,384]{3,2,1,0:T(8,128)(2,1)S(1)}, bf16[3,8,8,384]{3,2,1,0:T(8,128)(2,1)}, u32[]{:S(2)}) copy-start(bf16[3,8,8,384]{3,2,1,0:T(8,128)(2,1)} %copy-done.8) | copy-start | bytes 442372
  49.8 31.9 %all-to-all-start.1 = ((bf16[16,136,384]{2,1,0:T(8,128)(2,1)}), bf16[16,136,384]{2,1,0:T(8,128)(2,1)S(1)}, u32[]{:S(2)}, u32[]{:S(2)}) async-start(bf16[16,136,384]{2,1,0:T(8,128)(2,1)} %boundary_first.1), calls=%async_computation.1 | async-start | bytes 3342336 | tf_op jit(solution)/shard_map/all_to_all | solution.py:395
  55.7 5.3 %collective-permute-start.11 = (bf16[3,8,8,384]{3,2,1,0:T(8,128)(2,1)}, bf16[3,8,8,384]{3,2,1,0:T(8,128)(2,1)S(1)}, u32[]{:S(2)}, u32[]{:S(2)}) collective-permute-start(bf16[3,8,8,384]{3,2,1,0:T(8,128)(2,1)} %get-tuple-element.47), channel_id=1, source_target_pairs={{0,16},{16,0},{32,48},{48,32},{64,80},{80,64},{96,112},{112,96},{1... | collective-permute-start | bytes 442376 | tf_op jit(solution)/shard_map/ppermute | solution.py:352
  56.3 6.7 %collective-permute-start.12 = (bf16[3,8,8,384]{3,2,1,0:T(8,128)(2,1)}, bf16[3,8,8,384]{3,2,1,0:T(8,128)(2,1)S(1)}, u32[]{:S(2)}, u32[]{:S(2)}) collective-permute-start(bf16[3,8,8,384]{3,2,1,0:T(8,128)(2,1)} %get-tuple-element.48), channel_id=1, source_target_pairs={{16,32},{32,16},{48,64},{64,48},{80,96},{96,80},{17,33},{33,17},{4... | collective-permute-start | bytes 442376 | tf_op jit(solution)/shard_map/ppermute | solution.py:353
  58.5 21.5 %collective-permute-start.13 = (bf16[3,8,8,384]{3,2,1,0:T(8,128)(2,1)}, bf16[3,8,8,384]{3,2,1,0:T(8,128)(2,1)S(1)}, u32[]{:S(2)}, u32[]{:S(2)}) collective-permute-start(bf16[3,8,8,384]{3,2,1,0:T(8,128)(2,1)} %copy-done.10), channel_id=1, source_target_pairs={{0,1},{1,0},{2,3},{3,2},{4,5},{5,4},{6,7},{7,6},{8,9},{9,8},{10,11... | collective-permute-start | bytes 442376 | tf_op jit(solution)/shard_map/ppermute | solution.py:354
  60.4 19.6 %collective-permute-start.14 = (bf16[3,8,8,384]{3,2,1,0:T(8,128)(2,1)S(1)}, bf16[3,8,8,384]{3,2,1,0:T(8,128)(2,1)S(1)}, u32[]{:S(2)}, u32[]{:S(2)}) collective-permute-start(bf16[3,8,8,384]{3,2,1,0:T(8,128)(2,1)S(1)} %copy-done.9), channel_id=1, source_target_pairs={{1,2},{2,1},{3,4},{4,3},{5,6},{6,5},{7,8},{8,7},{9,10},{10,9},{11,... | collective-permute-start | bytes 442376 | tf_op jit(solution)/shard_map/ppermute | solution.py:355
  80.0 2.4 %copy-start.2 = (bf16[3,8,8,384]{3,2,1,0:T(8,128)(2,1)}, bf16[3,8,8,384]{3,2,1,0:T(8,128)(2,1)S(1)}, u32[]{:S(2)}) copy-start(bf16[3,8,8,384]{3,2,1,0:T(8,128)(2,1)S(1)} %collective-permute-done.14.refs_6_) | copy-start | bytes 442372
  82.4 9.4 %collective-permute-start.15 = (bf16[2,128,384]{2,1,0:T(8,128)(2,1)S(1)}, bf16[2,128,384]{2,1,0:T(8,128)(2,1)S(1)}, u32[]{:S(2)}, u32[]{:S(2)}) collective-permute-start(bf16[2,128,384]{2,1,0:T(8,128)(2,1)S(1)} %middle.1.refs_4_), channel_id=1, source_target_pairs={{0,64},{16,80},{32,96},{48,112},{64,0},{80,16},{96,32},{112,48},{1... | collective-permute-start | bytes 589832 | tf_op jit(solution)/shard_map/ppermute | solution.py:343
  83.1 8.7 %collective-permute-start.16 = (bf16[2,128,384]{2,1,0:T(8,128)(2,1)S(1)}, bf16[2,128,384]{2,1,0:T(8,128)(2,1)S(1)}, u32[]{:S(2)}, u32[]{:S(2)}) collective-permute-start(bf16[2,128,384]{2,1,0:T(8,128)(2,1)S(1)} %middle.1.refs_4_), channel_id=1, source_target_pairs={{0,32},{16,48},{32,0},{48,16},{64,96},{80,112},{96,64},{112,80},{1... | collective-permute-start | bytes 589832 | tf_op jit(solution)/shard_map/ppermute | solution.py:343
  85.4 8.6 %collective-permute-start.17 = (bf16[2,128,384]{2,1,0:T(8,128)(2,1)S(1)}, bf16[2,128,384]{2,1,0:T(8,128)(2,1)S(1)}, u32[]{:S(2)}, u32[]{:S(2)}) collective-permute-start(bf16[2,128,384]{2,1,0:T(8,128)(2,1)S(1)} %middle.1.refs_4_), channel_id=1, source_target_pairs={{0,96},{16,112},{32,64},{48,80},{64,32},{80,48},{96,0},{112,16},{1... | collective-permute-start | bytes 589832 | tf_op jit(solution)/shard_map/ppermute | solution.py:343
  86.6 7.5 %collective-permute-start.18 = (bf16[2,128,384]{2,1,0:T(8,128)(2,1)S(1)}, bf16[2,128,384]{2,1,0:T(8,128)(2,1)S(1)}, u32[]{:S(2)}, u32[]{:S(2)}) collective-permute-start(bf16[2,128,384]{2,1,0:T(8,128)(2,1)S(1)} %middle.1.refs_4_), channel_id=1, source_target_pairs={{0,16},{16,0},{32,48},{48,32},{64,80},{80,64},{96,112},{112,96},{1... | collective-permute-start | bytes 589832 | tf_op jit(solution)/shard_map/ppermute | solution.py:344
  91.8 2.3 %collective-permute-start.19 = (bf16[2,128,384]{2,1,0:T(8,128)(2,1)S(1)}, bf16[2,128,384]{2,1,0:T(8,128)(2,1)S(1)}, u32[]{:S(2)}, u32[]{:S(2)}) collective-permute-start(bf16[2,128,384]{2,1,0:T(8,128)(2,1)S(1)} %collective-permute-done.15.refs_5_), channel_id=1, source_target_pairs={{0,16},{16,0},{32,48},{48,32},{64,80},{80,64},{96,112},{112,96},{1... | collective-permute-start | bytes 589832 | tf_op jit(solution)/shard_map/ppermute | solution.py:344
  91.8 2.3 %collective-permute-start.20 = (bf16[2,128,384]{2,1,0:T(8,128)(2,1)S(1)}, bf16[2,128,384]{2,1,0:T(8,128)(2,1)S(1)}, u32[]{:S(2)}, u32[]{:S(2)}) collective-permute-start(bf16[2,128,384]{2,1,0:T(8,128)(2,1)S(1)} %collective-permute-done.16.refs_6_), channel_id=1, source_target_pairs={{0,16},{16,0},{32,48},{48,32},{64,80},{80,64},{96,112},{112,96},{1... | collective-permute-start | bytes 589832 | tf_op jit(solution)/shard_map/ppermute | solution.py:344
  94.0 1.4 %collective-permute-start.21 = (bf16[2,128,384]{2,1,0:T(8,128)(2,1)S(1)}, bf16[2,128,384]{2,1,0:T(8,128)(2,1)S(1)}, u32[]{:S(2)}, u32[]{:S(2)}) collective-permute-start(bf16[2,128,384]{2,1,0:T(8,128)(2,1)S(1)} %collective-permute-done.17.refs_7_), channel_id=1, source_target_pairs={{0,16},{16,0},{32,48},{48,32},{64,80},{80,64},{96,112},{112,96},{1... | collective-permute-start | bytes 589832 | tf_op jit(solution)/shard_map/ppermute | solution.py:344
  103.5 33.6 %all-to-all-start.2 = ((bf16[16,136,384]{2,1,0:T(8,128)(2,1)}), bf16[16,136,384]{2,1,0:T(8,128)(2,1)S(1)}, u32[]{:S(2)}, u32[]{:S(2)}) async-start(bf16[16,136,384]{2,1,0:T(8,128)(2,1)} %boundary_second.1), calls=%async_computation.2 | async-start | bytes 3342336 | tf_op jit(solution)/shard_map/all_to_all | solution.py:402
  112.5 0.9 copy-start.3

commit v5 on v4

--- a/solution.py
+++ b/solution.py
@@ -22,13 +22,9 @@
     by_panel = onehot(route_ref[...], 128)
     out_ref[:, 0:WAVES] = jnp.dot(by_panel, flux_ref[...].astype(BF), preferred_element_type=F32).astype(BF)
 
-    def step(x, carry):
-        for y in range(8):
-            trace_ref[pl.ds(x * 8 + y, 1), :] = comp_ref[x, y, 0:1]
-            trace_ref[pl.ds(64 + x * 8 + y, 1), :] = comp_ref[x, y, 7:8]
-        return carry
-
-    lax.fori_loop(0, 8, step, 0)
+    for x in range(8):
+        trace_ref[x * 8 : x * 8 + 8, :] = comp_ref[x, :, 0, :]
+        trace_ref[64 + x * 8 : 64 + x * 8 + 8, :] = comp_ref[x, :, 7, :]
     out_ref[:, WAVES : 2 * WAVES] = jnp.dot(
         by_panel, trace_ref[...].astype(BF), preferred_element_type=F32
     ).astype(BF)
@@ -184,32 +180,27 @@
 
     for i in range(2048 // ROWS):
         part = pl.ds(i * ROWS, ROWS)
-        acc_ref[...] = jnp.dot(single_ref[part, :], phi_ref[...], preferred_element_type=F32) + jnp.dot(
+        acc_ref[part, :] = jnp.dot(single_ref[part, :], phi_ref[...], preferred_element_type=F32) + jnp.dot(
             double_ref[part, :], w_ref[...], preferred_element_type=F32
         )
 
-        def add_near(k, carry, i=i):
-            @pl.when((k < count_ref[0]) & (rows_ref[k] // (ROWS // 128) == i))
-            def _():
-                row = pl.multiple_of((rows_ref[k] % (ROWS // 128)) * 128, 128)
-                col = pl.multiple_of(cols_ref[k] * 128, 128)
-                acc_ref[pl.ds(row, 128), :] += jnp.dot(
-                    near_ref[k], phi_ref[pl.ds(col, 128), :], preferred_element_type=F32
-                )
-
-            return carry
-
-        lax.fori_loop(0, 8, add_near, 0)
-        total = acc_ref[...].astype(BF)
-        if first:
-            for p in range(ROWS // 256):
-                pair = i * (ROWS // 256) + p
-                select = (place == keys[0][pair]).astype(F32).astype(BF)
-                packed = jnp.dot(select, total[p * 256 : p * 256 + 256], preferred_element_type=F32).astype(BF)
-                out_ref[:, pair * 16 : pair * 16 + 16, :] = packed.reshape(16, 16, WAVES)
-        else:
-            owners = ROWS // 128
-            out_ref[i * owners : (i + 1) * owners, 0:128, :] = total.reshape(owners, 128, WAVES)
+    def add_near(k, carry):
+        row = pl.multiple_of(rows_ref[k] * 128, 128)
+        col = pl.multiple_of(cols_ref[k] * 128, 128)
+        acc_ref[pl.ds(row, 128), :] += jnp.dot(
+            near_ref[k], phi_ref[pl.ds(col, 128), :], preferred_element_type=F32
+        )
+        return carry
+
+    lax.fori_loop(0, jnp.minimum(count_ref[0], 8), add_near, 0)
+    if first:
+        for pair in range(8):
+            total = acc_ref[pair * 256 : pair * 256 + 256, :].astype(BF)
+            select = (place == keys[0][pair]).astype(F32).astype(BF)
+            packed = jnp.dot(select, total, preferred_element_type=F32).astype(BF)
+            out_ref[:, pair * 16 : pair * 16 + 16, :] = packed.reshape(16, 16, WAVES)
+    else:
+        out_ref[:, 0:128, :] = acc_ref[...].astype(BF).reshape(16, 128, WAVES)
     out_ref[:, 128:136, :] = extra_ref[...]
 
 
@@ -225,7 +216,7 @@
         scratch_shapes=[
             pltpu.VMEM((1024, WAVES), BF),
             pltpu.VMEM((1024, WAVES), BF),
-            pltpu.VMEM((ROWS, WAVES), F32),
+            pltpu.VMEM((2048, WAVES), F32),
         ],
         compiler_params=pltpu.CompilerParams(vmem_limit_bytes=LIMIT << 20),
         name="boundary_first" if first else "boundary_second",

time: 140 us -> 138 us (0.986)
  Pallas kernels: 40.6 us -> 37.9 us
    pallas_call x2, Pallas kernels: 16.6 us -> 14.3 us  [boundary(): pl.pallas_call(lambda *refs: boundary_kernel(first, *refs), in_specs=[pl....]
  transfers between devices with their start and end apart: 25 -> 25, of which waited for: 12 -> 13; matrix products, arithmetic and copies ran while one was open for 0% -> 0% of each run, Pallas kernels for 14% -> 15%
where the time goes in v5:
time: 138 us; the launch traced here: 136 us
  waiting for transfers between devices  51 us (37%)
  starting transfers between devices  43.6 us (32%)
  Pallas kernels  37.9 us (27%)
  between operations  1.81 us (1%)
  local copies, waits for them, and re-layouts  1.64 us (1%)
    all_to_all x2, waiting for transfers between devices, local(): got = lax.all_to_all(sums, 'col', 0, 0, tiled=True)  21.9 us
    ppermute x2, waiting for transfers between devices, swap_faces(): lax.ppermute(even, 'col', swapped(16, 1))  16.8 us
    all_to_all x2, starting transfers between devices, local(): got = lax.all_to_all(sums, 'col', 0, 0, tiled=True)  15 us
    pallas_call x2, Pallas kernels, boundary(): pl.pallas_call(lambda *refs: boundary_kernel(first, *refs), in_specs=[pl....  14.3 us
    pallas_call x2, Pallas kernels, stencil(): pl.pallas_call(lambda *refs: stencil_kernel(first, *refs), grid=(WAVES //...  9.5 us
    all_to_all x1, starting transfers between devices, local(): lax.all_to_all(packed.reshape(16, 8, 2 * WAVES + 128), 'col', 0, 0, tiled...  9.2 us
    ppermute x6, starting transfers between devices, across_rows(): lax.ppermute(chunk, 'row', swapped(8, k))  8.35 us
    pallas_call x2, Pallas kernels, stage(): pl.pallas_call(stage_kernel, in_specs=[pl.BlockSpec(memory_space=pltpu.SM...  8.05 us
  transfers between devices with their start and end apart: 25, of which 13 were waited for; matrix products, arithmetic and copies ran while one was open for 0% of the time, Pallas kernels for 15%

profile of v5, /device:TPU:2, one launch (start us, length us, event | category | flops | bytes accessed | tf_op | source)
XLA Modules:
  0.0 136.0 jit_solution(12736726838757822688)
XLA Ops:
  0.6 0.1 pad_add_fusion.side_ref.refs_0_
  0.7 1.4 %faces.1 = (bf16[3,8,8,384]{3,2,1,0:T(8,128)(2,1)S(1)}, bf16[3,8,8,384]{3,2,1,0:T(8,128)(2,1)S(1)}, bf16[3,8,8,384]{3,2,1,0:T(8,128)(2,1)S(1)}, bf16[3,8,8,384]{3,2,1,0:T(8,128)(2,1)S(1)}) custom-call(s32[2]{0:T(128)S(1)} %pad_add_fusion.side_ref.refs_0_, f32[3,8,8,8,384]{4,3,2,1,0:T(8,128)} %refs_2_.1, f32[3,8,8,8,384]{4,3,2,1,0:T(8,128)} %refs_2_.1, ...), custom_call_target="tpu_custom_call" | custom-call | tf_op jit(solution)/shard_map/faces/pallas_call | solution.py:239
  2.1 0.0 copy-start.11
  2.1 0.0 copy-start.1
  2.1 0.0 copy-start.4
  2.1 0.1 collective-permute-start
  2.2 2.4 %collective-permute-start.1 = (bf16[3,8,8,384]{3,2,1,0:T(8,128)(2,1)S(1)}, bf16[3,8,8,384]{3,2,1,0:T(8,128)(2,1)S(1)}, u32[]{:S(2)}, u32[]{:S(2)}) collective-permute-start(bf16[3,8,8,384]{3,2,1,0:T(8,128)(2,1)S(1)} %get-tuple-element.35), channel_id=1, source_target_pairs={{16,32},{32,16},{48,64},{64,48},{80,96},{96,80},{17,33},{33,17},{4... | collective-permute-start | bytes 442376 | tf_op jit(solution)/shard_map/ppermute | solution.py:344
  4.7 2.1 %collective-permute-start.2 = (bf16[3,8,8,384]{3,2,1,0:T(8,128)(2,1)S(1)}, bf16[3,8,8,384]{3,2,1,0:T(8,128)(2,1)S(1)}, u32[]{:S(2)}, u32[]{:S(2)}) collective-permute-start(bf16[3,8,8,384]{3,2,1,0:T(8,128)(2,1)S(1)} %get-tuple-element.36), channel_id=1, source_target_pairs={{0,1},{1,0},{2,3},{3,2},{4,5},{5,4},{6,7},{7,6},{8,9},{9,8},{10,11... | collective-permute-start | bytes 442376 | tf_op jit(solution)/shard_map/ppermute | solution.py:345
  6.8 0.7 collective-permute-start.3
  7.4 2.2 %pack.1 = bf16[128,896]{1,0:T(8,128)(2,1)} custom-call(f32[128,384]{1,0:T(8,128)} %refs_8_.1, f32[3,8,8,8,384]{4,3,2,1,0:T(8,128)} %refs_2_.1, s32[1,128]{1,0:T(1,128)S(1)} %bitcast.26), custom_call_target="tpu_custom_call" | custom-call | tf_op jit(solution)/shard_map/pack/pallas_call | solution.py:35
  9.6 9.2 %all-to-all-start = ((bf16[16,8,896]{2,1,0:T(8,128)(2,1)}), bf16[16,8,896]{2,1,0:T(8,128)(2,1)S(1)}, u32[]{:S(2)}, u32[]{:S(2)}) async-start(bf16[16,8,896]{2,1,0:T(8,128)(2,1)} %bitcast.4), calls=%async_computation | async-start | bytes 458752 | tf_op jit(solution)/shard_map/all_to_all | solution.py:373
  18.8 0.0 copy-start.12
  18.9 0.4 copy.18.refs_7_
  20.0 0.1 broadcast_bitcast_fusion
  20.0 0.0 collective-permute-done.refs_3_
  20.0 0.0 collective-permute-done.1.refs_4_
  20.1 4.9 %stencil_first.1 = (f32[3,8,8,8,384]{4,3,2,1,0:T(8,128)}, f32[128,384]{1,0:T(8,128)S(1)}, bf16[128,384]{1,0:T(8,128)(2,1)S(1)}, bf16[3,8,8,384]{3,2,1,0:T(8,128)...) custom-call(s32[2]{0:T(128)S(1)} %pad_add_fusion.side_ref.refs_0_, ...), custom_call_target="tpu_custom_call" | custom-call | tf_op jit(solution)/shard_map/stencil_first/pallas_call | solution.py:135
  25.0 2.6 %all-to-all-done = bf16[16,8,896]{2,1,0:T(8,128)(2,1)S(1)} async-done(((bf16[16,8,896]{2,1,0:T(8,128)(2,1)}), bf16[16,8,896]{2,1,0:T(8,128)(2,1)S(1)}, u32[]{:S(2)}, u32[]{:S(2)}) %all-to-all-start) | async-done | bytes 229408 | tf_op jit(solution)/shard_map/all_to_all | solution.py:373
  27.6 1.3 collective-permute-start.6
  28.9 0.8 collective-permute-start.4
  29.8 2.1 %collective-permute-start.5 = (bf16[2,128,384]{2,1,0:T(8,128)(2,1)S(1)}, bf16[2,128,384]{2,1,0:T(8,128)(2,1)S(1)}, u32[]{:S(2)}, u32[]{:S(2)}) collective-permute-start(bf16[2,128,384]{2,1,0:T(8,128)(2,1)S(1)} %pad_maximum_fusion.refs_4_.chunk_ref), channel_id=1, source_target_pairs={{0,32},{16,48},{32,0},{48,16},{64,96},{80,112},{96,64},{112,80},{1... | collective-permute-start | bytes 589832 | tf_op jit(solution)/shard_map/ppermute | solution.py:334
  31.8 0.0 collective-permute-start.7
  31.8 0.0 copy-start
  31.9 0.0 copy-start.6
  31.9 0.0 copy-start.7
  31.9 4.0 %stage.2 = (bf16[2048,1024]{1,0:T(8,128)(2,1)S(1)}, bf16[2048,1024]{1,0:T(8,128)(2,1)S(1)}) custom-call(s32[2]{0:T(128)S(1)} %pad_add_fusion.side_ref.refs_0_, bf16[2048,1024]{1,0:T(8,128)(2,1)} %single_hbm.3, bf16[2048,1024]{1,0:T(8,128)(2,1)} %double_hbm.3), custom_call_target="tpu_custom_call" | custom-call | tf_op jit(solution)/shard_map/stage/pallas_call | solution.py:159
  35.9 1.1 collective-permute-done.6.refs_7_
  37.0 0.8 collective-permute-done.4.refs_5_
  37.9 0.0 collective-permute-start.8
  37.9 1.6 %collective-permute-done.5.refs_6_ = bf16[2,128,384]{2,1,0:T(8,128)(2,1)S(1)} collective-permute-done((bf16[2,128,384]{2,1,0:T(8,128)(2,1)S(1)}, bf16[2,128,384]{2,1,0:T(8,128)(2,1)S(1)}, u32[]{:S(2)}, u32[]{:S(2)}) %collective-permute-start.5) | collective-permute-done | bytes 196640 | tf_op jit(solution)/shard_map/ppermute | solution.py:334
  39.4 0.0 collective-permute-done.7.refs_8_
  39.5 1.4 %collective-permute-done.9.refs_10_ = bf16[2,128,384]{2,1,0:T(8,128)(2,1)S(1)} collective-permute-done((bf16[2,128,384]{2,1,0:T(8,128)(2,1)S(1)}, bf16[2,128,384]{2,1,0:T(8,128)(2,1)S(1)}, u32[]{:S(2)}, u32[]{:S(2)}) %collective-permute-start.9) | collective-permute-done | bytes 196640 | tf_op jit(solution)/shard_map/ppermute | solution.py:335
  40.9 7.4 %boundary_first.1 = bf16[16,136,384]{2,1,0:T(8,128)(2,1)} custom-call(s32[8]{0:T(128)S(1)} %broadcast_xor_fusion.refs_0_, s32[8]{0:T(128)S(1)} %bitcast.29, s32[8]{0:T(128)S(1)} %bitcast.31, s32[1]{0:T(128)} %bitcast.21.refs_3_, bf16[2,128,384]{2,1,0:T(8,128)(2,1)S(1)} %pad_maximum_fusion.refs_4_.chunk_ref, ...), custom_call_target="tpu_custom_call" | custom-call | tf_op jit(solution)/shard_map/boundary_first/pallas_call | solution.py:211
  48.3 6.4 %all-to-all-start.1 = ((bf16[16,136,384]{2,1,0:T(8,128)(2,1)}), bf16[16,136,384]{2,1,0:T(8,128)(2,1)S(1)}, u32[]{:S(2)}, u32[]{:S(2)}) async-start(bf16[16,136,384]{2,1,0:T(8,128)(2,1)} %boundary_first.1), calls=%async_computation.1 | async-start | bytes 3342336 | tf_op jit(solution)/shard_map/all_to_all | solution.py:386
  54.7 0.1 collective-permute-start.11
  54.8 2.7 %collective-permute-start.12 = (bf16[3,8,8,384]{3,2,1,0:T(8,128)(2,1)}, bf16[3,8,8,384]{3,2,1,0:T(8,128)(2,1)S(1)}, u32[]{:S(2)}, u32[]{:S(2)}) collective-permute-start(bf16[3,8,8,384]{3,2,1,0:T(8,128)(2,1)} %get-tuple-element.48), channel_id=1, source_target_pairs={{16,32},{32,16},{48,64},{64,48},{80,96},{96,80},{17,33},{33,17},{4... | collective-permute-start | bytes 442376 | tf_op jit(solution)/shard_map/ppermute | solution.py:344
  57.5 1.9 %collective-permute-start.13 = (bf16[3,8,8,384]{3,2,1,0:T(8,128)(2,1)}, bf16[3,8,8,384]{3,2,1,0:T(8,128)(2,1)S(1)}, u32[]{:S(2)}, u32[]{:S(2)}) collective-permute-start(bf16[3,8,8,384]{3,2,1,0:T(8,128)(2,1)} %copy-done.10), channel_id=1, source_target_pairs={{0,1},{1,0},{2,3},{3,2},{4,5},{5,4},{6,7},{7,6},{8,9},{9,8},{10,11... | collective-permute-start | bytes 442376 | tf_op jit(solution)/shard_map/ppermute | solution.py:345
  59.4 0.7 collective-permute-start.14
  60.1 0.0 collective-permute-done.11.refs_3_
  60.1 1.4 collective-permute-done.12.refs_4_
  61.5 16.8 %collective-permute-done.13.refs_5_ = bf16[3,8,8,384]{3,2,1,0:T(8,128)(2,1)S(1)} collective-permute-done((bf16[3,8,8,384]{3,2,1,0:T(8,128)(2,1)}, bf16[3,8,8,384]{3,2,1,0:T(8,128)(2,1)S(1)}, u32[]{:S(2)}, u32[]{:S(2)}) %collective-permute-start.13) | collective-permute-done | bytes 147488 | tf_op jit(solution)/shard_map/ppermute | solution.py:345
  78.3 0.0 collective-permute-done.14.refs_6_
  78.3 1.9 %all-to-all-done.1.got_ref = bf16[16,136,384]{2,1,0:T(8,128)(2,1)S(1)} async-done(((bf16[16,136,384]{2,1,0:T(8,128)(2,1)}), bf16[16,136,384]{2,1,0:T(8,128)(2,1)S(1)}, u32[]{:S(2)}, u32[]{:S(2)}) %all-to-all-start.1) | async-done | bytes 1671200 | tf_op jit(solution)/shard_map/all_to_all | solution.py:386
  80.3 0.6 middle.1.refs_4_
  80.9 0.6 collective-permute-start.15
  81.5 2.2 %collective-permute-start.16 = (bf16[2,128,384]{2,1,0:T(8,128)(2,1)S(1)}, bf16[2,128,384]{2,1,0:T(8,128)(2,1)S(1)}, u32[]{:S(2)}, u32[]{:S(2)}) collective-permute-start(bf16[2,128,384]{2,1,0:T(8,128)(2,1)S(1)} %middle.1.refs_4_), channel_id=1, source_target_pairs={{0,32},{16,48},{32,0},{48,16},{64,96},{80,112},{96,64},{112,80},{1... | collective-permute-start | bytes 589832 | tf_op jit(solution)/shard_map/ppermute | solution.py:334
  83.6 1.4 %collective-permute-start.17 = (bf16[2,128,384]{2,1,0:T(8,128)(2,1)S(1)}, bf16[2,128,384]{2,1,0:T(8,128)(2,1)S(1)}, u32[]{:S(2)}, u32[]{:S(2)}) collective-permute-start(bf16[2,128,384]{2,1,0:T(8,128)(2,1)S(1)} %middle.1.refs_4_), channel_id=1, source_target_pairs={{0,96},{16,112},{32,64},{48,80},{64,32},{80,48},{96,0},{112,16},{1... | collective-permute-start | bytes 589832 | tf_op jit(solution)/shard_map/ppermute | solution.py:334
  85.1 4.0 %stage.3 = (bf16[2048,1024]{1,0:T(8,128)(2,1)S(1)}, bf16[2048,1024]{1,0:T(8,128)(2,1)S(1)}) custom-call(s32[2]{0:T(128)S(1)} %pad_add_fusion.side_ref.refs_0_, bf16[2048,1024]{1,0:T(8,128)(2,1)} %single_hbm.3, bf16[2048,1024]{1,0:T(8,128)(2,1)} %double_hbm.3), custom_call_target="tpu_custom_call" | custom-call | tf_op jit(solution)/shard_map/stage/pallas_call | solution.py:159
  89.1 0.4 collective-permute-done.15.refs_5_
  89.5 0.2 collective-permute-start.19
  89.7 0.2 collective-permute-done.16.refs_6_
  89.9 0.1 collective-permute-start.20
  90.0 1.5 %collective-permute-done.17.refs_7_ = bf16[2,128,384]{2,1,0:T(8,128)(2,1)S(1)} collective-permute-done((bf16[2,128,384]{2,1,0:T(8,128)(2,1)S(1)}, bf16[2,128,384]{2,1,0:T(8,128)(2,1)S(1)}, u32[]{:S(2)}, u32[]{:S(2)}) %collective-permute-start.17) | collective-permute-done | bytes 196640 | tf_op jit(solution)/shard_map/ppermute | solution.py:334
  91.5 0.0 collective-permute-start.21
  91.5 0.0 collective-permute-done.19.refs_9_
  91.5 0.0 collective-permute-done.20.refs_10_
  91.5 1.4 %collective-permute-done.21.refs_11_ = bf16[2,128,384]{2,1,0:T(8,128)(2,1)S(1)} collective-permute-done((bf16[2,128,384]{2,1,0:T(8,128)(2,1)S(1)}, bf16[2,128,384]{2,1,0:T(8,128)(2,1)S(1)}, u32[]{:S(2)}, u32[]{:S(2)}) %collective-permute-start.21) | collective-permute-done | bytes 196640 | tf_op jit(solution)/shard_map/ppermute | solution.py:335
  92.9 6.9 %boundary_second.1 = bf16[16,136,384]{2,1,0:T(8,128)(2,1)} custom-call(s32[8]{0:T(128)S(1)} %broadcast_xor_fusion.refs_0_, s32[8]{0:T(128)S(1)} %bitcast.30, s32[8]{0:T(128)S(1)} %bitcast.32, s32[1]{0:T(128)} %bitcast.22.refs_3_, bf16[2,128,384]{2,1,0:T(8,128)(2,1)S(1)} %middle.1.refs_4_, bf16[2,128,384]{2,1,0:T(8,128)(2,1)S(1)} %collective-permute-done.15.refs_5_, ...), custom_call_target="tpu_custom_call" | custom-call | tf_op jit(solution)/shard_map/boundary_second/pallas_call | solution.py:211
  99.8 8.6 %all-to-all-start.2 = ((bf16[16,136,384]{2,1,0:T(8,128)(2,1)}), bf16[16,136,384]{2,1,0:T(8,128)(2,1)S(1)}, u32[]{:S(2)}, u32[]{:S(2)}) async-start(bf16[16,136,384]{2,1,0:T(8,128)(2,1)} %boundary_second.1), calls=%async_computation.2 | async-start | bytes 3342336 | tf_op jit(solution)/shard_map/all_to_all | solution.py:393
  108.4 0.1 copy.20.route_ref
  108.5 0.9 copy-done.3
  109.4 4.6 %stencil_second.1 = (f32[3,8,8,8,384]{4,3,2,1,0:T(8,128)}, f32[8,8,8,384]{3,2,1,0:T(8,128)S(1)}) custom-call(s32[2]{0:T(128)S(1)} %pad_add_fusion.side_ref.refs_0_, f32[3,3]{1,0:T(4,128)S(1)} %copy-done.4, f32[3,8,8,8,384]{4,3,2,1,0:T(8,128)} %get-tuple-element.55.refs_2_, bf16[3,8,8,384]{3,2,1,0:T(8,128)(2,1)S(1)} %collective-permute-done.11.refs_3_, ...), custom_call_target="tpu_custom_call" | custom-call | tf_op jit(solution)/shard_map/stencil_second/pallas_call | solution.py:135
  114.0 20.0 %all-to-all-done.2.got_ref = bf16[16,136,384]{2,1,0:T(8,128)(2,1)S(1)} async-done(((bf16[16,136,384]{2,1,0:T(8,128)(2,1)}), bf16[16,136,384]{2,1,0:T(8,128)(2,1)S(1)}, u32[]{:S(2)}, u32[]{:S(2)}) %all-to-all-start.2) | async-done | bytes 1671200 | tf_op jit(solution)/shard_map/all_to_all | solution.py:393
  133.9 1.9 %last.1 = (f32[128,384]{1,0:T(8,128)}, f32[3,8,8,8,384]{4,3,2,1,0:T(8,128)}) custom-call(bf16[16,136,384]{2,1,0:T(8,128)(2,1)S(1)} %all-to-all-done.2.got_ref, f32[128,384]{1,0:T(8,128)S(1)} %get-tuple-element.62.w_ref, s32[128,1]{1,0:T(8,128)S(1)} %copy.20.route_ref, ...), custom_call_target="tpu_custom_call", output_to_operand_aliasing={{1}: (4, {})} | custom-call | tf_op jit(solution)/shard_map/last/pallas_call | solution.py:305
  (33 shorter events, 0.1 us)
Async XLA Ops:
  0.7 6.7 %copy-start.5 = (s32[128]{0:T(128)S(1)}, s32[128]{0:T(128)}, u32[]{:S(2)}) copy-start(s32[128]{0:T(128)} %param.24) | copy-start | bytes 1540
  2.1 16.8 %copy-start.11 = (f32[8,8,8]{2,1,0:T(8,128)S(1)}, f32[8,8,8]{2,1,0:T(8,128)}, u32[]{:S(2)}) copy-start(f32[8,8,8]{2,1,0:T(8,128)} %param.16) | copy-start | bytes 6148
  2.1 17.9 %copy-start.1 = (f32[128,384]{1,0:T(8,128)S(1)}, f32[128,384]{1,0:T(8,128)}, u32[]{:S(2)}) copy-start(f32[128,384]{1,0:T(8,128)} %refs_8_.1) | copy-start | bytes 589828
  2.1 17.9 %copy-start.4 = (f32[3,3]{1,0:T(4,128)S(1)}, f32[3,3]{1,0:T(4,128)}, u32[]{:S(2)}) copy-start(f32[3,3]{1,0:T(4,128)} %refs_1_.3) | copy-start | bytes 112
  2.1 17.9 %collective-permute-start = (bf16[3,8,8,384]{3,2,1,0:T(8,128)(2,1)S(1)}, bf16[3,8,8,384]{3,2,1,0:T(8,128)(2,1)S(1)}, u32[]{:S(2)}, u32[]{:S(2)}) collective-permute-start(bf16[3,8,8,384]{3,2,1,0:T(8,128)(2,1)S(1)} %get-tuple-element.34), channel_id=1, source_target_pairs={{0,16},{16,0},{32,48},{48,32},{64,80},{80,64},{96,112},{112,96},{1... | collective-permute-start | bytes 442376 | tf_op jit(solution)/shard_map/ppermute | solution.py:343
  2.2 17.8 %collective-permute-start.1 = (bf16[3,8,8,384]{3,2,1,0:T(8,128)(2,1)S(1)}, bf16[3,8,8,384]{3,2,1,0:T(8,128)(2,1)S(1)}, u32[]{:S(2)}, u32[]{:S(2)}) collective-permute-start(bf16[3,8,8,384]{3,2,1,0:T(8,128)(2,1)S(1)} %get-tuple-element.35), channel_id=1, source_target_pairs={{16,32},{32,16},{48,64},{64,48},{80,96},{96,80},{17,33},{33,17},{4... | collective-permute-start | bytes 442376 | tf_op jit(solution)/shard_map/ppermute | solution.py:344
  4.7 15.4 %collective-permute-start.2 = (bf16[3,8,8,384]{3,2,1,0:T(8,128)(2,1)S(1)}, bf16[3,8,8,384]{3,2,1,0:T(8,128)(2,1)S(1)}, u32[]{:S(2)}, u32[]{:S(2)}) collective-permute-start(bf16[3,8,8,384]{3,2,1,0:T(8,128)(2,1)S(1)} %get-tuple-element.36), channel_id=1, source_target_pairs={{0,1},{1,0},{2,3},{3,2},{4,5},{5,4},{6,7},{7,6},{8,9},{9,8},{10,11... | collective-permute-start | bytes 442376 | tf_op jit(solution)/shard_map/ppermute | solution.py:345
  6.8 13.3 %collective-permute-start.3 = (bf16[3,8,8,384]{3,2,1,0:T(8,128)(2,1)S(1)}, bf16[3,8,8,384]{3,2,1,0:T(8,128)(2,1)S(1)}, u32[]{:S(2)}, u32[]{:S(2)}) collective-permute-start(bf16[3,8,8,384]{3,2,1,0:T(8,128)(2,1)S(1)} %get-tuple-element.37), channel_id=1, source_target_pairs={{1,2},{2,1},{3,4},{4,3},{5,6},{6,5},{7,8},{8,7},{9,10},{10,9},{11,... | collective-permute-start | bytes 442376 | tf_op jit(solution)/shard_map/ppermute | solution.py:346
  9.6 18.0 %all-to-all-start = ((bf16[16,8,896]{2,1,0:T(8,128)(2,1)}), bf16[16,8,896]{2,1,0:T(8,128)(2,1)S(1)}, u32[]{:S(2)}, u32[]{:S(2)}) async-start(bf16[16,8,896]{2,1,0:T(8,128)(2,1)} %bitcast.4), calls=%async_computation | async-start | bytes 458752 | tf_op jit(solution)/shard_map/all_to_all | solution.py:373
  18.8 13.0 %copy-start.12 = (s32[8]{0:T(128)S(1)}, s32[8]{0:T(128)}, u32[]{:S(2)}) copy-start(s32[8]{0:T(128)} %constant.32.clone) | copy-start | bytes 100
  25.0 10.9 %copy-start.8 = (bf16[3,8,8,384]{3,2,1,0:T(8,128)(2,1)}, bf16[3,8,8,384]{3,2,1,0:T(8,128)(2,1)S(1)}, u32[]{:S(2)}) copy-start(bf16[3,8,8,384]{3,2,1,0:T(8,128)(2,1)S(1)} %get-tuple-element.50) | copy-start | bytes 442372
  25.0 23.2 %copy-start.10 = (bf16[3,8,8,384]{3,2,1,0:T(8,128)(2,1)}, bf16[3,8,8,384]{3,2,1,0:T(8,128)(2,1)S(1)}, u32[]{:S(2)}) copy-start(bf16[3,8,8,384]{3,2,1,0:T(8,128)(2,1)S(1)} %get-tuple-element.49) | copy-start | bytes 442372
  27.6 9.4 %collective-permute-start.6 = (bf16[2,128,384]{2,1,0:T(8,128)(2,1)S(1)}, bf16[2,128,384]{2,1,0:T(8,128)(2,1)S(1)}, u32[]{:S(2)}, u32[]{:S(2)}) collective-permute-start(bf16[2,128,384]{2,1,0:T(8,128)(2,1)S(1)} %pad_maximum_fusion.refs_4_.chunk_ref), channel_id=1, source_target_pairs={{0,96},{16,112},{32,64},{48,80},{64,32},{80,48},{96,0},{112,16},{1... | collective-permute-start | bytes 589832 | tf_op jit(solution)/shard_map/ppermute | solution.py:334
  28.9 8.9 %collective-permute-start.4 = (bf16[2,128,384]{2,1,0:T(8,128)(2,1)S(1)}, bf16[2,128,384]{2,1,0:T(8,128)(2,1)S(1)}, u32[]{:S(2)}, u32[]{:S(2)}) collective-permute-start(bf16[2,128,384]{2,1,0:T(8,128)(2,1)S(1)} %pad_maximum_fusion.refs_4_.chunk_ref), channel_id=1, source_target_pairs={{0,64},{16,80},{32,96},{48,112},{64,0},{80,16},{96,32},{112,48},{1... | collective-permute-start | bytes 589832 | tf_op jit(solution)/shard_map/ppermute | solution.py:334
  29.8 9.7 %collective-permute-start.5 = (bf16[2,128,384]{2,1,0:T(8,128)(2,1)S(1)}, bf16[2,128,384]{2,1,0:T(8,128)(2,1)S(1)}, u32[]{:S(2)}, u32[]{:S(2)}) collective-permute-start(bf16[2,128,384]{2,1,0:T(8,128)(2,1)S(1)} %pad_maximum_fusion.refs_4_.chunk_ref), channel_id=1, source_target_pairs={{0,32},{16,48},{32,0},{48,16},{64,96},{80,112},{96,64},{112,80},{1... | collective-permute-start | bytes 589832 | tf_op jit(solution)/shard_map/ppermute | solution.py:334
  31.8 7.6 %collective-permute-start.7 = (bf16[2,128,384]{2,1,0:T(8,128)(2,1)S(1)}, bf16[2,128,384]{2,1,0:T(8,128)(2,1)S(1)}, u32[]{:S(2)}, u32[]{:S(2)}) collective-permute-start(bf16[2,128,384]{2,1,0:T(8,128)(2,1)S(1)} %pad_maximum_fusion.refs_4_.chunk_ref), channel_id=1, source_target_pairs={{0,16},{16,0},{32,48},{48,32},{64,80},{80,64},{96,112},{112,96},{1... | collective-permute-start | bytes 589832 | tf_op jit(solution)/shard_map/ppermute | solution.py:335
  31.8 9.0 %copy-start = (bf16[8,1,128,128]{3,2,1,0:T(8,128)(2,1)S(1)}, bf16[8,1,128,128]{3,2,1,0:T(8,128)(2,1)}, u32[]{:S(2)}) copy-start(bf16[8,1,128,128]{3,2,1,0:T(8,128)(2,1)} %param.20) | copy-start | bytes 786436
  31.9 9.0 %copy-start.6 = (s32[8,1]{0,1:T(1,128)S(1)}, s32[8,1]{0,1:T(1,128)}, u32[]{:S(2)}) copy-start(s32[8,1]{0,1:T(1,128)} %param.21) | copy-start | bytes 100
  31.9 9.0 %copy-start.7 = (s32[8,1]{0,1:T(1,128)S(1)}, s32[8,1]{0,1:T(1,128)}, u32[]{:S(2)}) copy-start(s32[8,1]{0,1:T(1,128)} %param.22) | copy-start | bytes 100
  37.0 2.4 %collective-permute-start.10 = (bf16[2,128,384]{2,1,0:T(8,128)(2,1)S(1)}, bf16[2,128,384]{2,1,0:T(8,128)(2,1)S(1)}, u32[]{:S(2)}, u32[]{:S(2)}) collective-permute-start(bf16[2,128,384]{2,1,0:T(8,128)(2,1)S(1)} %collective-permute-done.6.refs_7_), channel_id=1, source_target_pairs={{0,16},{16,0},{32,48},{48,32},{64,80},{80,64},{96,112},{112,96},{1... | collective-permute-start | bytes 589832 | tf_op jit(solution)/shard_map/ppermute | solution.py:335
  37.9 1.6 %collective-permute-start.8 = (bf16[2,128,384]{2,1,0:T(8,128)(2,1)S(1)}, bf16[2,128,384]{2,1,0:T(8,128)(2,1)S(1)}, u32[]{:S(2)}, u32[]{:S(2)}) collective-permute-start(bf16[2,128,384]{2,1,0:T(8,128)(2,1)S(1)} %collective-permute-done.4.refs_5_), channel_id=1, source_target_pairs={{0,16},{16,0},{32,48},{48,32},{64,80},{80,64},{96,112},{112,96},{1... | collective-permute-start | bytes 589832 | tf_op jit(solution)/shard_map/ppermute | solution.py:335
  39.4 1.4 %collective-permute-start.9 = (bf16[2,128,384]{2,1,0:T(8,128)(2,1)S(1)}, bf16[2,128,384]{2,1,0:T(8,128)(2,1)S(1)}, u32[]{:S(2)}, u32[]{:S(2)}) collective-permute-start(bf16[2,128,384]{2,1,0:T(8,128)(2,1)S(1)} %collective-permute-done.5.refs_6_), channel_id=1, source_target_pairs={{0,16},{16,0},{32,48},{48,32},{64,80},{80,64},{96,112},{112,96},{1... | collective-permute-start | bytes 589832 | tf_op jit(solution)/shard_map/ppermute | solution.py:335
  48.3 11.2 %copy-start.9 = (bf16[3,8,8,384]{3,2,1,0:T(8,128)(2,1)S(1)}, bf16[3,8,8,384]{3,2,1,0:T(8,128)(2,1)}, u32[]{:S(2)}) copy-start(bf16[3,8,8,384]{3,2,1,0:T(8,128)(2,1)} %copy-done.8) | copy-start | bytes 442372
  48.3 32.0 %all-to-all-start.1 = ((bf16[16,136,384]{2,1,0:T(8,128)(2,1)}), bf16[16,136,384]{2,1,0:T(8,128)(2,1)S(1)}, u32[]{:S(2)}, u32[]{:S(2)}) async-start(bf16[16,136,384]{2,1,0:T(8,128)(2,1)} %boundary_first.1), calls=%async_computation.1 | async-start | bytes 3342336 | tf_op jit(solution)/shard_map/all_to_all | solution.py:386
  54.7 5.4 %collective-permute-start.11 = (bf16[3,8,8,384]{3,2,1,0:T(8,128)(2,1)}, bf16[3,8,8,384]{3,2,1,0:T(8,128)(2,1)S(1)}, u32[]{:S(2)}, u32[]{:S(2)}) collective-permute-start(bf16[3,8,8,384]{3,2,1,0:T(8,128)(2,1)} %get-tuple-element.47), channel_id=1, source_target_pairs={{0,16},{16,0},{32,48},{48,32},{64,80},{80,64},{96,112},{112,96},{1... | collective-permute-start | bytes 442376 | tf_op jit(solution)/shard_map/ppermute | solution.py:343
  54.8 6.7 %collective-permute-start.12 = (bf16[3,8,8,384]{3,2,1,0:T(8,128)(2,1)}, bf16[3,8,8,384]{3,2,1,0:T(8,128)(2,1)S(1)}, u32[]{:S(2)}, u32[]{:S(2)}) collective-permute-start(bf16[3,8,8,384]{3,2,1,0:T(8,128)(2,1)} %get-tuple-element.48), channel_id=1, source_target_pairs={{16,32},{32,16},{48,64},{64,48},{80,96},{96,80},{17,33},{33,17},{4... | collective-permute-start | bytes 442376 | tf_op jit(solution)/shard_map/ppermute | solution.py:344
  57.5 20.8 %collective-permute-start.13 = (bf16[3,8,8,384]{3,2,1,0:T(8,128)(2,1)}, bf16[3,8,8,384]{3,2,1,0:T(8,128)(2,1)S(1)}, u32[]{:S(2)}, u32[]{:S(2)}) collective-permute-start(bf16[3,8,8,384]{3,2,1,0:T(8,128)(2,1)} %copy-done.10), channel_id=1, source_target_pairs={{0,1},{1,0},{2,3},{3,2},{4,5},{5,4},{6,7},{7,6},{8,9},{9,8},{10,11... | collective-permute-start | bytes 442376 | tf_op jit(solution)/shard_map/ppermute | solution.py:345
  59.4 18.9 %collective-permute-start.14 = (bf16[3,8,8,384]{3,2,1,0:T(8,128)(2,1)S(1)}, bf16[3,8,8,384]{3,2,1,0:T(8,128)(2,1)S(1)}, u32[]{:S(2)}, u32[]{:S(2)}) collective-permute-start(bf16[3,8,8,384]{3,2,1,0:T(8,128)(2,1)S(1)} %copy-done.9), channel_id=1, source_target_pairs={{1,2},{2,1},{3,4},{4,3},{5,6},{6,5},{7,8},{8,7},{9,10},{10,9},{11,... | collective-permute-start | bytes 442376 | tf_op jit(solution)/shard_map/ppermute | solution.py:346
  78.3 2.6 %copy-start.2 = (bf16[3,8,8,384]{3,2,1,0:T(8,128)(2,1)}, bf16[3,8,8,384]{3,2,1,0:T(8,128)(2,1)S(1)}, u32[]{:S(2)}) copy-start(bf16[3,8,8,384]{3,2,1,0:T(8,128)(2,1)S(1)} %collective-permute-done.14.refs_6_) | copy-start | bytes 442372
  80.9 8.6 %collective-permute-start.15 = (bf16[2,128,384]{2,1,0:T(8,128)(2,1)S(1)}, bf16[2,128,384]{2,1,0:T(8,128)(2,1)S(1)}, u32[]{:S(2)}, u32[]{:S(2)}) collective-permute-start(bf16[2,128,384]{2,1,0:T(8,128)(2,1)S(1)} %middle.1.refs_4_), channel_id=1, source_target_pairs={{0,64},{16,80},{32,96},{48,112},{64,0},{80,16},{96,32},{112,48},{1... | collective-permute-start | bytes 589832 | tf_op jit(solution)/shard_map/ppermute | solution.py:334
  81.5 8.4 %collective-permute-start.16 = (bf16[2,128,384]{2,1,0:T(8,128)(2,1)S(1)}, bf16[2,128,384]{2,1,0:T(8,128)(2,1)S(1)}, u32[]{:S(2)}, u32[]{:S(2)}) collective-permute-start(bf16[2,128,384]{2,1,0:T(8,128)(2,1)S(1)} %middle.1.refs_4_), channel_id=1, source_target_pairs={{0,32},{16,48},{32,0},{48,16},{64,96},{80,112},{96,64},{112,80},{1... | collective-permute-start | bytes 589832 | tf_op jit(solution)/shard_map/ppermute | solution.py:334
  83.6 7.8 %collective-permute-start.17 = (bf16[2,128,384]{2,1,0:T(8,128)(2,1)S(1)}, bf16[2,128,384]{2,1,0:T(8,128)(2,1)S(1)}, u32[]{:S(2)}, u32[]{:S(2)}) collective-permute-start(bf16[2,128,384]{2,1,0:T(8,128)(2,1)S(1)} %middle.1.refs_4_), channel_id=1, source_target_pairs={{0,96},{16,112},{32,64},{48,80},{64,32},{80,48},{96,0},{112,16},{1... | collective-permute-start | bytes 589832 | tf_op jit(solution)/shard_map/ppermute | solution.py:334
  85.1 6.4 %collective-permute-start.18 = (bf16[2,128,384]{2,1,0:T(8,128)(2,1)S(1)}, bf16[2,128,384]{2,1,0:T(8,128)(2,1)S(1)}, u32[]{:S(2)}, u32[]{:S(2)}) collective-permute-start(bf16[2,128,384]{2,1,0:T(8,128)(2,1)S(1)} %middle.1.refs_4_), channel_id=1, source_target_pairs={{0,16},{16,0},{32,48},{48,32},{64,80},{80,64},{96,112},{112,96},{1... | collective-permute-start | bytes 589832 | tf_op jit(solution)/shard_map/ppermute | solution.py:335
  89.5 2.0 %collective-permute-start.19 = (bf16[2,128,384]{2,1,0:T(8,128)(2,1)S(1)}, bf16[2,128,384]{2,1,0:T(8,128)(2,1)S(1)}, u32[]{:S(2)}, u32[]{:S(2)}) collective-permute-start(bf16[2,128,384]{2,1,0:T(8,128)(2,1)S(1)} %collective-permute-done.15.refs_5_), channel_id=1, source_target_pairs={{0,16},{16,0},{32,48},{48,32},{64,80},{80,64},{96,112},{112,96},{1... | collective-permute-start | bytes 589832 | tf_op jit(solution)/shard_map/ppermute | solution.py:335
  89.9 1.6 %collective-permute-start.20 = (bf16[2,128,384]{2,1,0:T(8,128)(2,1)S(1)}, bf16[2,128,384]{2,1,0:T(8,128)(2,1)S(1)}, u32[]{:S(2)}, u32[]{:S(2)}) collective-permute-start(bf16[2,128,384]{2,1,0:T(8,128)(2,1)S(1)} %collective-permute-done.16.refs_6_), channel_id=1, source_target_pairs={{0,16},{16,0},{32,48},{48,32},{64,80},{80,64},{96,112},{112,96},{1... | collective-permute-start | bytes 589832 | tf_op jit(solution)/shard_map/ppermute | solution.py:335
  91.5 1.4 %collective-permute-start.21 = (bf16[2,128,384]{2,1,0:T(8,128)(2,1)S(1)}, bf16[2,128,384]{2,1,0:T(8,128)(2,1)S(1)}, u32[]{:S(2)}, u32[]{:S(2)}) collective-permute-start(bf16[2,128,384]{2,1,0:T(8,128)(2,1)S(1)} %collective-permute-done.17.refs_7_), channel_id=1, source_target_pairs={{0,16},{16,0},{32,48},{48,32},{64,80},{80,64},{96,112},{112,96},{1... | collective-permute-start | bytes 589832 | tf_op jit(solution)/shard_map/ppermute | solution.py:335
  99.8 34.2 %all-to-all-start.2 = ((bf16[16,136,384]{2,1,0:T(8,128)(2,1)}), bf16[16,136,384]{2,1,0:T(8,128)(2,1)S(1)}, u32[]{:S(2)}, u32[]{:S(2)}) async-start(bf16[16,136,384]{2,1,0:T(8,128)(2,1)} %boundary_second.1), calls=%async_computation.2 | async-start | bytes 3342336 | tf_op jit(solution)/shard_map/all_to_all | solution.py:393
  108.5 0.9 copy-start.3
